TPU v7x, 32 devices: a whole 2x2x4 slice. The times are simulated.
32 devices in a mesh: group: 8 (over z, y), expert: 4 (over x, core).
Axes of the slice: x: 2, y: 2, z: 4, core: 2. Of those that a mesh axis runs over, the one named last changes fastest.
Arguments:
- layer_in: bfloat16 [4, 1024, 2048], P('expert', 'group'), may hold values from -6 to 6
- segment_ids: int32 [4, 1024], P('expert', 'group'), may hold values from 0 to 4, never falling along the last dimension, each value on 1 to 512 neighbouring positions
- routing: int32 [4, 1024, 8], P('expert', 'group'), may hold values from 0 to 15, all different within a row; in each aligned block of 128 rows (0 to 127, 128 to 255, ..., all dimensions but the last counted through in order) at most 85 rows name the same one
- out_grad: bfloat16 [4, 1024, 2048], P('expert', 'group'), may hold values from -6 to 6
- attn_gain: float32 [2048], replicated, may hold values from 0.5 to 1.5
- w_query: bfloat16 [2048, 2048], replicated, may hold values from -0.125 to 0.125
- w_key: bfloat16 [2048, 2048], replicated, may hold values from -0.125 to 0.125
- w_value: bfloat16 [2048, 2048], replicated, may hold values from -0.125 to 0.125
- query_gain: float32 [2048], replicated, may hold values from 0.5 to 1.5
- key_gain: float32 [2048], replicated, may hold values from 0.5 to 1.5
- w_out: bfloat16 [2048, 2048], replicated, may hold values from -1 to 1
- mlp_gain: float32 [2048], replicated, may hold values from 0.5 to 1.5
- w_router: bfloat16 [2048, 16], replicated, may hold values from -0.0625 to 0.0625
- w_gate: bfloat16 [16, 2048, 1024], P('expert', 'group'), may hold values from -0.125 to 0.125
- w_up: bfloat16 [16, 2048, 1024], P('expert', 'group'), may hold values from -0.125 to 0.125
- w_down: bfloat16 [16, 1024, 2048], P('expert', None, 'group'), may hold values from -2 to 2
Outputs:
- layer_out: bfloat16 [4, 1024, 2048], P('expert', 'group')
- x_grad: float32 [4, 1024, 2048], P('expert', 'group')
- attn_gain_grad: float32 [2048], P(('group', 'expert'))
- query_w_grad: float32 [2048, 2048], P(('group', 'expert'))
- key_w_grad: float32 [2048, 2048], P(('group', 'expert'))
- value_w_grad: float32 [2048, 2048], P(('group', 'expert'))
- query_gain_grad: float32 [2048], P(('group', 'expert'))
- key_gain_grad: float32 [2048], P(('group', 'expert'))
- out_w_grad: float32 [2048, 2048], P(('group', 'expert'))
- mlp_gain_grad: float32 [2048], P(('group', 'expert'))
- router_grad: float32 [2048, 16], P(('group', 'expert'))
- gate_grad: float32 [16, 2048, 1024], P('expert', 'group')
- up_grad: float32 [16, 2048, 1024], P('expert', 'group')
- down_grad: float32 [16, 1024, 2048], P('expert', None, 'group')
Inputs may be any that keep to these rules, and one draw needn't show every extreme that they name: `routing`: each row names 8 different experts. Within each aligned block of 128 rows of a sequence no expert is named by more than 85 rows. `segment_ids`: document numbers never fall along a sequence; a document has at most 512 tokens.
All inputs are finite; a program needn't handle non-finite values.
Results may differ from a plain program's by a relative error of at most 0.019.
Values may be sent and summed in bfloat16 or wider, within the bound.
A program may use at most 320 MiB of HBM per device.

v0:
```python
import math

import jax
import jax.numpy as jnp
from jax import lax
from jax.sharding import PartitionSpec as P

HEADS = 16
CAP = 85


EPSILON = 1e-05
MASKED = -1000000000.0


def rms_norm(values_in, gain_vec):
    return (
        values_in
        * lax.rsqrt(jnp.mean(values_in * values_in, axis=-1, keepdims=True) + EPSILON)
        * gain_vec
    )


def angles(row_start, row_count, head_dim):
    places = (row_start + jnp.arange(row_count, dtype=jnp.int32)).astype(jnp.float32)
    frequency = jnp.exp(
        -math.log(10000.0) * 2.0 * jnp.arange(head_dim // 2, dtype=jnp.float32) / head_dim
    )
    turn_angle = places[:, None] * frequency[None, :]
    return (jnp.cos(turn_angle)[:, None, :], jnp.sin(turn_angle)[:, None, :])


def rotate(values_in, cosine, sine):
    half_dim = values_in.shape[-1] // 2
    first_half = values_in[..., :half_dim]
    second = values_in[..., half_dim:]
    return jnp.concatenate(
        [first_half * cosine - second * sine, second * cosine + first_half * sine], axis=-1
    )


def inner_rows(left, right):
    return lax.dot_general(
        left, right, (((0,), (0,)), ((), ())), preferred_element_type=jnp.float32
    )


def times_trans(left, right):
    return lax.dot_general(
        left, right, (((1,), (1,)), ((), ())), preferred_element_type=jnp.float32
    )


def slot_numbers(flat_expert, experts):
    onehot = (flat_expert[:, None] == jnp.arange(experts, dtype=jnp.int32)[None, :]).astype(
        jnp.int32
    )
    before = jnp.cumsum(onehot, axis=0) - onehot
    return jnp.sum(before * onehot, axis=1)


def masked_scores(queries, key_rows, query_pos, key_pos, query_seg, key_seg, score_scale):
    raw_scores = (
        jnp.einsum("qhd,khd->hqk", queries, key_rows, preferred_element_type=jnp.float32)
        * score_scale
    )
    allowed = (query_seg[:, None] == key_seg[None, :]) & (key_pos[None, :] <= query_pos[:, None])
    return jnp.where(allowed[None], raw_scores, MASKED)


def expert_forward(rows_in, gate_full, up_full, down_full):
    gate_pre = jnp.einsum("secd,edf->secf", rows_in, gate_full, preferred_element_type=jnp.float32)
    up_pre = jnp.einsum("secd,edf->secf", rows_in, up_full, preferred_element_type=jnp.float32)
    hidden_b = (jax.nn.silu(gate_pre) * up_pre).astype(jnp.bfloat16)
    expert_out = jnp.einsum(
        "secf,efd->secd", hidden_b, down_full, preferred_element_type=jnp.float32
    ).astype(jnp.bfloat16)
    return (gate_pre, up_pre, hidden_b, expert_out)


def shards(
    layer_in,
    segment_ids,
    routing,
    out_grad,
    attn_gain,
    w_query,
    w_key,
    w_value,
    query_gain,
    key_gain,
    w_out,
    mlp_gain,
    w_router,
    w_gate,
    w_up,
    w_down,
):
    tok_rows = layer_in.shape[1]
    width = layer_in.shape[2]
    head_dim = width // HEADS
    top_count = routing.shape[2]
    sources = lax.axis_size("expert")
    local_experts = w_gate.shape[0]
    all_experts = local_experts * sources
    capacity = CAP
    score_scale = 1.0 / math.sqrt(head_dim)
    row_start = lax.axis_index("group") * tok_rows
    query_pos = row_start + jnp.arange(tok_rows, dtype=jnp.int32)
    cosine, sine = angles(row_start, tok_rows, head_dim)
    inputs = layer_in[0].astype(jnp.float32)
    own_seg = segment_ids[0]
    route_rows = routing[0]
    route_flat = route_rows.reshape(-1)
    token_of = jnp.arange(tok_rows * top_count, dtype=jnp.int32) // top_count
    slot = slot_numbers(route_flat, all_experts)
    place = route_flat * capacity + slot

    def head_side(raw_rows, gain_vec):
        return rotate(rms_norm(raw_rows, gain_vec).reshape(tok_rows, HEADS, head_dim), cosine, sine)

    normed = rms_norm(inputs, attn_gain)
    normed_b = normed.astype(jnp.bfloat16)
    query_raw = jnp.dot(normed_b, w_query, preferred_element_type=jnp.float32)
    key_raw = jnp.dot(normed_b, w_key, preferred_element_type=jnp.float32)
    values_b = (
        jnp.dot(normed_b, w_value, preferred_element_type=jnp.float32)
        .astype(jnp.bfloat16)
        .reshape(tok_rows, HEADS, head_dim)
    )
    queries_b = head_side(query_raw, query_gain).astype(jnp.bfloat16)
    keys_b = head_side(key_raw, key_gain).astype(jnp.bfloat16)
    key_all, value_all, seg_all = (
        lax.all_gather(keys_b, "group", axis=0, tiled=True),
        lax.all_gather(values_b, "group", axis=0, tiled=True),
        lax.all_gather(own_seg, "group", axis=0, tiled=True),
    )
    key_pos = jnp.arange(key_all.shape[0], dtype=jnp.int32)
    scores = masked_scores(queries_b, key_all, query_pos, key_pos, own_seg, seg_all, score_scale)
    top_score = jnp.max(scores, axis=-1, keepdims=True)
    log_total = top_score + jnp.log(jnp.sum(jnp.exp(scores - top_score), axis=-1, keepdims=True))
    probs = jnp.exp(scores - log_total)
    probs_b = probs.astype(jnp.bfloat16)
    mixed_b = (
        jnp.einsum("hqk,khd->qhd", probs_b, value_all, preferred_element_type=jnp.float32)
        .reshape(tok_rows, width)
        .astype(jnp.bfloat16)
    )
    resid = inputs + jnp.dot(mixed_b, w_out, preferred_element_type=jnp.float32)
    normed_mlp_b = rms_norm(resid, mlp_gain).astype(jnp.bfloat16)
    router = jax.nn.softmax(
        jnp.dot(normed_mlp_b, w_router, preferred_element_type=jnp.float32), axis=-1
    )
    picked = jnp.take_along_axis(router, route_rows, axis=1)
    gate_full, up_full, down_full = (
        lax.all_gather(w_gate, "group", axis=1, tiled=True),
        lax.all_gather(w_up, "group", axis=1, tiled=True),
        lax.all_gather(w_down, "group", axis=2, tiled=True),
    )
    send = (
        jnp.zeros((all_experts * capacity, width), jnp.bfloat16)
        .at[place]
        .set(normed_mlp_b[token_of])
    )
    rows_in = lax.all_to_all(
        send.reshape(sources, local_experts * capacity, width),
        "expert",
        split_axis=0,
        concat_axis=0,
        tiled=True,
    ).reshape(sources, local_experts, capacity, width)
    gate_pre, up_pre, hidden_b, expert_out = expert_forward(rows_in, gate_full, up_full, down_full)
    returned = lax.all_to_all(
        expert_out.reshape(sources, local_experts * capacity, width),
        "expert",
        split_axis=0,
        concat_axis=0,
        tiled=True,
    ).reshape(all_experts * capacity, width)
    picked_rows = returned[place].reshape(tok_rows, top_count, width)
    mixture = jnp.sum(picked[:, :, None] * picked_rows.astype(jnp.float32), axis=1)
    result = (resid + mixture).astype(jnp.bfloat16)
    grad_out = out_grad[0].astype(jnp.float32)
    picked_grad = jnp.sum(grad_out[:, None, :] * picked_rows.astype(jnp.float32), axis=2)
    grad_rows = (
        (picked[:, :, None] * grad_out[:, None, :])
        .astype(jnp.bfloat16)
        .reshape(tok_rows * top_count, width)
    )
    grad_send = jnp.zeros((all_experts * capacity, width), jnp.bfloat16).at[place].set(grad_rows)
    grad_in = lax.all_to_all(
        grad_send.reshape(sources, local_experts * capacity, width),
        "expert",
        split_axis=0,
        concat_axis=0,
        tiled=True,
    ).reshape(sources, local_experts, capacity, width)
    gate_full, up_full, down_full = (
        lax.all_gather(w_gate, "group", axis=1, tiled=True),
        lax.all_gather(w_up, "group", axis=1, tiled=True),
        lax.all_gather(w_down, "group", axis=2, tiled=True),
    )
    hidden_grad = jnp.einsum(
        "secd,efd->secf", grad_in, down_full, preferred_element_type=jnp.float32
    )
    down_w_grad = jnp.einsum(
        "secf,secd->efd", hidden_b, grad_in, preferred_element_type=jnp.float32
    )
    sigma = jax.nn.sigmoid(gate_pre)
    gate_grad_b = (hidden_grad * up_pre * sigma * (1.0 + gate_pre * (1.0 - sigma))).astype(
        jnp.bfloat16
    )
    up_grad_b = (hidden_grad * gate_pre * sigma).astype(jnp.bfloat16)
    gate_w_grad = jnp.einsum(
        "secd,secf->edf", rows_in, gate_grad_b, preferred_element_type=jnp.float32
    )
    up_w_grad = jnp.einsum("secd,secf->edf", rows_in, up_grad_b, preferred_element_type=jnp.float32)
    slot_grad = jnp.einsum(
        "secf,edf->secd", gate_grad_b, gate_full, preferred_element_type=jnp.float32
    )
    slot_grad = (
        slot_grad
        + jnp.einsum("secf,edf->secd", up_grad_b, up_full, preferred_element_type=jnp.float32)
    ).astype(jnp.bfloat16)
    returned_grad = lax.all_to_all(
        slot_grad.reshape(sources, local_experts * capacity, width),
        "expert",
        split_axis=0,
        concat_axis=0,
        tiled=True,
    ).reshape(all_experts * capacity, width)
    mlp_in_grad = jnp.sum(
        returned_grad[place].reshape(tok_rows, top_count, width).astype(jnp.float32), axis=1
    )
    onehot_pick = (
        route_rows[:, :, None] == jnp.arange(all_experts, dtype=jnp.int32)[None, None, :]
    ).astype(jnp.float32)
    router_full_grad = jnp.sum(picked_grad[:, :, None] * onehot_pick, axis=1)
    logits_grad_b = (
        router * (router_full_grad - jnp.sum(router * router_full_grad, axis=-1, keepdims=True))
    ).astype(jnp.bfloat16)
    router_w_grad = inner_rows(normed_mlp_b, logits_grad_b)
    mlp_in_grad = mlp_in_grad + times_trans(logits_grad_b, w_router)
    _, mlp_back = jax.vjp(rms_norm, resid, mlp_gain)
    resid_part, mlp_gain_grad = mlp_back(mlp_in_grad)
    resid_grad = grad_out + resid_part
    attn_grad_b = resid_grad.astype(jnp.bfloat16)
    out_w_grad = inner_rows(mixed_b, attn_grad_b)
    mixed_grad_b = (
        times_trans(attn_grad_b, w_out).astype(jnp.bfloat16).reshape(tok_rows, HEADS, head_dim)
    )
    prob_grad = jnp.einsum(
        "qhd,khd->hqk", mixed_grad_b, value_all, preferred_element_type=jnp.float32
    )
    delta = jnp.sum(probs * prob_grad, axis=-1, keepdims=True)
    score_grad_b = (probs * (prob_grad - delta) * score_scale).astype(jnp.bfloat16)
    query_grad = jnp.einsum(
        "hqk,khd->qhd", score_grad_b, key_all, preferred_element_type=jnp.float32
    )
    key_part = jnp.einsum(
        "hqk,qhd->khd", score_grad_b, queries_b, preferred_element_type=jnp.float32
    )
    value_part = jnp.einsum(
        "hqk,qhd->khd", probs_b, mixed_grad_b, preferred_element_type=jnp.float32
    )
    kv_grad = lax.psum_scatter(
        jnp.concatenate(
            [
                key_part.reshape(tok_rows * lax.axis_size("group"), width),
                value_part.reshape(tok_rows * lax.axis_size("group"), width),
            ],
            axis=1,
        ).astype(jnp.bfloat16),
        "group",
        scatter_dimension=0,
        tiled=True,
    ).astype(jnp.float32)
    key_grad = kv_grad[:, :width].reshape(tok_rows, HEADS, head_dim)
    value_grad_b = kv_grad[:, width:].astype(jnp.bfloat16)
    _, query_back = jax.vjp(head_side, query_raw, query_gain)
    query_raw_grad, query_gain_grad = query_back(query_grad)
    _, key_back = jax.vjp(head_side, key_raw, key_gain)
    key_raw_grad, key_gain_grad = key_back(key_grad)
    query_raw_b = query_raw_grad.astype(jnp.bfloat16)
    key_raw_b = key_raw_grad.astype(jnp.bfloat16)
    query_w_grad = inner_rows(normed_b, query_raw_b)
    key_w_grad = inner_rows(normed_b, key_raw_b)
    value_w_grad = inner_rows(normed_b, value_grad_b)
    normed_grad = (
        times_trans(query_raw_b, w_query)
        + times_trans(key_raw_b, w_key)
        + times_trans(value_grad_b, w_value)
    )
    _, attn_back = jax.vjp(rms_norm, inputs, attn_gain)
    input_part, attn_gain_grad = attn_back(normed_grad)
    input_grad = resid_grad + input_part
    gate_sum, up_sum, down_sum = (
        lax.psum_scatter(
            gate_w_grad.astype(jnp.bfloat16), "group", scatter_dimension=1, tiled=True
        ).astype(jnp.float32),
        lax.psum_scatter(
            up_w_grad.astype(jnp.bfloat16), "group", scatter_dimension=1, tiled=True
        ).astype(jnp.float32),
        lax.psum_scatter(
            down_w_grad.astype(jnp.bfloat16), "group", scatter_dimension=2, tiled=True
        ).astype(jnp.float32),
    )
    dense_sums = (
        lax.psum_scatter(attn_gain_grad, ("group", "expert"), scatter_dimension=0, tiled=True),
        lax.psum_scatter(query_w_grad, ("group", "expert"), scatter_dimension=0, tiled=True),
        lax.psum_scatter(key_w_grad, ("group", "expert"), scatter_dimension=0, tiled=True),
        lax.psum_scatter(value_w_grad, ("group", "expert"), scatter_dimension=0, tiled=True),
        lax.psum_scatter(query_gain_grad, ("group", "expert"), scatter_dimension=0, tiled=True),
        lax.psum_scatter(key_gain_grad, ("group", "expert"), scatter_dimension=0, tiled=True),
        lax.psum_scatter(out_w_grad, ("group", "expert"), scatter_dimension=0, tiled=True),
        lax.psum_scatter(mlp_gain_grad, ("group", "expert"), scatter_dimension=0, tiled=True),
        lax.psum_scatter(router_w_grad, ("group", "expert"), scatter_dimension=0, tiled=True),
    )
    return (
        result[None],
        input_grad[None],
        dense_sums[0],
        dense_sums[1],
        dense_sums[2],
        dense_sums[3],
        dense_sums[4],
        dense_sums[5],
        dense_sums[6],
        dense_sums[7],
        dense_sums[8],
        gate_sum,
        up_sum,
        down_sum,
    )


def solution(mesh):
    return jax.shard_map(
        shards,
        mesh=mesh,
        in_specs=(
            P("expert", "group", None),
            P("expert", "group"),
            P("expert", "group", None),
            P("expert", "group", None),
            P(),
            P(),
            P(),
            P(),
            P(),
            P(),
            P(),
            P(),
            P(),
            P("expert", "group", None),
            P("expert", "group", None),
            P("expert", None, "group"),
        ),
        out_specs=(
            P("expert", "group", None),
            P("expert", "group", None),
            P(("group", "expert")),
            P(("group", "expert"), None),
            P(("group", "expert"), None),
            P(("group", "expert"), None),
            P(("group", "expert")),
            P(("group", "expert")),
            P(("group", "expert"), None),
            P(("group", "expert")),
            P(("group", "expert"), None),
            P("expert", "group", None),
            P("expert", "group", None),
            P("expert", None, "group"),
        ),
        check_vma=False,
    )
```

profile of v0, /device:TPU:0, one launch (start us, length us, event | category | flops | bytes accessed | tf_op | source)
XLA Modules:
  0.0 3003.4 jit_solution(1693062904540151108)
XLA Ops:
  33.7 22.6 all-gather
  56.7 39.2 %all-gather.9.cloned.1.call-done = bf16[1024,16,128]{2,0,1:T(8,128)(2,1)} async-done(((bf16[128,16,128]{2,0,1:T(8,128)(2,1)}), bf16[1024,16,128]{2,0,1:T(8,128)(2,1)}) %all-gather.9.cloned.1.call-update) | async-done | bytes 4194320 | tf_op jit(solution)/shard_map/all_gather | solution.py:134
  105.8 65.8 %all-gather.7.cloned.1.call-done = bf16[1024,16,128]{0,2,1:T(8,128)(2,1)} async-done(((bf16[128,16,128]{0,2,1:T(8,128)(2,1)}), bf16[1024,16,128]{0,2,1:T(8,128)(2,1)}) %all-gather.7.cloned.1.call-update) | async-done | bytes 4194320 | tf_op jit(solution)/shard_map/all_gather | solution.py:135
  214.1 23.5 scatter_custom_fusion
  242.4 35.4 %all-to-all-done.2 = bf16[4,340,2048]{2,1,0:T(8,128)(2,1)} async-done(((bf16[4,340,2048]{2,1,0:T(8,128)(2,1)}), bf16[4,340,2048]{2,1,0:T(8,128)(2,1)}, u32[]{:S(2)}, u32[]{:S(2)}) %all-to-all-start.2) | async-done | bytes 5570592 | tf_op jit(solution)/shard_map/all_to_all | solution.py:191
  288.9 57.6 %all-to-all-done = bf16[4,340,2048]{2,1,0:T(8,128)(2,1)} async-done(((bf16[4,340,2048]{2,1,0:T(8,128)(2,1)}), bf16[4,340,2048]{2,1,0:T(8,128)(2,1)}, u32[]{:S(2)}, u32[]{:S(2)}) %all-to-all-start) | async-done | bytes 5570592 | tf_op jit(solution)/shard_map/all_to_all | solution.py:165
  352.6 46.7 %all-gather.13.cloned.1.call-done = bf16[4,2048,1024]{2,1,0:T(8,128)(2,1)} async-done(((bf16[4,256,1024]{2,1,0:T(8,128)(2,1)}), bf16[4,2048,1024]{2,1,0:T(8,128)(2,1)}) %all-gather.13.cloned.1.call-update) | async-done | bytes 16777232 | tf_op jit(solution)/shard_map/all_gather | solution.py:157
  399.3 14.5 fusion.3
  413.9 213.0 %all-gather.11.cloned.1.call-done = bf16[4,2048,1024]{2,1,0:T(8,128)(2,1)} async-done(((bf16[4,256,1024]{2,1,0:T(8,128)(2,1)}), bf16[4,2048,1024]{2,1,0:T(8,128)(2,1)}) %all-gather.11.cloned.1.call-update) | async-done | bytes 16777232 | tf_op jit(solution)/shard_map/all_gather | solution.py:156
  626.8 14.5 fusion.7
  641.3 212.9 %all-gather.15.cloned.1.call-done = bf16[4,1024,2048]{2,1,0:T(8,128)(2,1)} async-done(((bf16[4,1024,256]{2,1,0:T(8,128)(2,1)}), bf16[4,1024,2048]{2,1,0:T(8,128)(2,1)}) %all-gather.15.cloned.1.call-update) | async-done | bytes 16777232 | tf_op jit(solution)/shard_map/all_gather | solution.py:158
  854.2 18.9 fusion.21
  873.1 12.8 convert_bitcast_fusion
  900.1 13.1 fusion.1
  913.1 15.3 fusion.18
  940.6 23.1 all-to-all-done.1
  991.5 41.0 %all-to-all-done.3 = bf16[4,340,2048]{2,1,0:T(8,128)(2,1)} async-done(((bf16[4,340,2048]{2,1,0:T(8,128)(2,1)}), bf16[4,340,2048]{2,1,0:T(8,128)(2,1)}, u32[]{:S(2)}, u32[]{:S(2)}) %all-to-all-start.3) | async-done | bytes 5570592 | tf_op jit(solution)/shard_map/all_to_all | solution.py:225
  1076.0 25.4 fusion.72
  1123.1 16.3 bitcast_convert_fusion
  1139.4 15.8 bitcast_convert_fusion.2
  1155.2 15.4 bitcast_convert_fusion.1
  1179.9 85.6 %reduce-scatter.28.cloned.1.call-done = bf16[128,4096]{1,0:T(8,128)(2,1)} async-done(((bf16[1024,4096]{1,0:T(8,128)(2,1)}), bf16[128,4096]{1,0:T(8,128)(2,1)}) %reduce-scatter.28.cloned.1.call-update) | async-done | bytes 1048592
  1274.9 23.2 fusion.75
  1334.0 69.5 %reduce-scatter.30.cloned.1.call-done = f32[64,16]{1,0:T(8,128)} async-done(((f32[2048,16]{1,0:T(8,128)}), f32[64,16]{1,0:T(8,128)}) %reduce-scatter.30.cloned.1.call-update) | async-done | bytes 4112
  1420.9 40.7 %all-reduce.8 = (f32[2048]{0:T(1024)S(1)}, f32[2048]{0:T(1024)S(1)}, f32[2048]{0:T(1024)S(1)}, f32[2048]{0:T(1024)S(1)}) all-reduce(f32[2048]{0:T(1024)S(1)} %get-tuple-element.22, f32[2048]{0:T(1024)S(1)} %get-tuple-element.20, f32[2048]{0:T(1024)S(1)} %get-tuple-element.18, ...), channel_id=4, replica_groups=mesh['group'=8,'expert'=4] {'group','expert'}, use_global_device_ids=true, to_apply=%region_25.26.clone | all-reduce | flops 8192 | bytes 65536
  1465.3 219.2 %reduce-scatter.26.cloned.1.call-done = bf16[4,1024,256]{2,1,0:T(8,128)(2,1)} async-done(((bf16[4,1024,2048]{2,1,0:T(8,128)(2,1)}), bf16[4,1024,256]{2,1,0:T(8,128)(2,1)}) %reduce-scatter.26.cloned.1.call-update) | async-done | bytes 2097168 | tf_op jit(solution)/shard_map/reduce_scatter | solution.py:304
  1688.5 278.6 %reduce-scatter.22.cloned.1.call-done = bf16[4,256,1024]{2,1,0:T(8,128)(2,1)} async-done(((bf16[4,2048,1024]{2,1,0:T(8,128)(2,1)}), bf16[4,256,1024]{2,1,0:T(8,128)(2,1)}) %reduce-scatter.22.cloned.1.call-update) | async-done | bytes 2097168 | tf_op jit(solution)/shard_map/reduce_scatter | solution.py:298
  1971.2 278.3 %reduce-scatter.24.cloned.1.call-done = bf16[4,256,1024]{2,1,0:T(8,128)(2,1)} async-done(((bf16[4,2048,1024]{2,1,0:T(8,128)(2,1)}), bf16[4,256,1024]{2,1,0:T(8,128)(2,1)}) %reduce-scatter.24.cloned.1.call-update) | async-done | bytes 2097168 | tf_op jit(solution)/shard_map/reduce_scatter | solution.py:301
  2253.5 180.9 %reduce-scatter.20.cloned.1.call-done = f32[64,2048]{1,0:T(8,128)} async-done(((f32[2048,2048]{1,0:T(8,128)}), f32[64,2048]{1,0:T(8,128)}) %reduce-scatter.20.cloned.1.call-update) | async-done | bytes 524304 | tf_op jit(solution)/shard_map/reduce_scatter | solution.py:315
  2434.4 187.4 %reduce-scatter.18.cloned.1.call-done = f32[64,2048]{1,0:T(8,128)} async-done(((f32[2048,2048]{1,0:T(8,128)}), f32[64,2048]{1,0:T(8,128)}) %reduce-scatter.18.cloned.1.call-update) | async-done | bytes 524304 | tf_op jit(solution)/shard_map/reduce_scatter | solution.py:312
  2621.8 187.5 %reduce-scatter.16.cloned.1.call-done = f32[64,2048]{1,0:T(8,128)} async-done(((f32[2048,2048]{1,0:T(8,128)}), f32[64,2048]{1,0:T(8,128)}) %reduce-scatter.16.cloned.1.call-update) | async-done | bytes 524304 | tf_op jit(solution)/shard_map/reduce_scatter | solution.py:311
  2809.3 187.4 %reduce-scatter.14.cloned.1.call-done = f32[64,2048]{1,0:T(8,128)} async-done(((f32[2048,2048]{1,0:T(8,128)}), f32[64,2048]{1,0:T(8,128)}) %reduce-scatter.14.cloned.1.call-update) | async-done | bytes 524304 | tf_op jit(solution)/shard_map/reduce_scatter | solution.py:310
  (290 shorter events, 307.4 us)
Async XLA Ops:
  7.2 178.4 %copy-start = (bf16[2048,16]{0,1:T(8,128)(2,1)S(1)}, bf16[2048,16]{0,1:T(8,128)(2,1)}, u32[]{:S(2)}) copy-start(bf16[2048,16]{0,1:T(8,128)(2,1)} %param.28) | copy-start | bytes 196612
  7.2 88.7 %all-gather.9.cloned.1.call-start = ((), (), s32[]{:S(2)}) async-start(), calls=%async_computation.14 | async-start | bytes 4718592 | tf_op jit(solution)/shard_map/all_gather | solution.py:134
  19.0 76.9 %copy-start.26 = (bf16[128,16,64]{2,0,1:T(8,128)(2,1)}, bf16[128,16,64]{2,0,1:T(8,128)(2,1)S(1)}, u32[]{:S(2)}) copy-start(bf16[128,16,64]{2,0,1:T(8,128)(2,1)S(1)} %get-tuple-element.33) | copy-start | bytes 786436
  19.0 76.9 %copy-start.28 = (bf16[128,16,64]{2,0,1:T(8,128)(2,1)}, bf16[128,16,64]{2,0,1:T(8,128)(2,1)S(1)}, u32[]{:S(2)}) copy-start(bf16[128,16,64]{2,0,1:T(8,128)(2,1)S(1)} %get-tuple-element.34) | copy-start | bytes 786436
  20.2 151.5 %all-gather.7.cloned.1.call-start = ((), (), s32[]{:S(2)}) async-start(), calls=%async_computation.13 | async-start | bytes 4718592 | tf_op jit(solution)/shard_map/all_gather | solution.py:135
  24.9 31.7 %copy-start.24 = (bf16[1,128,2048]{2,1,0:T(8,128)(2,1)S(1)}, bf16[1,128,2048]{2,1,0:T(8,128)(2,1)}, u32[]{:S(2)}) copy-start(bf16[1,128,2048]{2,1,0:T(8,128)(2,1)} %param.19) | copy-start | bytes 1572868
  26.0 373.4 %all-gather.13.cloned.1.call-start = ((), (), s32[]{:S(2)}) async-start(), calls=%async_computation.16 | async-start | bytes 18874368 | tf_op jit(solution)/shard_map/all_gather | solution.py:157
  26.7 600.1 %all-gather.11.cloned.1.call-start = ((), (), s32[]{:S(2)}) async-start(), calls=%async_computation.15 | async-start | bytes 18874368 | tf_op jit(solution)/shard_map/all_gather | solution.py:156
  27.3 827.0 %all-gather.15.cloned.1.call-start = ((), (), s32[]{:S(2)}) async-start(), calls=%async_computation.17 | async-start | bytes 18874368 | tf_op jit(solution)/shard_map/all_gather | solution.py:158
  56.6 115.1 %copy-start.22 = (pred[128,1024]{1,0:T(8,128)(4,1)}, pred[128,1024]{1,0:T(8,128)(4,1)S(1)}, u32[]{:S(2)}) copy-start(pred[128,1024]{1,0:T(8,128)(4,1)S(1)} %fusion.92) | copy-start | bytes 393220
  105.8 73.0 %copy-start.48 = (f32[16,128]{1,0:T(8,128)}, f32[16,128]{1,0:T(8,128)S(1)}, u32[]{:S(2)}) copy-start(f32[16,128]{1,0:T(8,128)S(1)} %log_add_fusion) | copy-start | bytes 24580
  208.6 69.2 %all-to-all-start.2 = ((bf16[4,340,2048]{2,1,0:T(8,128)(2,1)}), bf16[4,340,2048]{2,1,0:T(8,128)(2,1)}, u32[]{:S(2)}, u32[]{:S(2)}) async-start(bf16[4,340,2048]{2,1,0:T(8,128)(2,1)} %reshape.468), calls=%async_computation.2 | async-start | bytes 11272192 | tf_op jit(solution)/shard_map/all_to_all | solution.py:191
  277.7 68.8 %all-to-all-start = ((bf16[4,340,2048]{2,1,0:T(8,128)(2,1)}), bf16[4,340,2048]{2,1,0:T(8,128)(2,1)}, u32[]{:S(2)}, u32[]{:S(2)}) async-start(bf16[4,340,2048]{2,1,0:T(8,128)(2,1)} %reshape.464), calls=%async_computation | async-start | bytes 11272192 | tf_op jit(solution)/shard_map/all_to_all | solution.py:165
  894.9 68.8 %all-to-all-start.1 = ((bf16[4,340,2048]{2,1,0:T(8,128)(2,1)}), bf16[4,340,2048]{2,1,0:T(8,128)(2,1)}, u32[]{:S(2)}, u32[]{:S(2)}) async-start(bf16[4,340,2048]{2,1,0:T(8,128)(2,1)} %reshape.466), calls=%async_computation.1 | async-start | bytes 11272192 | tf_op jit(solution)/shard_map/all_to_all | solution.py:173
  963.7 68.8 %all-to-all-start.3 = ((bf16[4,340,2048]{2,1,0:T(8,128)(2,1)}), bf16[4,340,2048]{2,1,0:T(8,128)(2,1)}, u32[]{:S(2)}, u32[]{:S(2)}) async-start(bf16[4,340,2048]{2,1,0:T(8,128)(2,1)} %reshape.470), calls=%async_computation.3 | async-start | bytes 11272192 | tf_op jit(solution)/shard_map/all_to_all | solution.py:225
  968.8 296.7 %reduce-scatter.28.cloned.1.call-start = ((), (), s32[]{:S(2)}) async-start(), calls=%async_computation.25 | async-start | bytes 9437184
  1120.6 282.9 %reduce-scatter.30.cloned.1.call-start = ((), (), s32[]{:S(2)}) async-start(), calls=%async_computation.26 | async-start | bytes 1081344
  1123.0 561.6 %reduce-scatter.26.cloned.1.call-start = ((), (), s32[]{:S(2)}) async-start(), calls=%async_computation.24 | async-start | bytes 18874368 | tf_op jit(solution)/shard_map/reduce_scatter | solution.py:304
  1139.3 827.7 %reduce-scatter.22.cloned.1.call-start = ((), (), s32[]{:S(2)}) async-start(), calls=%async_computation.22 | async-start | bytes 18874368 | tf_op jit(solution)/shard_map/reduce_scatter | solution.py:298
  1155.2 1094.3 %reduce-scatter.24.cloned.1.call-start = ((), (), s32[]{:S(2)}) async-start(), calls=%async_computation.23 | async-start | bytes 18874368 | tf_op jit(solution)/shard_map/reduce_scatter | solution.py:301
  1170.6 1263.8 %reduce-scatter.20.cloned.1.call-start = ((), (), s32[]{:S(2)}) async-start(), calls=%async_computation.21 | async-start | bytes 17301504 | tf_op jit(solution)/shard_map/reduce_scatter | solution.py:315
  1179.7 85.8 %copy-start.3 = (bf16[1,128,2048]{2,1,0:T(8,128)(2,1)S(1)}, bf16[1,128,2048]{2,1,0:T(8,128)(2,1)}, u32[]{:S(2)}) copy-start(bf16[1,128,2048]{2,1,0:T(8,128)(2,1)} %param.16) | copy-start | bytes 1572868
  1179.7 85.8 %copy-start.20 = (f32[2048]{0:T(1024)S(1)}, f32[2048]{0:T(1024)}, u32[]{:S(2)}) copy-start(f32[2048]{0:T(1024)} %param.20) | copy-start | bytes 24580
  1179.7 85.8 %copy-start.39 = (f32[128]{0:T(128)S(1)}, f32[128]{0:T(128)}, u32[]{:S(2)}) copy-start(f32[128]{0:T(128)} %copy-done.38) | copy-start | bytes 1540
  1179.7 1442.0 %reduce-scatter.18.cloned.1.call-start = ((), (), s32[]{:S(2)}) async-start(), calls=%async_computation.20 | async-start | bytes 17301504 | tf_op jit(solution)/shard_map/reduce_scatter | solution.py:312
  1274.8 32.3 %copy-start.33 = (f32[128,64]{1,0:T(8,128)S(1)}, f32[128,64]{1,0:T(8,128)}, u32[]{:S(2)}) copy-start(f32[128,64]{1,0:T(8,128)} %copy-done.32) | copy-start | bytes 98308
  1274.9 32.3 %copy-start.35 = (f32[128,64]{1,0:T(8,128)S(1)}, f32[128,64]{1,0:T(8,128)}, u32[]{:S(2)}) copy-start(f32[128,64]{1,0:T(8,128)} %copy-done.34) | copy-start | bytes 98308
  1274.9 1534.4 %reduce-scatter.16.cloned.1.call-start = ((), (), s32[]{:S(2)}) async-start(), calls=%async_computation.19 | async-start | bytes 17301504 | tf_op jit(solution)/shard_map/reduce_scatter | solution.py:311
  1320.5 1676.1 %reduce-scatter.14.cloned.1.call-start = ((), (), s32[]{:S(2)}) async-start(), calls=%async_computation.18 | async-start | bytes 17301504 | tf_op jit(solution)/shard_map/reduce_scatter | solution.py:310
  1334.0 77.4 %copy-start.15 = (bf16[128,2048]{1,0:T(8,128)(2,1)S(1)}, bf16[128,2048]{1,0:T(8,128)(2,1)}, u32[]{:S(2)}) copy-start(bf16[128,2048]{1,0:T(8,128)(2,1)} %copy-done.14) | copy-start | bytes 1572868
  1417.8 46.2 %copy-start.64 = (f32[128]{0:T(128)S(1)}, f32[128]{0:T(128)}, u32[]{:S(2)}) copy-start(f32[128]{0:T(128)} %copy-done.63) | copy-start | bytes 1540
  1464.0 1532.6 %copy-start.1 = (bf16[2048,16]{0,1:T(8,128)(2,1)S(1)}, bf16[2048,16]{0,1:T(8,128)(2,1)}, u32[]{:S(2)}) copy-start(bf16[2048,16]{0,1:T(8,128)(2,1)} %param.28) | copy-start | bytes 196612
  (57 other events, 438.7 us)
Sparse Core Ops, SparseCore 0:
  20.3 75.5 all-gather.8
  98.5 73.1 all-gather.6
  173.8 225.4 all-gather.12
  401.4 225.4 all-gather.10
  628.7 225.4 all-gather.14
  1120.7 144.7 reduce-scatter.27
  1267.8 135.6 reduce-scatter.29
  1407.3 277.2 reduce-scatter.25
  1688.3 278.6 reduce-scatter.21
  1970.7 278.6 reduce-scatter.23
  2252.3 182.0 reduce-scatter.19
  2437.1 184.6 reduce-scatter.17
  2624.6 184.5 reduce-scatter.15
  2812.0 184.5 reduce-scatter.13
where the time goes:
time: 3010 us; the launch traced here: 3000 us
  waiting for transfers between devices  2410 us (80%)
  matrix products  285 us (9%)
  local copies, waits for them, and re-layouts  144 us (5%)
  other arithmetic  63.6 us (2%)
  blocking collectives  63.3 us (2%)
    reduce_scatter x1, waiting for transfers between devices, shards(): lax.psum_scatter(gate_w_grad.astype(jnp.bfloat16), 'group', scatter_dimen...  279 us
    reduce_scatter x1, waiting for transfers between devices, shards(): lax.psum_scatter(up_w_grad.astype(jnp.bfloat16), 'group', scatter_dimensi...  278 us
    reduce_scatter x1, waiting for transfers between devices, shards(): lax.psum_scatter(down_w_grad.astype(jnp.bfloat16), 'group', scatter_dimen...  219 us
    all_gather x1, waiting for transfers between devices, shards(): lax.all_gather(w_gate, 'group', axis=1, tiled=True)  213 us
    all_gather x1, waiting for transfers between devices, shards(): lax.all_gather(w_down, 'group', axis=2, tiled=True)  213 us
    reduce_scatter x1, waiting for transfers between devices, shards(): lax.psum_scatter(key_w_grad, ('group', 'expert'), scatter_dimension=0, ti...  187 us
    reduce_scatter x1, waiting for transfers between devices, shards(): lax.psum_scatter(value_w_grad, ('group', 'expert'), scatter_dimension=0,...  187 us
    reduce_scatter x1, waiting for transfers between devices, shards(): lax.psum_scatter(query_w_grad, ('group', 'expert'), scatter_dimension=0,...  187 us
  transfers between devices with their start and end apart: 18, of which 18 were waited for; matrix products, arithmetic and copies ran while one was open for 11% of the time, Pallas kernels for 0%

commit v1 on v0

v1 whole, which is shorter than its diff:
```python
import math

import jax
import jax.numpy as jnp
from jax import lax
from jax.sharding import PartitionSpec as P

HEADS = 16
EPSILON = 1e-05
MASKED = -1000000000.0
BF16 = jnp.bfloat16
F32 = jnp.float32


def rms_norm(values_in, gain_vec):
    return (
        values_in
        * lax.rsqrt(jnp.mean(values_in * values_in, axis=-1, keepdims=True) + EPSILON)
        * gain_vec
    )


def angles(row_count, head_dim):
    places = jnp.arange(row_count, dtype=jnp.int32).astype(F32)
    frequency = jnp.exp(-math.log(10000.0) * 2.0 * jnp.arange(head_dim // 2, dtype=F32) / head_dim)
    turn_angle = places[:, None] * frequency[None, :]
    return (jnp.cos(turn_angle)[:, None, :], jnp.sin(turn_angle)[:, None, :])


def rotate(values_in, cosine, sine):
    half_dim = values_in.shape[-1] // 2
    first_half = values_in[..., :half_dim]
    second = values_in[..., half_dim:]
    return jnp.concatenate(
        [first_half * cosine - second * sine, second * cosine + first_half * sine], axis=-1
    )


def mm(left, right):
    return jnp.dot(left, right, preferred_element_type=F32)


def mm_tn(left, right):
    return lax.dot_general(left, right, (((0,), (0,)), ((), ())), preferred_element_type=F32)


def mm_nt(left, right):
    return lax.dot_general(left, right, (((1,), (1,)), ((), ())), preferred_element_type=F32)


def ein(spec, *ops):
    return jnp.einsum(spec, *ops, preferred_element_type=F32)


def shards(
    layer_in,
    segment_ids,
    routing,
    out_grad,
    attn_gain,
    w_query,
    w_key,
    w_value,
    query_gain,
    key_gain,
    w_out,
    mlp_gain,
    w_router,
    w_gate,
    w_up,
    w_down,
):
    groups = lax.axis_size("group")
    sources = lax.axis_size("expert")
    me = lax.axis_index("group")
    rows = layer_in.shape[1]
    width = layer_in.shape[2]
    length = rows * groups
    head_dim = width // HEADS
    heads = HEADS // groups
    cols = width // groups
    local_experts = w_gate.shape[0]
    experts = local_experts * sources
    hidden_size = w_gate.shape[2]
    parts = groups // local_experts
    part = hidden_size // parts
    score_scale = 1.0 / math.sqrt(head_dim)

    def gather(block):
        return lax.all_gather(block, "group", axis=0, tiled=True)

    def own_cols(matrix, axis):
        return lax.dynamic_slice_in_dim(matrix, me * cols, cols, axis)

    def slices_in(w):
        w = w.reshape(local_experts, w.shape[1], parts, part).transpose(0, 2, 1, 3)
        w = w.reshape(groups, w.shape[2], part)
        w = lax.all_to_all(w, "group", 0, 0, tiled=True).reshape(width, part)
        return lax.all_gather(w, "expert", axis=0, tiled=False)

    gate_w = slices_in(w_gate)
    up_w = slices_in(w_up)
    down_w = w_down.reshape(groups, part, cols)
    down_w = lax.all_to_all(down_w, "group", 0, 0, tiled=True).transpose(1, 0, 2)
    down_w = lax.all_gather(down_w.reshape(part, width), "expert", axis=0, tiled=False)

    inputs = layer_in[0].astype(F32)
    normed_b = rms_norm(inputs, attn_gain).astype(BF16)
    normed_all = gather(normed_b)
    seg_all = gather(segment_ids[0])
    route_all = gather(routing[0])
    grad_all = gather(out_grad[0])
    wq, wk, wv = own_cols(w_query, 1), own_cols(w_key, 1), own_cols(w_value, 1)
    query_raw, key_raw = mm(normed_all, wq), mm(normed_all, wk)
    values_b = mm(normed_all, wv).astype(BF16).reshape(length, heads, head_dim)
    squares = jnp.stack(
        [jnp.sum(query_raw * query_raw, axis=1), jnp.sum(key_raw * key_raw, axis=1)], axis=1
    )
    scales = lax.rsqrt(lax.psum(squares, "group") / width + EPSILON)
    query_scale, key_scale = scales[:, :1], scales[:, 1:]
    query_gain_c, key_gain_c = own_cols(query_gain, 0), own_cols(key_gain, 0)
    cosine, sine = angles(length, head_dim)

    def turned(raw, scale, gain):
        return rotate((raw * scale * gain).reshape(length, heads, head_dim), cosine, sine)

    queries_b = turned(query_raw, query_scale, query_gain_c).astype(BF16)
    keys_b = turned(key_raw, key_scale, key_gain_c).astype(BF16)
    place = jnp.arange(length, dtype=jnp.int32)
    allowed = (seg_all[:, None] == seg_all[None, :]) & (place[None, :] <= place[:, None])
    scores = jnp.where(allowed[None], ein("qhd,khd->hqk", queries_b, keys_b) * score_scale, MASKED)
    top_score = jnp.max(scores, axis=-1, keepdims=True)
    log_total = top_score + jnp.log(jnp.sum(jnp.exp(scores - top_score), axis=-1, keepdims=True))
    probs = jnp.exp(scores - log_total)
    probs_b = probs.astype(BF16)
    mixed_c = ein("hqk,khd->qhd", probs_b, values_b).reshape(length, cols).astype(BF16)
    mixed_b = lax.all_to_all(mixed_c, "group", 0, 1, tiled=True)
    resid = inputs + mm(mixed_b, w_out)
    normed_mlp_b = rms_norm(resid, mlp_gain).astype(BF16)
    mlp_all = gather(normed_mlp_b)

    expert_ids = jnp.arange(experts, dtype=jnp.int32)
    chosen = jnp.any(route_all[:, :, None] == expert_ids[None, None, :], axis=1)
    router_all = jax.nn.softmax(mm(mlp_all, w_router), axis=-1)
    picked = jnp.where(chosen, router_all, 0.0).reshape(length, sources, local_experts)
    picked = lax.dynamic_index_in_dim(picked, me // parts, 2, keepdims=True)
    gate_pre = ein("td,edf->tef", mlp_all, gate_w)
    up_pre = ein("td,edf->tef", mlp_all, up_w)
    sigma = jax.nn.sigmoid(gate_pre)
    hidden = gate_pre * sigma * up_pre
    hidden_b = (hidden * picked).astype(BF16)
    out_part = ein("tef,efd->td", hidden_b, down_w).astype(BF16)
    mixture = lax.psum_scatter(out_part, "group", scatter_dimension=0, tiled=True)
    hidden_grad = ein("td,efd->tef", grad_all, down_w)
    picked_grad = jnp.sum(hidden * hidden_grad, axis=2)
    hidden_grad = hidden_grad * picked
    gate_grad_b = (hidden_grad * up_pre * sigma * (1.0 + gate_pre * (1.0 - sigma))).astype(BF16)
    up_grad_b = (hidden_grad * gate_pre * sigma).astype(BF16)
    slot_part = ein("tef,edf->td", gate_grad_b, gate_w) + ein("tef,edf->td", up_grad_b, up_w)
    slot_sum = lax.psum_scatter(slot_part.astype(BF16), "group", scatter_dimension=0, tiled=True)
    own_expert = jnp.arange(local_experts, dtype=jnp.int32) == me // parts
    full_part = jnp.where(own_expert[None, None, :], picked_grad[:, :, None], 0.0)
    full_part = jnp.where(chosen, full_part.reshape(length, experts), 0.0)
    router_full_grad = lax.psum_scatter(full_part, "group", scatter_dimension=0, tiled=True)
    gate_w_part = ein("td,tef->edf", mlp_all, gate_grad_b).astype(BF16)
    up_w_part = ein("td,tef->edf", mlp_all, up_grad_b).astype(BF16)
    down_w_part = ein("tef,td->efd", hidden_b, grad_all).astype(BF16)

    def slices_out(w):
        w = lax.psum_scatter(w, "expert", scatter_dimension=0, tiled=False)
        w = lax.all_to_all(w.reshape(groups, cols, part), "group", 0, 0, tiled=True)
        w = w.reshape(local_experts, parts, cols, part).transpose(0, 2, 1, 3)
        return w.reshape(local_experts, cols, hidden_size).astype(F32)

    gate_sum = slices_out(gate_w_part)
    up_sum = slices_out(up_w_part)
    down_sum = lax.psum_scatter(down_w_part, "expert", scatter_dimension=0, tiled=False)
    down_sum = down_sum.reshape(part, groups, cols).transpose(1, 0, 2)
    down_sum = lax.all_to_all(down_sum, "group", 0, 0, tiled=True)
    down_sum = down_sum.reshape(local_experts, hidden_size, cols).astype(F32)

    result = (resid + mixture.astype(F32)).astype(BF16)
    grad_out = out_grad[0].astype(F32)
    router = jax.nn.softmax(mm(normed_mlp_b, w_router), axis=-1)
    logits_grad_b = (
        router * (router_full_grad - jnp.sum(router * router_full_grad, axis=-1, keepdims=True))
    ).astype(BF16)
    router_w_grad = mm_tn(normed_mlp_b, logits_grad_b)
    mlp_in_grad = slot_sum.astype(F32) + mm_nt(logits_grad_b, w_router)
    _, mlp_back = jax.vjp(rms_norm, resid, mlp_gain)
    resid_part, mlp_gain_grad = mlp_back(mlp_in_grad)
    resid_grad = grad_out + resid_part
    attn_grad_b = resid_grad.astype(BF16)
    attn_grad_all = gather(attn_grad_b)
    out_w_part = mm_tn(mixed_c, attn_grad_all).astype(BF16)
    out_w_grad = lax.psum_scatter(out_w_part, "expert", scatter_dimension=0, tiled=True)
    mixed_grad_b = mm_nt(attn_grad_b, w_out).astype(BF16)
    mixed_grad_c = lax.all_to_all(mixed_grad_b, "group", 1, 0, tiled=True)
    mixed_grad_c = mixed_grad_c.reshape(length, heads, head_dim)

    prob_grad = ein("qhd,khd->hqk", mixed_grad_c, values_b)
    delta = jnp.sum(probs * prob_grad, axis=-1, keepdims=True)
    score_grad_b = (probs * (prob_grad - delta) * score_scale).astype(BF16)
    query_grad = ein("hqk,khd->qhd", score_grad_b, keys_b)
    key_grad = ein("hqk,qhd->khd", score_grad_b, queries_b)
    value_grad_b = ein("hqk,qhd->khd", probs_b, mixed_grad_c).astype(BF16).reshape(length, cols)

    def unturned(grad):
        return rotate(grad, cosine, -sine).reshape(length, cols)

    query_turn, key_turn = unturned(query_grad), unturned(key_grad)
    query_mix, key_mix = query_turn * query_gain_c, key_turn * key_gain_c
    dots = jnp.stack(
        [jnp.sum(query_mix * query_raw, axis=1), jnp.sum(key_mix * key_raw, axis=1)], axis=1
    )
    dots = lax.psum(dots, "group") / width
    query_raw_b = (
        query_scale * query_mix - query_raw * query_scale**3 * dots[:, :1]
    ).astype(BF16)
    key_raw_b = (key_scale * key_mix - key_raw * key_scale**3 * dots[:, 1:]).astype(BF16)
    query_gain_part = jnp.sum(query_turn * query_raw * query_scale, axis=0)
    key_gain_part = jnp.sum(key_turn * key_raw * key_scale, axis=0)
    raw_grads = jnp.concatenate([query_raw_b, key_raw_b, value_grad_b], axis=1)
    qkv_part = mm_tn(normed_all, raw_grads).astype(BF16).reshape(groups, sources, -1, 3 * cols)
    qkv_part = lax.psum_scatter(qkv_part, "expert", scatter_dimension=1, tiled=False)
    qkv_part = lax.all_to_all(qkv_part, "group", 0, 0, tiled=True)
    qkv_part = qkv_part.transpose(1, 0, 2).reshape(-1, groups, 3, cols).astype(F32)
    gain_part = jnp.stack([query_gain_part, key_gain_part])
    gain_grads = lax.psum_scatter(gain_part, "expert", scatter_dimension=1, tiled=True)
    raw_own = lax.all_to_all(raw_grads, "group", 0, 1, tiled=True).reshape(rows, groups, 3, cols)
    normed_grad = (
        mm_nt(raw_own[:, :, 0].reshape(rows, width), w_query)
        + mm_nt(raw_own[:, :, 1].reshape(rows, width), w_key)
        + mm_nt(raw_own[:, :, 2].reshape(rows, width), w_value)
    )
    _, attn_back = jax.vjp(rms_norm, inputs, attn_gain)
    input_part, attn_gain_grad = attn_back(normed_grad)
    input_grad = resid_grad + input_part
    small = jnp.concatenate(
        [router_w_grad, mlp_gain_grad[:, None], attn_gain_grad[:, None]], axis=1
    )
    small = lax.psum_scatter(small, ("group", "expert"), scatter_dimension=0, tiled=True)
    return (
        result[None],
        input_grad[None],
        small[:, experts + 1],
        qkv_part[:, :, 0].reshape(-1, width),
        qkv_part[:, :, 1].reshape(-1, width),
        qkv_part[:, :, 2].reshape(-1, width),
        gain_grads[0],
        gain_grads[1],
        out_w_grad.astype(F32),
        small[:, experts],
        small[:, :experts],
        gate_sum,
        up_sum,
        down_sum,
    )


def solution(mesh):
    token = P("expert", "group", None)
    every = P(("group", "expert"))
    return jax.shard_map(
        shards,
        mesh=mesh,
        in_specs=(token, P("expert", "group"), token, token)
        + (P(),) * 9
        + (token, token, P("expert", None, "group")),
        out_specs=(token, token)
        + (every,) * 9
        + (token, token, P("expert", None, "group")),
        check_vma=False,
    )
```

time: 3010 us -> 1500 us (0.50)
  waiting for transfers between devices: 2410 us -> 741 us
  blocking collectives: 63.3 us -> 337 us
  local copies, waits for them, and re-layouts: 144 us -> 84.8 us
  matrix products: 285 us -> 243 us
    reduce_scatter x7 -> x8, waiting for transfers between devices: 1520 us -> 330 us  [the longest x2 109 us: slices_out(): w = lax.psum_scatter(w, 'expert', scatter_dimension=0, tiled=False)]
    all_gather x5 -> x7, waiting for transfers between devices: 578 us -> 228 us  [the longest x4 137 us: gather(): return lax.all_gather(block, 'group', axis=0, tiled=True)]
    all_to_all x0 -> x5, blocking collectives: none -> 243 us  [the longest x2 161 us: slices_in(): w = lax.all_to_all(w, 'group', 0, 0, tiled=True).reshape(width, part)]
    all_to_all x4 -> x5, waiting for transfers between devices: 157 us -> 31.3 us  [the longest x1 31.3 us: shards(): lax.all_to_all(raw_grads, 'group', 0, 1, tiled=True)]
    unnamed x1 -> x0, blocking collectives: 40.7 us -> none
    dot_general x29, matrix products: 283 us -> 243 us  [the longest x15 185 us: ein(): return jnp.einsum(spec, *ops, preferred_element_type=F32)]
    psum x0 -> x2, blocking collectives: none -> 39.6 us  [the longest x1 20.2 us: shards(): dots = lax.psum(dots, 'group') / width]
    reshape x10 -> x5, local copies, waits for them, and re-layouts: 45 us -> 6.88 us  [the longest x2 4.76 us: slices_in(): w = w.reshape(groups, w.shape[2], part)]
  transfers between devices with their start and end apart: 18 -> 22, of which waited for: 18 -> 14; matrix products, arithmetic and copies ran while one was open for 11% -> 15% of each run, Pallas kernels for 0% -> 0%
where the time goes in v1:
time: 1500 us; the launch traced here: 1490 us
  waiting for transfers between devices  741 us (49%)
  blocking collectives  337 us (22%)
  matrix products  243 us (16%)
  local copies, waits for them, and re-layouts  84.8 us (6%)
  other arithmetic  42.2 us (3%)
  starting transfers between devices  25.4 us (2%)
  between operations  15.5 us (1%)
    dot_general x15, matrix products, ein(): return jnp.einsum(spec, *ops, preferred_element_type=F32)  185 us
    all_to_all x2, blocking collectives, slices_in(): w = lax.all_to_all(w, 'group', 0, 0, tiled=True).reshape(width, part)  161 us
    unnamed x19, waiting for transfers between devices  152 us
    all_gather x4, waiting for transfers between devices, gather(): return lax.all_gather(block, 'group', axis=0, tiled=True)  137 us
    reduce_scatter x2, waiting for transfers between devices, slices_out(): w = lax.psum_scatter(w, 'expert', scatter_dimension=0, tiled=False)  109 us
    reduce_scatter x1, waiting for transfers between devices, shards(): lax.psum_scatter(out_part, 'group', scatter_dimension=0, tiled=True)  90.3 us
    reduce_scatter x1, waiting for transfers between devices, shards(): lax.psum_scatter(slot_part.astype(BF16), 'group', scatter_dimension=0, ti...  90.2 us
    all_gather x2, blocking collectives, gather(): return lax.all_gather(block, 'group', axis=0, tiled=True)  54.7 us
  transfers between devices with their start and end apart: 22, of which 14 were waited for; matrix products, arithmetic and copies ran while one was open for 15% of the time, Pallas kernels for 0%

profile of v1, /device:TPU:0, one launch (start us, length us, event | category | flops | bytes accessed | tf_op | source)
XLA Modules:
  0.0 1489.4 jit_solution(15747274927207068161)
XLA Ops:
  13.1 22.8 %all-gather = s32[1,1024]{1,0:T(1,128)S(1)} all-gather(s32[1,128]{1,0:T(1,128)} %param.17), channel_id=2, replica_groups=mesh['group'=8,'expert'=4] {'group'}, dimensions={1}, use_global_device_ids=true | all-gather | bytes 4608 | tf_op jit(solution)/shard_map/all_gather | solution.py:90
  40.5 46.7 %all-gather.11.cloned.1.call-done = bf16[1024,2048]{1,0:T(8,128)(2,1)} async-done(((bf16[128,2048]{1,0:T(8,128)(2,1)}), bf16[1024,2048]{1,0:T(8,128)(2,1)}) %all-gather.11.cloned.1.call-update) | async-done | bytes 4194320 | tf_op jit(solution)/shard_map/all_gather | solution.py:90
  94.2 19.4 %psum.14 = f32[1024,2]{0,1:T(2,128)S(1)} all-reduce(f32[1024,2]{0,1:T(2,128)S(1)} %pad_maximum_fusion.12), channel_id=1, replica_groups=mesh['group'=8,'expert'=4] {'group'}, use_global_device_ids=true, to_apply=%region_3.0 | all-reduce | flops 2048 | bytes 16384 | tf_op jit(solution)/shard_map/psum | solution.py:119
  139.7 13.4 all_to_all.80
  158.5 93.3 %all_to_all.81 = bf16[8,256,512]{1,2,0:T(8,128)(2,1)S(1)} all-to-all(bf16[8,256,512]{1,2,0:T(8,128)(2,1)} %copy.211), channel_id=1, replica_groups=mesh['group'=8,'expert'=4] {'group'}, dimensions={0} | all-to-all | bytes 4194304 | tf_op jit(solution)/shard_map/all_to_all | solution.py:98
  254.8 49.5 %all_to_all.82 = bf16[8,512,256]{2,1,0:T(8,128)(2,1)} all-to-all(bf16[8,512,256]{2,1,0:T(8,128)(2,1)} %bitcast.252), channel_id=1, replica_groups=mesh['group'=8,'expert'=4] {'group'}, dimensions={0} | all-to-all | bytes 4194304 | tf_op jit(solution)/shard_map/all_to_all | solution.py:104
  313.9 67.8 %all_to_all.83 = bf16[8,256,512]{1,2,0:T(8,128)(2,1)S(1)} all-to-all(bf16[8,256,512]{1,2,0:T(8,128)(2,1)} %copy.208), channel_id=1, replica_groups=mesh['group'=8,'expert'=4] {'group'}, dimensions={0} | all-to-all | bytes 4194304 | tf_op jit(solution)/shard_map/all_to_all | solution.py:98
  384.2 31.8 %all-gather.1 = s32[1,1024,8]{1,2,0:T(8,128)S(1)} all-gather(s32[1,128,8]{1,2,0:T(8,128)S(1)} %copy-done.59), channel_id=3, replica_groups=mesh['group'=8,'expert'=4] {'group'}, dimensions={1}, use_global_device_ids=true | all-gather | bytes 36864 | tf_op jit(solution)/shard_map/all_gather | solution.py:90
  419.7 14.6 fusion.18
  434.4 45.0 %all-gather.19.cloned.1.call-done = bf16[4,512,2048]{2,1,0:T(8,128)(2,1)} async-done(((bf16[1,512,2048]{2,1,0:T(8,128)(2,1)}), bf16[4,512,2048]{2,1,0:T(8,128)(2,1)}) %all-gather.19.cloned.1.call-update) | async-done | bytes 8388624 | tf_op jit(solution)/shard_map/all_gather | solution.py:105
  479.3 14.6 fusion.14
  493.9 45.7 %all-gather.15.cloned.1.call-done = bf16[4,2048,512]{2,1,0:T(8,128)(2,1)} async-done(((bf16[1,2048,512]{2,1,0:T(8,128)(2,1)}), bf16[4,2048,512]{2,1,0:T(8,128)(2,1)}) %all-gather.15.cloned.1.call-update) | async-done | bytes 8388624 | tf_op jit(solution)/shard_map/all_gather | solution.py:99
  539.6 21.2 %multiply_convert_fusion.2 = (bf16[1024,4,512]{0,2,1:T(8,128)(2,1)}, f32[1024,4]{0,1:T(4,128)S(1)}, bf16[1024,4,512]{0,2,1:T(8,128)(2,1)}, f32[1024,4,512]{0,2,1:T(8,128)}) fusion(f32[1024,4,512]{0,2,1:T(8,128)} %fusion.18, f32[1024,4,512]{0,2,1:T(8,128)} %fusion.14, f32[1024,4]{0,1:T(4,128)S(1)} %bitcast.295, ...), kind=kOutput, calls=%fused_computation.11 | convolution fusion | flops 8627679232 | bytes 46170112 | tf_op jit(solution)/shard_map/td,edf->tef/dot_general | solution.py:52
  561.7 12.9 fusion.107
  574.7 12.8 fusion.1
  587.8 28.8 %reduce-scatter.19.cloned.1.call-done = f32[128,16]{0,1:T(8,128)} async-done(((f32[1024,16]{0,1:T(8,128)}), f32[128,16]{0,1:T(8,128)}) %reduce-scatter.19.cloned.1.call-update) | async-done | bytes 8208 | tf_op jit(solution)/shard_map/reduce_scatter | solution.py:164
  618.0 90.2 %reduce-scatter.17.cloned.1.call-done = bf16[128,2048]{1,0:T(8,128)(2,1)} async-done(((bf16[1024,2048]{1,0:T(8,128)(2,1)}), bf16[128,2048]{1,0:T(8,128)(2,1)}) %reduce-scatter.17.cloned.1.call-update) | async-done | bytes 524304 | tf_op jit(solution)/shard_map/reduce_scatter | solution.py:160
  718.4 18.9 %all_to_all.84 = bf16[128,8,256]{0,2,1:T(8,128)(2,1)S(1)} all-to-all(bf16[128,8,256]{0,2,1:T(8,128)(2,1)S(1)} %bitcast.258), channel_id=1, replica_groups=mesh['group'=8,'expert'=4] {'group'}, dimensions={1} | all-to-all | bytes 1048576 | tf_op jit(solution)/shard_map/all_to_all | solution.py:198
  750.4 15.2 %fusion.44 = f32[1024,2,128]{2,0,1:T(8,128)} fusion(f32[2,1024,1024]{1,2,0:T(8,128)} %fusion.108, f32[2,1024,1024]{1,2,0:T(8,128)} %copy-done.14, f32[2,1024]{1,0:T(2,128)S(1)} %log_add_fusion, pred[1024,1024]{0,1:T(8,128)(4,1)S(1)} %copy-done.24, bf16[1024,2,64]{2,0,1:T(8,128)(2,1)S(1)} %copy-done.35, bf16[1024,2,64]{2,0,1:T(8,128)(2,1)S(1)} %copy-done.37), kind=kOutput, calls=%fused_computation.66 | convolution fusion | flops 560991232 | bytes 19406848 | tf_op jit(solution)/shard_map/hqk,khd->qhd/dot_general | solution.py:52
  765.6 13.9 fusion.47
  788.1 20.2 %psum.15 = f32[1024,2]{0,1:T(2,128)S(1)} all-reduce(f32[1024,2]{0,1:T(2,128)S(1)} %pad_maximum_fusion.13), channel_id=1, replica_groups=mesh['group'=8,'expert'=4] {'group'}, use_global_device_ids=true, to_apply=%region_21.22 | all-reduce | flops 2048 | bytes 16384 | tf_op jit(solution)/shard_map/psum | solution.py:216
  817.9 16.8 %convolution_convert_fusion = bf16[4,512,2048]{2,1,0:T(8,128)(2,1)} fusion(bf16[1,1024,2048]{2,1,0:T(8,128)(2,1)} %all-gather.23.cloned.1.call-done, f32[1024,4]{0,1:T(4,128)S(1)} %bitcast.296, f32[1024,4,512]{0,2,1:T(8,128)} %fusion.18, f32[1024,4,512]{0,2,1:T(8,128)} %get-tuple-element.76), kind=kOutput, calls=%fused_computation.19 | convolution fusion | flops 8608808960 | bytes 29376512 | tf_op jit(solution)/shard_map/tef,td->efd/dot_general | solution.py:52
  834.7 14.0 convert_bitcast_fusion.1
  849.0 14.1 convert_bitcast_fusion
  870.5 31.3 %all-to-all-done.5 = bf16[8,128,768]{1,2,0:T(8,128)(2,1)S(1)} async-done(((bf16[8,128,768]{1,2,0:T(8,128)(2,1)}), bf16[8,128,768]{1,2,0:T(8,128)(2,1)S(1)}, u32[]{:S(2)}, u32[]{:S(2)}) %all-to-all-start.5) | async-done | bytes 1572896 | tf_op jit(solution)/shard_map/all_to_all | solution.py:230
  905.4 17.2 %bitcast_convert_fusion = bf16[1024,2048]{1,0:T(8,128)(2,1)} fusion(bf16[4,512,2048]{2,1,0:T(8,128)(2,1)} %all-gather.19.cloned.1.call-done, f32[1024,4]{0,1:T(4,128)S(1)} %bitcast.297, f32[1024,4,512]{0,2,1:T(8,128)} %fusion.18, f32[1024,4,512]{0,2,1:T(8,128)} %get-tuple-element.76), kind=kOutput, calls=%fused_computation.3 | convolution fusion | flops 8606711808 | bytes 29376512 | tf_op jit(solution)/shard_map/tef,efd->td/dot_general | solution.py:52
  937.8 63.2 %reduce-scatter.25.cloned.1.call-done = bf16[1,2048,512]{1,2,0:T(8,128)(2,1)} async-done(((bf16[4,2048,512]{1,2,0:T(8,128)(2,1)}), bf16[1,2048,512]{1,2,0:T(8,128)(2,1)}) %reduce-scatter.25.cloned.1.call-update) | async-done | bytes 2097168 | tf_op jit(solution)/shard_map/reduce_scatter | solution.py:170
  1028.9 46.0 %reduce-scatter.27.cloned.1.call-done = bf16[1,2048,512]{1,2,0:T(8,128)(2,1)} async-done(((bf16[4,2048,512]{1,2,0:T(8,128)(2,1)}), bf16[1,2048,512]{1,2,0:T(8,128)(2,1)}) %reduce-scatter.27.cloned.1.call-update) | async-done | bytes 2097168 | tf_op jit(solution)/shard_map/reduce_scatter | solution.py:170
  1095.1 90.1 %all-gather.21.cloned.1.call-done = bf16[1024,2048]{1,0:T(8,128)(2,1)} async-done(((bf16[128,2048]{1,0:T(8,128)(2,1)}), bf16[1024,2048]{1,0:T(8,128)(2,1)}) %all-gather.21.cloned.1.call-update) | async-done | bytes 4194320 | tf_op jit(solution)/shard_map/all_gather | solution.py:90
  1189.8 15.1 %reduce-scatter.33.cloned.1.call-done = f32[64,2]{1,0:T(8,128)} async-done(((f32[256,2]{1,0:T(8,128)}), f32[64,2]{1,0:T(8,128)}) %reduce-scatter.33.cloned.1.call-update) | async-done | bytes 528
  1207.0 90.3 %reduce-scatter.15.cloned.1.call-done = bf16[128,2048]{1,0:T(8,128)(2,1)} async-done(((bf16[1024,2048]{1,0:T(8,128)(2,1)}), bf16[128,2048]{1,0:T(8,128)(2,1)}) %reduce-scatter.15.cloned.1.call-update) | async-done | bytes 524304 | tf_op jit(solution)/shard_map/reduce_scatter | solution.py:153
  1300.3 135.8 %reduce-scatter.31.cloned.1.call-done = f32[64,18]{1,0:T(8,128)} async-done(((f32[2048,18]{1,0:T(8,128)}), f32[64,18]{1,0:T(8,128)}) %reduce-scatter.31.cloned.1.call-update) | async-done | bytes 4624
  (315 shorter events, 241.4 us)
Async XLA Ops:
  7.2 409.0 %copy-start = (bf16[2048,16]{0,1:T(8,128)(2,1)S(1)}, bf16[2048,16]{0,1:T(8,128)(2,1)}, u32[]{:S(2)}) copy-start(bf16[2048,16]{0,1:T(8,128)(2,1)} %param.28) | copy-start | bytes 196612
  7.2 80.0 %all-gather.11.cloned.1.call-start = ((), (), s32[]{:S(2)}) async-start(), calls=%async_computation.20 | async-start | bytes 4718592 | tf_op jit(solution)/shard_map/all_gather | solution.py:90
  11.6 404.6 %all-gather.13.cloned.1.call-start = ((), (), s32[]{:S(2)}) async-start(), calls=%async_computation.21 | async-start | bytes 4718592 | tf_op jit(solution)/shard_map/all_gather | solution.py:90
  154.6 555.8 %copy-start.2 = (f32[128,2048]{1,0:T(8,128)}, f32[128,2048]{1,0:T(8,128)S(1)}, u32[]{:S(2)}) copy-start(f32[128,2048]{1,0:T(8,128)S(1)} %get-tuple-element.73) | copy-start | bytes 3145732
  154.6 555.8 %copy-start.55 = (f32[128]{0:T(128)}, f32[128]{0:T(128)S(1)}, u32[]{:S(2)}) copy-start(f32[128]{0:T(128)S(1)} %fusion.81) | copy-start | bytes 1540
  155.7 264.0 %all-gather.17.cloned.1.call-start = ((), (), s32[]{:S(2)}) async-start(), calls=%async_computation.23 | async-start | bytes 10485760 | tf_op jit(solution)/shard_map/all_gather | solution.py:99
  254.2 180.2 %all-gather.23.cloned.1.call-start = ((), (), s32[]{:S(2)}) async-start(), calls=%async_computation.34 | async-start | bytes 4718592 | tf_op jit(solution)/shard_map/all_gather | solution.py:90
  254.8 224.6 %all-gather.19.cloned.1.call-start = ((), (), s32[]{:S(2)}) async-start(), calls=%async_computation.24 | async-start | bytes 10485760 | tf_op jit(solution)/shard_map/all_gather | solution.py:105
  309.6 230.0 %all-gather.15.cloned.1.call-start = ((), (), s32[]{:S(2)}) async-start(), calls=%async_computation.22 | async-start | bytes 10485760 | tf_op jit(solution)/shard_map/all_gather | solution.py:99
  384.1 232.5 %reduce-scatter.19.cloned.1.call-start = ((), (), s32[]{:S(2)}) async-start(), calls=%async_computation.27 | async-start | bytes 73728 | tf_op jit(solution)/shard_map/reduce_scatter | solution.py:164
  561.6 146.5 %reduce-scatter.17.cloned.1.call-start = ((), (), s32[]{:S(2)}) async-start(), calls=%async_computation.26 | async-start | bytes 4718592 | tf_op jit(solution)/shard_map/reduce_scatter | solution.py:160
  574.6 136.7 %copy-start.20 = (bf16[1,128,2048]{2,1,0:T(8,128)(2,1)S(1)}, bf16[1,128,2048]{2,1,0:T(8,128)(2,1)}, u32[]{:S(2)}) copy-start(bf16[1,128,2048]{2,1,0:T(8,128)(2,1)} %param.19) | copy-start | bytes 1572868
  587.5 314.3 %reduce-scatter.21.cloned.1.call-start = ((), (), s32[]{:S(2)}) async-start(), calls=%async_computation.28 | async-start | bytes 3932160 | tf_op jit(solution)/shard_map/reduce_scatter | solution.py:225
  817.9 109.2 %reduce-scatter.29.cloned.1.call-start = ((), (), s32[]{:S(2)}) async-start(), calls=%async_computation.33 | async-start | bytes 10485760 | tf_op jit(solution)/shard_map/reduce_scatter | solution.py:177
  834.7 166.3 %reduce-scatter.25.cloned.1.call-start = ((), (), s32[]{:S(2)}) async-start(), calls=%async_computation.31 | async-start | bytes 10485760 | tf_op jit(solution)/shard_map/reduce_scatter | solution.py:170
  848.7 226.2 %reduce-scatter.27.cloned.1.call-start = ((), (), s32[]{:S(2)}) async-start(), calls=%async_computation.32 | async-start | bytes 10485760 | tf_op jit(solution)/shard_map/reduce_scatter | solution.py:170
  863.0 322.2 %all-gather.21.cloned.1.call-start = ((), (), s32[]{:S(2)}) async-start(), calls=%async_computation.29 | async-start | bytes 4718592 | tf_op jit(solution)/shard_map/all_gather | solution.py:90
  865.9 35.8 %all-to-all-start.5 = ((bf16[8,128,768]{1,2,0:T(8,128)(2,1)}), bf16[8,128,768]{1,2,0:T(8,128)(2,1)S(1)}, u32[]{:S(2)}, u32[]{:S(2)}) async-start(bf16[8,128,768]{1,2,0:T(8,128)(2,1)} %pad_maximum_fusion.2), calls=%async_computation.8 | async-start | bytes 3145728 | tf_op jit(solution)/shard_map/all_to_all | solution.py:230
  869.6 335.3 %reduce-scatter.33.cloned.1.call-start = ((), (), s32[]{:S(2)}) async-start(), calls=%async_computation.36 | async-start | bytes 163840
  901.8 29.3 %all-to-all-start.6 = ((bf16[8,64,768]{2,1,0:T(8,128)(2,1)}), bf16[8,64,768]{2,1,0:T(8,128)(2,1)S(1)}, u32[]{:S(2)}, u32[]{:S(2)}) async-start(bf16[8,64,768]{2,1,0:T(8,128)(2,1)} %bitcast.266), calls=%async_computation.10 | async-start | bytes 1572864 | tf_op jit(solution)/shard_map/all_to_all | solution.py:226
  905.3 392.0 %reduce-scatter.15.cloned.1.call-start = ((), (), s32[]{:S(2)}) async-start(), calls=%async_computation.25 | async-start | bytes 4718592 | tf_op jit(solution)/shard_map/reduce_scatter | solution.py:153
  931.9 73.1 %all-to-all-start.9 = ((bf16[8,512,256]{2,1,0:T(8,128)(2,1)}), bf16[8,512,256]{2,1,0:T(8,128)(2,1)S(1)}, u32[]{:S(2)}, u32[]{:S(2)}) async-start(bf16[8,512,256]{2,1,0:T(8,128)(2,1)} %bitcast.240), calls=%async_computation.17 | async-start | bytes 4194304 | tf_op jit(solution)/shard_map/all_to_all | solution.py:179
  1005.1 73.9 %all-to-all-start.7 = ((bf16[8,256,512]{1,2,0:T(8,128)(2,1)}), bf16[8,256,512]{1,2,0:T(8,128)(2,1)}, u32[]{:S(2)}, u32[]{:S(2)}) async-start(bf16[8,256,512]{1,2,0:T(8,128)(2,1)} %copy.237), calls=%async_computation.13 | async-start | bytes 4194304 | tf_op jit(solution)/shard_map/all_to_all | solution.py:171
  1079.0 394.3 %all-to-all-start.8 = ((bf16[8,256,512]{1,2,0:T(8,128)(2,1)}), bf16[8,256,512]{1,2,0:T(8,128)(2,1)}, u32[]{:S(2)}, u32[]{:S(2)}) async-start(bf16[8,256,512]{1,2,0:T(8,128)(2,1)} %copy.239), calls=%async_computation.15 | async-start | bytes 4194304 | tf_op jit(solution)/shard_map/all_to_all | solution.py:171
  1084.6 351.5 %reduce-scatter.31.cloned.1.call-start = ((), (), s32[]{:S(2)}) async-start(), calls=%async_computation.35 | async-start | bytes 1081344
  1084.7 212.6 %copy-start.3 = (f32[128,2048]{1,0:T(8,128)S(1)}, f32[128,2048]{1,0:T(8,128)}, u32[]{:S(2)}) copy-start(f32[128,2048]{1,0:T(8,128)} %copy-done.2) | copy-start | bytes 3145732
  1084.7 212.6 %copy-start.11 = (f32[128,2048]{1,0:T(8,128)S(1)}, f32[128,2048]{1,0:T(8,128)}, u32[]{:S(2)}) copy-start(f32[128,2048]{1,0:T(8,128)} %copy-done.10) | copy-start | bytes 3145732
  1084.8 212.6 %copy-start.21 = (bf16[1,128,2048]{2,1,0:T(8,128)(2,1)S(1)}, bf16[1,128,2048]{2,1,0:T(8,128)(2,1)}, u32[]{:S(2)}) copy-start(bf16[1,128,2048]{2,1,0:T(8,128)(2,1)} %param.19) | copy-start | bytes 1572868
  1084.8 212.5 %copy-start.42 = (f32[2048]{0:T(1024)S(1)}, f32[2048]{0:T(1024)}, u32[]{:S(2)}) copy-start(f32[2048]{0:T(1024)} %param.27) | copy-start | bytes 24580
  1084.8 212.5 %copy-start.56 = (f32[128]{0:T(128)S(1)}, f32[128]{0:T(128)}, u32[]{:S(2)}) copy-start(f32[128]{0:T(128)} %copy-done.55) | copy-start | bytes 1540
  1084.8 212.5 %copy-start.61 = (f32[128]{0:T(128)S(1)}, f32[128]{0:T(128)}, u32[]{:S(2)}) copy-start(f32[128]{0:T(128)} %copy-done.60) | copy-start | bytes 1540
  1094.8 365.0 %reduce-scatter.23.cloned.1.call-start = ((), (), s32[]{:S(2)}) async-start(), calls=%async_computation.30 | async-start | bytes 1310720 | tf_op jit(solution)/shard_map/reduce_scatter | solution.py:196
  (60 other events, 1438.0 us)
Sparse Core Ops, SparseCore 0:
  11.7 75.5 all-gather.10
  155.8 114.5 all-gather.12
  272.5 61.2 all-gather.16
  335.9 84.5 all-gather.22
  422.5 56.8 all-gather.18
  481.3 58.2 all-gather.14
  561.8 54.7 reduce-scatter.18
  620.8 87.3 reduce-scatter.16
  818.0 35.1 reduce-scatter.20
  855.6 71.4 reduce-scatter.28
  929.6 71.3 reduce-scatter.24
  1003.5 71.3 reduce-scatter.26
  1077.0 108.1 all-gather.20
  1188.1 16.7 reduce-scatter.32
  1209.0 88.2 reduce-scatter.14
  1300.0 136.1 reduce-scatter.30
  1439.1 20.6 reduce-scatter.22

commit v2 on v1

--- a/solution.py
+++ b/solution.py
@@ -1,8 +1,11 @@
+import functools
 import math
 
 import jax
 import jax.numpy as jnp
 from jax import lax
+from jax.experimental import pallas as pl
+from jax.experimental.pallas import tpu as pltpu
 from jax.sharding import PartitionSpec as P
 
 HEADS = 16
@@ -10,6 +13,346 @@
 MASKED = -1000000000.0
 BF16 = jnp.bfloat16
 F32 = jnp.float32
+MESH = pl.DeviceIdType.MESH
+DMA = pltpu.SemaphoreType.DMA
+VMEM_SPEC = pl.BlockSpec(memory_space=pltpu.VMEM)
+
+
+def remote(src, dst, send_sem, recv_sem, where):
+    return pltpu.make_async_remote_copy(
+        src, dst, send_sem, recv_sem, device_id=where, device_id_type=MESH
+    )
+
+
+def comm_params(collective_id):
+    return pltpu.CompilerParams(collective_id=collective_id, has_side_effects=True)
+
+
+def greet(peers):
+    barrier = pltpu.get_barrier_semaphore()
+    total = 0
+    for here, where in peers:
+
+        @pl.when(here)
+        def _(where=where):
+            pl.semaphore_signal(barrier, inc=1, device_id=where, device_id_type=MESH)
+
+        total = total + jnp.where(here, 1, 0)
+    pl.semaphore_wait(barrier, total)
+
+
+def greet_all(count, device):
+    barrier = pltpu.get_barrier_semaphore()
+
+    def body(k, carry):
+        pl.semaphore_signal(barrier, inc=1, device_id=device(k), device_id_type=MESH)
+        return carry
+
+    lax.fori_loop(1, count, body, 0)
+    pl.semaphore_wait(barrier, count - 1)
+
+
+def gather_kernel(nz, ny, pieces, block, out, own_sem, send_sem, recv_sem):
+    me = lax.axis_index("group")
+    z, y = me // ny, me % ny
+    rows = block.shape[0] // pieces
+
+    def at(z_to, y_to):
+        return {"group": z_to * ny + y_to}
+
+    greet(
+        [
+            (z > 0, at(z - 1, y)),
+            (z < nz - 1, at(z + 1, y)),
+            (y > 0, at(z, y - 1)),
+            (y < ny - 1, at(z, y + 1)),
+        ]
+    )
+    own = pltpu.make_async_copy(block, out.at[me], own_sem)
+    own.start()
+
+    def part(ref, c):
+        return ref.at[pl.ds(c * rows, rows)]
+
+    def copy(slot, source, c, where, first):
+        return remote(
+            part(block, c) if first else part(out.at[source], c),
+            part(out.at[source], c),
+            send_sem.at[slot, source, c],
+            recv_sem.at[source, c],
+            where,
+        )
+
+    def outgoing(source, go):
+        sz, sy = source // ny, source % ny
+        column = go & (sy == y)
+        return [
+            (column & (sz <= z) & (z < nz - 1), 0, at(z + 1, y)),
+            (column & (sz >= z) & (z > 0), 1, at(z - 1, y)),
+            (go & (sy <= y) & (y < ny - 1), 2, at(z, y + 1)),
+            (go & (sy >= y) & (y > 0), 3, at(z, y - 1)),
+        ]
+
+    def act(source, first, go, start):
+        for c in range(pieces):
+            if start and not first:
+
+                @pl.when(go)
+                def _():
+                    copy(0, source, c, at(z, y), False).wait_recv()
+
+            for cond, slot, where in outgoing(source, go):
+
+                @pl.when(cond)
+                def _(slot=slot, where=where):
+                    one = copy(slot, source, c, where, first)
+                    if start:
+                        one.start()
+                    else:
+                        one.wait_send()
+
+    order = []
+    for dz in range(nz):
+        for sz in [z] if dz == 0 else [z - dz, z + dz]:
+            for dy in range(ny):
+                for sy in [y] if dy == 0 else [y - dy, y + dy]:
+                    inside = (sz >= 0) & (sz < nz) & (sy >= 0) & (sy < ny)
+                    source = jnp.clip(sz, 0, nz - 1) * ny + jnp.clip(sy, 0, ny - 1)
+                    order.append((dz + dy, dz, source, inside))
+    order = sorted(order, key=lambda t: (t[0], -t[1]))
+    for start in (True, False):
+        for distance, _, source, inside in order:
+            act(source, distance == 0, inside, start)
+        if start:
+            own.wait()
+
+
+def gather_rows(block, groups, collective_id, pieces=2):
+    nz = min(4, groups)
+    return pl.pallas_call(
+        functools.partial(gather_kernel, nz, groups // nz, pieces),
+        name="gather_rows",
+        out_shape=jax.ShapeDtypeStruct((groups,) + block.shape, block.dtype),
+        in_specs=[VMEM_SPEC],
+        out_specs=pl.BlockSpec(memory_space=pl.ANY),
+        scratch_shapes=[DMA, DMA((4, groups, pieces)), DMA((groups, pieces))],
+        compiler_params=comm_params(collective_id),
+        cost_estimate=pl.CostEstimate(flops=0, bytes_accessed=100_000_000, transcendentals=0),
+    )(block).reshape(groups * block.shape[0], block.shape[1])
+
+
+def reduce_kernel(nz, ny, pieces, parts, out, ybuf, zbuf, ysend, yrecv, zsend, zrecv):
+    me = lax.axis_index("group")
+    z, y = me // ny, me % ny
+    rows = parts.shape[1] // pieces
+
+    def at(z_to, y_to):
+        return {"group": z_to * ny + y_to}
+
+    greet([(z > 0, at(z - 1, y)), (z < nz - 1, at(z + 1, y)), (z >= 0, at(z, 1 - y))])
+
+    def part(ref, c):
+        return ref.at[pl.ds(c * rows, rows)]
+
+    def y_copy(dest, c):
+        src, dst = part(parts.at[dest * ny + 1 - y], c), part(ybuf.at[dest], c)
+        return remote(src, dst, ysend.at[dest, c], yrecv.at[dest, c], at(z, 1 - y))
+
+    def z_copy(side, dest, c):
+        src, dst = part(ybuf.at[dest], c), part(zbuf.at[side, dest], c)
+        where = at(z - 1, y) if side else at(z + 1, y)
+        return remote(src, dst, zsend.at[dest, c], zrecv.at[side, dest, c], where)
+
+    order = []
+    for d in range(nz - 1, 0, -1):
+        order += [(z + d, z + d < nz, 0), (z - d, z - d >= 0, 1)]
+    order = [(jnp.clip(dest, 0, nz - 1), inside, side) for dest, inside, side in order]
+    for dest, inside, side in order:
+
+        @pl.when(inside)
+        def _():
+            for c in range(pieces):
+                y_copy(dest, c).start()
+
+    for c in range(pieces):
+        y_copy(z, c).start()
+    for dest, inside, side in order:
+        further = (z < nz - 1) if side else (z > 0)
+        for c in range(pieces):
+            span = pl.ds(c * rows, rows)
+
+            @pl.when(inside)
+            def _():
+                y_copy(dest, c).wait_recv()
+                pair = parts[dest * ny + y, span, :].astype(F32) + ybuf[dest, span, :].astype(F32)
+
+                @pl.when(further)
+                def _():
+                    z_copy(side, dest, c).wait_recv()
+                    ybuf[dest, span, :] = (pair + zbuf[side, dest, span, :].astype(F32)).astype(BF16)
+
+                @pl.when(jnp.logical_not(further))
+                def _():
+                    ybuf[dest, span, :] = pair.astype(BF16)
+
+                z_copy(side, dest, c).start()
+
+    for c in range(pieces):
+        span = pl.ds(c * rows, rows)
+        y_copy(z, c).wait_recv()
+        out[span, :] = parts[me, span, :].astype(F32) + ybuf[z, span, :].astype(F32)
+
+        @pl.when(z > 0)
+        def _():
+            z_copy(0, z, c).wait_recv()
+            out[span, :] += zbuf[0, z, span, :].astype(F32)
+
+        @pl.when(z < nz - 1)
+        def _():
+            z_copy(1, z, c).wait_recv()
+            out[span, :] += zbuf[1, z, span, :].astype(F32)
+
+    for dest, inside, side in order:
+
+        @pl.when(inside)
+        def _():
+            for c in range(pieces):
+                y_copy(dest, c).wait_send()
+                z_copy(side, dest, c).wait_send()
+
+    for c in range(pieces):
+        y_copy(z, c).wait_send()
+
+
+def reduce_rows(parts, groups, collective_id, pieces=2):
+    nz = min(4, groups)
+    ny = groups // nz
+    if ny != 2:
+        return lax.psum_scatter(parts, "group", scatter_dimension=0, tiled=True).astype(F32)
+    rows, width = parts.shape[0] // groups, parts.shape[1]
+    return pl.pallas_call(
+        functools.partial(reduce_kernel, nz, ny, pieces),
+        name="reduce_rows",
+        out_shape=jax.ShapeDtypeStruct((rows, width), F32),
+        in_specs=[VMEM_SPEC],
+        out_specs=VMEM_SPEC,
+        scratch_shapes=[
+            pltpu.VMEM((nz, rows, width), BF16),
+            pltpu.VMEM((2, nz, rows, width), BF16),
+            DMA((nz, pieces)),
+            DMA((nz, pieces)),
+            DMA((nz, pieces)),
+            DMA((2, nz, pieces)),
+        ],
+        compiler_params=comm_params(collective_id),
+        cost_estimate=pl.CostEstimate(flops=0, bytes_accessed=100_000_000, transcendentals=0),
+    )(parts.reshape(groups, rows, width))
+
+
+def swap_kernel(groups, to_rows, *refs):
+    count = (len(refs) - 2) // 2
+    ins, outs, (send_sem, recv_sem) = refs[:count], refs[count : 2 * count], refs[2 * count :]
+    me = lax.axis_index("group")
+    columns = ins[0].shape[-1] // (groups if to_rows else 1)
+    wide = lambda ref, i: ref.at[:, pl.ds(pl.multiple_of(i * columns, columns), columns)]
+    thin = lambda ref, i: ref.at[i]
+    source, target = (wide, thin) if to_rows else (thin, wide)
+
+    def peer(k):
+        return lax.rem(me + k, groups)
+
+    greet_all(groups, lambda k: {"group": peer(k)})
+
+    def copy(n, k):
+        to = peer(k)
+        return remote(
+            source(ins[n], to), target(outs[n], me), send_sem.at[n, k], recv_sem.at[n, k], {"group": to}
+        )
+
+    for k in range(1, groups):
+        for n in range(count):
+            copy(n, k).start()
+    for n in range(count):
+        if to_rows:
+            outs[n][me] = ins[n][:, pl.ds(pl.multiple_of(me * columns, columns), columns)]
+        else:
+            outs[n][:, pl.ds(pl.multiple_of(me * columns, columns), columns)] = ins[n][me]
+    for k in range(1, groups):
+        for n in range(count):
+            copy(n, k).wait()
+
+
+def swap(arrays, groups, to_rows, collective_id):
+    shape, count = arrays[0].shape, len(arrays)
+    if to_rows:
+        rows, columns = shape[0], shape[1] // groups
+        out = (groups, rows, columns)
+    else:
+        rows, columns = shape[0] // groups, shape[1]
+        arrays = [a.reshape(groups, rows, columns) for a in arrays]
+        out = (rows, groups * columns)
+    outs = pl.pallas_call(
+        functools.partial(swap_kernel, groups, to_rows),
+        name="swap",
+        out_shape=[jax.ShapeDtypeStruct(out, a.dtype) for a in arrays],
+        in_specs=[VMEM_SPEC] * count,
+        out_specs=[VMEM_SPEC] * count,
+        scratch_shapes=[DMA((count, groups)), DMA((count, groups))],
+        compiler_params=comm_params(collective_id),
+        cost_estimate=pl.CostEstimate(flops=0, bytes_accessed=30_000_000, transcendentals=0),
+    )(*arrays)
+    return [o.reshape(groups * rows, columns) if to_rows else o for o in outs]
+
+
+def small_sum_kernel(axes, scatter, values, out, landed, send_sem, recv_sem):
+    sizes = [lax.axis_size(a) for a in axes]
+    count = math.prod(sizes)
+    me = 0
+    for a, n in zip(axes, sizes):
+        me = me * n + lax.axis_index(a)
+
+    def peer(k):
+        return lax.rem(me + k, count)
+
+    def device(k):
+        to = peer(k)
+        if len(axes) == 1:
+            return {axes[0]: to}
+        return {axes[0]: to // sizes[1], axes[1]: lax.rem(to, sizes[1])}
+
+    greet_all(count, device)
+
+    def copy(k):
+        src = values.at[peer(k)] if scatter else values
+        return remote(src, landed.at[k], send_sem.at[k], recv_sem.at[k], device(k))
+
+    def start(k, carry):
+        copy(k).start()
+        return carry
+
+    def wait(k, carry):
+        copy(k).wait()
+        return carry
+
+    lax.fori_loop(1, count, start, 0)
+    landed[0] = values[me] if scatter else values[...]
+    lax.fori_loop(1, count, wait, 0)
+    out[...] = jnp.sum(landed[...], axis=0)
+
+
+def small_sum(values, axes, scatter, collective_id):
+    count = math.prod(lax.axis_size(a) for a in axes)
+    shape = values.shape[-2:]
+    return pl.pallas_call(
+        functools.partial(small_sum_kernel, axes, scatter),
+        name="small_sum",
+        out_shape=jax.ShapeDtypeStruct(shape, F32),
+        in_specs=[VMEM_SPEC],
+        out_specs=VMEM_SPEC,
+        scratch_shapes=[pltpu.VMEM((count,) + shape, F32), DMA((count,)), DMA((count,))],
+        compiler_params=comm_params(collective_id),
+        cost_estimate=pl.CostEstimate(flops=0, bytes_accessed=10_000_000, transcendentals=0),
+    )(values)
 
 
 def rms_norm(values_in, gain_vec):
@@ -106,18 +449,24 @@
 
     inputs = layer_in[0].astype(F32)
     normed_b = rms_norm(inputs, attn_gain).astype(BF16)
-    normed_all = gather(normed_b)
-    seg_all = gather(segment_ids[0])
-    route_all = gather(routing[0])
+    expert_ids = jnp.arange(experts, dtype=jnp.int32)
+    marks = jnp.any(routing[0][:, :, None] == expert_ids[None, None, :], axis=1).astype(F32)
+    marks = jnp.concatenate([marks.T, segment_ids[0].astype(F32)[None]], axis=0)
+    marks = lax.all_gather(marks, "group", axis=1, tiled=True)
+    chosen, seg_all = marks[:experts].T > 0.5, marks[experts]
+    normed_all = gather_rows(normed_b, groups, 1)
     grad_all = gather(out_grad[0])
     wq, wk, wv = own_cols(w_query, 1), own_cols(w_key, 1), own_cols(w_value, 1)
     query_raw, key_raw = mm(normed_all, wq), mm(normed_all, wk)
     values_b = mm(normed_all, wv).astype(BF16).reshape(length, heads, head_dim)
-    squares = jnp.stack(
-        [jnp.sum(query_raw * query_raw, axis=1), jnp.sum(key_raw * key_raw, axis=1)], axis=1
-    )
-    scales = lax.rsqrt(lax.psum(squares, "group") / width + EPSILON)
-    query_scale, key_scale = scales[:, :1], scales[:, 1:]
+
+    def row_sums(first, second, collective_id):
+        sums = jnp.stack([jnp.sum(first, axis=1), jnp.sum(second, axis=1)])
+        sums = small_sum(sums.reshape(-1, 128), ("group",), False, collective_id)
+        return sums.reshape(2, length, 1) / width
+
+    scales = lax.rsqrt(row_sums(query_raw * query_raw, key_raw * key_raw, 2) + EPSILON)
+    query_scale, key_scale = scales[0], scales[1]
     query_gain_c, key_gain_c = own_cols(query_gain, 0), own_cols(key_gain, 0)
     cosine, sine = angles(length, head_dim)
 
@@ -134,13 +483,11 @@
     probs = jnp.exp(scores - log_total)
     probs_b = probs.astype(BF16)
     mixed_c = ein("hqk,khd->qhd", probs_b, values_b).reshape(length, cols).astype(BF16)
-    mixed_b = lax.all_to_all(mixed_c, "group", 0, 1, tiled=True)
+    (mixed_b,) = swap([mixed_c], groups, False, 3)
     resid = inputs + mm(mixed_b, w_out)
     normed_mlp_b = rms_norm(resid, mlp_gain).astype(BF16)
-    mlp_all = gather(normed_mlp_b)
-
-    expert_ids = jnp.arange(experts, dtype=jnp.int32)
-    chosen = jnp.any(route_all[:, :, None] == expert_ids[None, None, :], axis=1)
+    mlp_all = gather_rows(normed_mlp_b, groups, 4)
+
     router_all = jax.nn.softmax(mm(mlp_all, w_router), axis=-1)
     picked = jnp.where(chosen, router_all, 0.0).reshape(length, sources, local_experts)
     picked = lax.dynamic_index_in_dim(picked, me // parts, 2, keepdims=True)
@@ -157,7 +504,7 @@
     gate_grad_b = (hidden_grad * up_pre * sigma * (1.0 + gate_pre * (1.0 - sigma))).astype(BF16)
     up_grad_b = (hidden_grad * gate_pre * sigma).astype(BF16)
     slot_part = ein("tef,edf->td", gate_grad_b, gate_w) + ein("tef,edf->td", up_grad_b, up_w)
-    slot_sum = lax.psum_scatter(slot_part.astype(BF16), "group", scatter_dimension=0, tiled=True)
+    slot_sum = reduce_rows(slot_part.astype(BF16), groups, 5)
     own_expert = jnp.arange(local_experts, dtype=jnp.int32) == me // parts
     full_part = jnp.where(own_expert[None, None, :], picked_grad[:, :, None], 0.0)
     full_part = jnp.where(chosen, full_part.reshape(length, experts), 0.0)
@@ -186,7 +533,7 @@
         router * (router_full_grad - jnp.sum(router * router_full_grad, axis=-1, keepdims=True))
     ).astype(BF16)
     router_w_grad = mm_tn(normed_mlp_b, logits_grad_b)
-    mlp_in_grad = slot_sum.astype(F32) + mm_nt(logits_grad_b, w_router)
+    mlp_in_grad = slot_sum + mm_nt(logits_grad_b, w_router)
     _, mlp_back = jax.vjp(rms_norm, resid, mlp_gain)
     resid_part, mlp_gain_grad = mlp_back(mlp_in_grad)
     resid_grad = grad_out + resid_part
@@ -195,7 +542,7 @@
     out_w_part = mm_tn(mixed_c, attn_grad_all).astype(BF16)
     out_w_grad = lax.psum_scatter(out_w_part, "expert", scatter_dimension=0, tiled=True)
     mixed_grad_b = mm_nt(attn_grad_b, w_out).astype(BF16)
-    mixed_grad_c = lax.all_to_all(mixed_grad_b, "group", 1, 0, tiled=True)
+    (mixed_grad_c,) = swap([mixed_grad_b], groups, True, 6)
     mixed_grad_c = mixed_grad_c.reshape(length, heads, head_dim)
 
     prob_grad = ein("qhd,khd->hqk", mixed_grad_c, values_b)
@@ -210,14 +557,11 @@
 
     query_turn, key_turn = unturned(query_grad), unturned(key_grad)
     query_mix, key_mix = query_turn * query_gain_c, key_turn * key_gain_c
-    dots = jnp.stack(
-        [jnp.sum(query_mix * query_raw, axis=1), jnp.sum(key_mix * key_raw, axis=1)], axis=1
-    )
-    dots = lax.psum(dots, "group") / width
+    dots = row_sums(query_mix * query_raw, key_mix * key_raw, 7)
     query_raw_b = (
-        query_scale * query_mix - query_raw * query_scale**3 * dots[:, :1]
+        query_scale * query_mix - query_raw * query_scale**3 * dots[0]
     ).astype(BF16)
-    key_raw_b = (key_scale * key_mix - key_raw * key_scale**3 * dots[:, 1:]).astype(BF16)
+    key_raw_b = (key_scale * key_mix - key_raw * key_scale**3 * dots[1]).astype(BF16)
     query_gain_part = jnp.sum(query_turn * query_raw * query_scale, axis=0)
     key_gain_part = jnp.sum(key_turn * key_raw * key_scale, axis=0)
     raw_grads = jnp.concatenate([query_raw_b, key_raw_b, value_grad_b], axis=1)
@@ -225,33 +569,34 @@
     qkv_part = lax.psum_scatter(qkv_part, "expert", scatter_dimension=1, tiled=False)
     qkv_part = lax.all_to_all(qkv_part, "group", 0, 0, tiled=True)
     qkv_part = qkv_part.transpose(1, 0, 2).reshape(-1, groups, 3, cols).astype(F32)
-    gain_part = jnp.stack([query_gain_part, key_gain_part])
-    gain_grads = lax.psum_scatter(gain_part, "expert", scatter_dimension=1, tiled=True)
-    raw_own = lax.all_to_all(raw_grads, "group", 0, 1, tiled=True).reshape(rows, groups, 3, cols)
-    normed_grad = (
-        mm_nt(raw_own[:, :, 0].reshape(rows, width), w_query)
-        + mm_nt(raw_own[:, :, 1].reshape(rows, width), w_key)
-        + mm_nt(raw_own[:, :, 2].reshape(rows, width), w_value)
-    )
+    query_own, key_own, value_own = swap([query_raw_b, key_raw_b, value_grad_b], groups, False, 8)
+    normed_grad = mm_nt(query_own, w_query) + mm_nt(key_own, w_key) + mm_nt(value_own, w_value)
     _, attn_back = jax.vjp(rms_norm, inputs, attn_gain)
     input_part, attn_gain_grad = attn_back(normed_grad)
     input_grad = resid_grad + input_part
-    small = jnp.concatenate(
-        [router_w_grad, mlp_gain_grad[:, None], attn_gain_grad[:, None]], axis=1
-    )
-    small = lax.psum_scatter(small, ("group", "expert"), scatter_dimension=0, tiled=True)
+    wide = [
+        lax.dynamic_update_slice_in_dim(jnp.zeros((width,), F32), part, me * cols, 0)
+        for part in (query_gain_part, key_gain_part)
+    ]
+    small = jnp.concatenate([router_w_grad.T, jnp.stack([mlp_gain_grad, attn_gain_grad] + wide)])
+    devices = groups * sources
+    small = small.reshape(-1, devices, width // devices).transpose(1, 0, 2).reshape(devices, -1)
+    used = small.shape[1]
+    small = jnp.pad(small, ((0, 0), (0, -used % 1024))).reshape(devices, -1, 128)
+    small = small_sum(small, ("group", "expert"), True, 9).reshape(-1)[:used]
+    small = small.reshape(-1, width // devices)
     return (
         result[None],
         input_grad[None],
-        small[:, experts + 1],
+        small[experts + 1],
         qkv_part[:, :, 0].reshape(-1, width),
         qkv_part[:, :, 1].reshape(-1, width),
         qkv_part[:, :, 2].reshape(-1, width),
-        gain_grads[0],
-        gain_grads[1],
+        small[experts + 2],
+        small[experts + 3],
         out_w_grad.astype(F32),
-        small[:, experts],
-        small[:, :experts],
+        small[experts],
+        small[:experts].T,
         gate_sum,
         up_sum,
         down_sum,

time: 1500 us -> 1180 us (0.79)
  waiting for transfers between devices: 741 us -> 236 us
  Pallas kernels: 0 us -> 299 us
  blocking collectives: 337 us -> 173 us
  starting transfers between devices: 25.4 us -> 46.4 us
    pallas_call x0 -> x9, Pallas kernels: none -> 299 us  [the longest x2 123 us: gather_rows(): pl.pallas_call(functools.partial(gather_kernel, nz, groups // nz, pieces)...]
    unnamed x19 -> x12, waiting for transfers between devices: 152 us -> 1.38 us
    reduce_scatter x1 -> x0, waiting for transfers between devices: 90.2 us -> none  [shards(): lax.psum_scatter(slot_part.astype(BF16), 'group', scatter_dimension=0, ti...]
    all_gather x4 -> x2, waiting for transfers between devices: 137 us -> 52.3 us  [gather(): return lax.all_gather(block, 'group', axis=0, tiled=True)]
    all_to_all x3 -> x0, blocking collectives: 81.9 us -> none  [the longest x1 49.5 us: shards(): lax.all_to_all(down_w, 'group', 0, 0, tiled=True).transpose(1, 0, 2)]
    all_to_all x2, blocking collectives: 161 us -> 107 us  [slices_in(): w = lax.all_to_all(w, 'group', 0, 0, tiled=True).reshape(width, part)]
    all_gather x2, waiting for transfers between devices: 45.7 us -> 0.02 us  [slices_in(): return lax.all_gather(w, 'expert', axis=0, tiled=False)]
    reduce_scatter x2, waiting for transfers between devices: 109 us -> 63.6 us  [slices_out(): w = lax.psum_scatter(w, 'expert', scatter_dimension=0, tiled=False)]
  transfers between devices with their start and end apart: 22 -> 17, of which waited for: 14 -> 5; matrix products, arithmetic and copies ran while one was open for 15% -> 24% of each run, Pallas kernels for 0% -> 24%
where the time goes in v2:
time: 1180 us; the launch traced here: 1170 us
  Pallas kernels  299 us (25%)
  matrix products  251 us (21%)
  waiting for transfers between devices  236 us (20%)
  blocking collectives  173 us (15%)
  local copies, waits for them, and re-layouts  94.3 us (8%)
  other arithmetic  55.6 us (5%)
  starting transfers between devices  46.4 us (4%)
  between operations  15.7 us (1%)
    dot_general x15, matrix products, ein(): return jnp.einsum(spec, *ops, preferred_element_type=F32)  190 us
    pallas_call x2, Pallas kernels, gather_rows(): pl.pallas_call(functools.partial(gather_kernel, nz, groups // nz, pieces)...  123 us
    all_to_all x2, blocking collectives, slices_in(): w = lax.all_to_all(w, 'group', 0, 0, tiled=True).reshape(width, part)  107 us
    pallas_call x3, Pallas kernels, swap(): pl.pallas_call(functools.partial(swap_kernel, groups, to_rows), name='swa...  93.4 us
    all_gather x1, blocking collectives, shards(): marks = lax.all_gather(marks, 'group', axis=1, tiled=True)  65.5 us
    reduce_scatter x2, waiting for transfers between devices, slices_out(): w = lax.psum_scatter(w, 'expert', scatter_dimension=0, tiled=False)  63.6 us
    reduce_scatter x1, waiting for transfers between devices, shards(): lax.psum_scatter(out_part, 'group', scatter_dimension=0, tiled=True)  52.4 us
    all_gather x2, waiting for transfers between devices, gather(): return lax.all_gather(block, 'group', axis=0, tiled=True)  52.3 us
  transfers between devices with their start and end apart: 17, of which 5 were waited for; matrix products, arithmetic and copies ran while one was open for 24% of the time, Pallas kernels for 24%

profile of v2, /device:TPU:0, one launch (start us, length us, event | category | flops | bytes accessed | tf_op | source)
XLA Modules:
  0.0 1171.7 jit_solution(10994812523081244094)
XLA Ops:
  11.4 55.5 %all_to_all.35 = bf16[8,256,512]{1,2,0:T(8,128)(2,1)S(1)} all-to-all(bf16[8,256,512]{1,2,0:T(8,128)(2,1)} %copy.187), channel_id=1, replica_groups=mesh['group'=8,'expert'=4] {'group'}, dimensions={0} | all-to-all | bytes 4194304 | tf_op jit(solution)/shard_map/all_to_all | solution.py:441
  73.6 51.9 %all_to_all.36 = bf16[8,256,512]{1,2,0:T(8,128)(2,1)} all-to-all(bf16[8,256,512]{1,2,0:T(8,128)(2,1)} %copy.184), channel_id=1, replica_groups=mesh['group'=8,'expert'=4] {'group'}, dimensions={0} | all-to-all | bytes 4194304 | tf_op jit(solution)/shard_map/all_to_all | solution.py:441
  136.5 65.5 %all_gather.18 = f32[17,1024]{1,0:T(8,128)S(1)} all-gather(f32[17,128]{1,0:T(8,128)S(1)} %pad_maximum_fusion.10), channel_id=1, replica_groups=mesh['group'=8,'expert'=4] {'group'}, dimensions={1}, use_global_device_ids=true | all-gather | bytes 78336 | tf_op jit(solution)/shard_map/all_gather | solution.py:455
  211.2 70.8 %gather_rows.2 = bf16[8,128,2048]{2,1,0:T(8,128)(2,1)} custom-call(bf16[128,2048]{1,0:T(8,128)(2,1)} %fusion.46.block), custom_call_target="tpu_custom_call" | custom-call | bytes 100000000 | tf_op jit(solution)/shard_map/gather_rows/pallas_call | solution.py:132
  289.7 8.0 small_sum.3
  326.6 12.3 %swap.3 = bf16[128,2048]{1,0:T(8,128)(2,1)} custom-call(bf16[8,128,256]{2,1,0:T(8,128)(2,1)} %copy.232.refs_0_), custom_call_target="tpu_custom_call" | custom-call | bytes 30000000 | tf_op jit(solution)/shard_map/swap/pallas_call | solution.py:294
  345.0 52.5 %gather_rows.3 = bf16[8,128,2048]{2,1,0:T(8,128)(2,1)} custom-call(bf16[128,2048]{1,0:T(8,128)(2,1)} %multiply_convert_fusion.6.block), custom_call_target="tpu_custom_call" | custom-call | bytes 100000000 | tf_op jit(solution)/shard_map/gather_rows/pallas_call | solution.py:132
  402.3 14.6 %fusion.100 = f32[1024,4,512]{0,2,1:T(8,128)} fusion(bf16[1024,2048,1]{1,0,2:T(8,128)(2,1)} %bitcast.228, bf16[4,2048,512]{2,1,0:T(8,128)(2,1)} %all-gather.9.cloned.1.call-done), kind=kOutput, calls=%fused_computation.184 | convolution fusion | flops 8589934592 | bytes 20971520 | tf_op jit(solution)/shard_map/td,edf->tef/dot_general | solution.py:395
  416.9 14.7 %fusion.99 = f32[1024,4,512]{0,2,1:T(8,128)} fusion(bf16[1024,2048,1]{1,0,2:T(8,128)(2,1)} %bitcast.229, bf16[4,2048,512]{2,1,0:T(8,128)(2,1)} %all-gather.7.cloned.1.call-done), kind=kOutput, calls=%fused_computation.183 | convolution fusion | flops 8589934592 | bytes 20971520 | tf_op jit(solution)/shard_map/td,edf->tef/dot_general | solution.py:395
  431.6 19.1 %multiply_reduce_fusion.1 = (f32[1024,4]{0,1:T(4,128)S(1)}, f32[1024,4,512]{0,2,1:T(8,128)}) fusion(f32[1024,4,512]{0,2,1:T(8,128)} %fusion.100, f32[1024,4,512]{0,2,1:T(8,128)} %fusion.99, bf16[4,512,2048]{2,1,0:T(8,128)(2,1)} %all-gather.11.cloned.1.call-done, bf16[1,1024,2048]{2,1,0:T(8,128)(2,1)} %all-gather.15.cloned.1.call-done), kind=kOutput, calls=%fused_computation.9 | convolution fusion | flops 8604610560 | bytes 37765120 | tf_op jit(solution)/shard_map/td,efd->tef/dot_general | solution.py:395
  451.6 10.5 multiply_convert_fusion.1
  462.2 16.3 %fusion.101 = f32[1024,2048,1]{1,0,2:T(8,128)} fusion(bf16[1024,4,512]{0,2,1:T(8,128)(2,1)S(1)} %get-tuple-element.34, bf16[4,2048,512]{2,1,0:T(8,128)(2,1)} %all-gather.7.cloned.1.call-done), kind=kOutput, calls=%fused_computation.185 | convolution fusion | flops 8589934592 | bytes 20971520 | tf_op jit(solution)/shard_map/tef,edf->td/dot_general | solution.py:395
  478.4 14.7 %fusion.1 = bf16[1024,2048]{1,0:T(8,128)(2,1)} fusion(f32[1024,2048,1]{1,0,2:T(8,128)} %fusion.101, bf16[1024,4,512]{0,2,1:T(8,128)(2,1)S(1)} %get-tuple-element.33, bf16[4,2048,512]{2,1,0:T(8,128)(2,1)} %all-gather.9.cloned.1.call-done), kind=kOutput, calls=%fused_computation.2 | convolution fusion | flops 8594128896 | bytes 25165824 | tf_op jit(solution)/shard_map/tef,edf->td/dot_general | solution.py:395
  493.1 50.3 %reduce_rows.1 = f32[128,2048]{1,0:T(8,128)} custom-call(bf16[8,128,2048]{2,1,0:T(8,128)(2,1)} %bitcast.244), custom_call_target="tpu_custom_call" | custom-call | bytes 100000000 | tf_op jit(solution)/shard_map/reduce_rows/pallas_call | solution.py:233
  555.8 13.0 %swap.4 = bf16[8,128,256]{2,1,0:T(8,128)(2,1)} custom-call(bf16[128,2048]{1,0:T(8,128)(2,1)} %convolution_convert_fusion.3.refs_0_), custom_call_target="tpu_custom_call" | custom-call | bytes 30000000 | tf_op jit(solution)/shard_map/swap/pallas_call | solution.py:294
  582.1 15.8 %fusion.38 = f32[1024,2,128]{2,0,1:T(8,128)} fusion(f32[2,1024,1024]{1,2,0:T(8,128)} %fusion.102, f32[2,1024,1024]{1,2,0:T(8,128)} %copy-done.15, f32[2,1024]{1,0:T(2,128)S(1)} %log_add_fusion, pred[1024,1024]{0,1:T(8,128)(4,1)} %copy-done.19, bf16[1024,2,64]{2,0,1:T(8,128)(2,1)S(1)} %copy-done.36, bf16[1024,2,64]{2,0,1:T(8,128)(2,1)} %copy-done.37), kind=kOutput, calls=%fused_computation.59 | convolution fusion | flops 560991232 | bytes 19406848 | tf_op jit(solution)/shard_map/hqk,khd->qhd/dot_general | solution.py:395
  597.9 14.3 %fusion.41 = f32[1024,2,128]{2,0,1:T(8,128)} fusion(f32[2,1024,1024]{1,2,0:T(8,128)} %fusion.102, f32[2,1024,1024]{1,2,0:T(8,128)} %copy-done.15, f32[2,1024]{1,0:T(2,128)S(1)} %log_add_fusion, pred[1024,1024]{0,1:T(8,128)(4,1)} %copy-done.19, bf16[1024,2,64]{2,0,1:T(8,128)(2,1)S(1)} %copy-done.34, bf16[1024,2,64]{2,0,1:T(8,128)(2,1)S(1)} %copy-done.32), kind=kOutput, calls=%fused_computation.60 | convolution fusion | flops 560991232 | bytes 19406848 | tf_op jit(solution)/shard_map/hqk,qhd->khd/dot_general | solution.py:395
  627.5 9.6 small_sum.4
  647.5 15.9 %convolution_convert_fusion = bf16[4,512,2048]{2,1,0:T(8,128)(2,1)} fusion(bf16[1,1024,2048]{2,1,0:T(8,128)(2,1)} %all-gather.15.cloned.1.call-done, f32[1024,4]{0,1:T(4,128)S(1)} %bitcast.277, f32[1024,4,512]{0,2,1:T(8,128)} %fusion.100, f32[1024,4,512]{0,2,1:T(8,128)} %fusion.99), kind=kOutput, calls=%fused_computation.19 | convolution fusion | flops 8608808960 | bytes 29376512 | tf_op jit(solution)/shard_map/tef,td->efd/dot_general | solution.py:395
  663.5 14.5 %convert_bitcast_fusion.1 = bf16[4,2048,512]{1,2,0:T(8,128)(2,1)} fusion(bf16[1024,4,512]{0,2,1:T(8,128)(2,1)} %copy-done.24, bf16[1024,2048,1]{1,0,2:T(8,128)(2,1)} %bitcast.230), kind=kOutput, calls=%fused_computation.5 | convolution fusion | flops 8594128896 | bytes 16777216 | tf_op jit(solution)/shard_map/td,tef->edf/dot_general | solution.py:395
  678.0 14.1 %convert_bitcast_fusion = bf16[4,2048,512]{1,2,0:T(8,128)(2,1)} fusion(bf16[1024,4,512]{0,2,1:T(8,128)(2,1)} %copy-done.23, bf16[1024,2048,1]{1,0,2:T(8,128)(2,1)} %bitcast.231), kind=kOutput, calls=%fused_computation.4 | convolution fusion | flops 8594128896 | bytes 16777216 | tf_op jit(solution)/shard_map/td,tef->edf/dot_general | solution.py:395
  697.1 19.6 %bitcast_convert_fusion = bf16[1024,2048]{1,0:T(8,128)(2,1)} fusion(bf16[4,512,2048]{2,1,0:T(8,128)(2,1)} %all-gather.11.cloned.1.call-done, f32[1024,4]{0,1:T(4,128)S(1)} %bitcast.278, f32[1024,4,512]{0,2,1:T(8,128)} %fusion.100, f32[1024,4,512]{0,2,1:T(8,128)} %fusion.99), kind=kOutput, calls=%fused_computation.3 | convolution fusion | flops 8606711808 | bytes 29376512 | tf_op jit(solution)/shard_map/tef,efd->td/dot_general | solution.py:395
  716.7 42.8 %reduce-scatter.20.cloned.1.call-done = bf16[1,512,2048]{2,1,0:T(8,128)(2,1)} async-done(((bf16[4,512,2048]{2,1,0:T(8,128)(2,1)}), bf16[1,512,2048]{2,1,0:T(8,128)(2,1)}) %reduce-scatter.20.cloned.1.call-update) | async-done | bytes 2097168 | tf_op jit(solution)/shard_map/reduce_scatter | solution.py:524
  769.9 63.6 %reduce-scatter.16.cloned.1.call-done = bf16[1,2048,512]{1,2,0:T(8,128)(2,1)} async-done(((bf16[4,2048,512]{1,2,0:T(8,128)(2,1)}), bf16[1,2048,512]{1,2,0:T(8,128)(2,1)}) %reduce-scatter.16.cloned.1.call-update) | async-done | bytes 2097168 | tf_op jit(solution)/shard_map/reduce_scatter | solution.py:517
  847.9 68.2 %swap.5 = (bf16[128,2048]{1,0:T(8,128)(2,1)}, bf16[128,2048]{1,0:T(8,128)(2,1)}, bf16[128,2048]{1,0:T(8,128)(2,1)}) custom-call(bf16[8,128,256]{2,1,0:T(8,128)(2,1)} %bitcast.252, bf16[8,128,256]{2,1,0:T(8,128)(2,1)} %bitcast.253, bf16[8,128,256]{2,1,0:T(8,128)(2,1)} %copy.233.refs_2_), custom_call_target="tpu_custom_call" | custom-call | bytes 30000000 | tf_op jit(solution)/shard_map/swap/pallas_call | solution.py:294
  933.6 25.8 %all-to-all-start.5 = ((bf16[8,256,512]{1,2,0:T(8,128)(2,1)}), bf16[8,256,512]{1,2,0:T(8,128)(2,1)}, u32[]{:S(2)}, u32[]{:S(2)}) async-start(bf16[8,256,512]{1,2,0:T(8,128)(2,1)} %copy.215), calls=%async_computation.11 | async-start | bytes 4194304 | tf_op jit(solution)/shard_map/all_to_all | solution.py:518
  959.6 7.5 fusion.47
  967.1 52.3 %all-gather.13.cloned.1.call-done = bf16[1024,2048]{1,0:T(8,128)(2,1)} async-done(((bf16[128,2048]{1,0:T(8,128)(2,1)}), bf16[1024,2048]{1,0:T(8,128)(2,1)}) %all-gather.13.cloned.1.call-update) | async-done | bytes 4194320 | tf_op jit(solution)/shard_map/all_gather | solution.py:433
  1027.7 14.6 %small_sum.5 = f32[16,128]{1,0:T(8,128)} custom-call(f32[32,16,128]{2,1,0:T(8,128)} %bitcast.264), custom_call_target="tpu_custom_call" | custom-call | bytes 10000000 | tf_op jit(solution)/shard_map/small_sum/pallas_call | solution.py:346
  1052.0 7.7 slice_reduce_fusion
  1062.5 52.4 %reduce-scatter.8.cloned.1.call-done = bf16[128,2048]{1,0:T(8,128)(2,1)} async-done(((bf16[1024,2048]{1,0:T(8,128)(2,1)}), bf16[128,2048]{1,0:T(8,128)(2,1)}) %reduce-scatter.8.cloned.1.call-update) | async-done | bytes 524304 | tf_op jit(solution)/shard_map/reduce_scatter | solution.py:500
  1118.0 23.8 %reduce-scatter.14.cloned.1.call-done = bf16[64,2048]{1,0:T(8,128)(2,1)} async-done(((bf16[256,2048]{1,0:T(8,128)(2,1)}), bf16[64,2048]{1,0:T(8,128)(2,1)}) %reduce-scatter.14.cloned.1.call-update) | async-done | bytes 262160 | tf_op jit(solution)/shard_map/reduce_scatter | solution.py:543
  (320 shorter events, 223.7 us)
Async XLA Ops:
  7.2 390.3 %copy-start = (bf16[2048,16]{0,1:T(8,128)(2,1)S(1)}, bf16[2048,16]{0,1:T(8,128)(2,1)}, u32[]{:S(2)}) copy-start(bf16[2048,16]{0,1:T(8,128)(2,1)} %param.28) | copy-start | bytes 196612
  7.2 395.1 %all-gather.9.cloned.1.call-start = ((), (), s32[]{:S(2)}) async-start(), calls=%async_computation.15 | async-start | bytes 10485760 | tf_op jit(solution)/shard_map/all_gather | solution.py:442
  69.4 347.5 %all-gather.7.cloned.1.call-start = ((), (), s32[]{:S(2)}) async-start(), calls=%async_computation.14 | async-start | bytes 10485760 | tf_op jit(solution)/shard_map/all_gather | solution.py:442
  73.6 128.4 %copy-start.4 = (bf16[1,128,2048]{2,1,0:T(8,128)(2,1)S(1)}, bf16[1,128,2048]{2,1,0:T(8,128)(2,1)}, u32[]{:S(2)}) copy-start(bf16[1,128,2048]{2,1,0:T(8,128)(2,1)} %param.16) | copy-start | bytes 1572868
  129.6 302.0 %all-gather.15.cloned.1.call-start = ((), (), s32[]{:S(2)}) async-start(), calls=%async_computation.25 | async-start | bytes 4718592 | tf_op jit(solution)/shard_map/all_gather | solution.py:433
  130.3 71.9 %all-to-all-start.2 = ((bf16[8,512,256]{2,1,0:T(8,128)(2,1)}), bf16[8,512,256]{2,1,0:T(8,128)(2,1)}, u32[]{:S(2)}, u32[]{:S(2)}) async-start(bf16[8,512,256]{2,1,0:T(8,128)(2,1)} %bitcast.254), calls=%async_computation.2 | async-start | bytes 4194304 | tf_op jit(solution)/shard_map/all_to_all | solution.py:447
  134.7 296.9 %all-gather.11.cloned.1.call-start = ((), (), s32[]{:S(2)}) async-start(), calls=%async_computation.16 | async-start | bytes 10485760 | tf_op jit(solution)/shard_map/all_gather | solution.py:448
  135.6 162.8 %copy-start.59 = (f32[256]{0:T(256)}, f32[256]{0:T(256)S(1)}, u32[]{:S(2)}) copy-start(f32[256]{0:T(256)S(1)} %dynamic_slice.22) | copy-start | bytes 3076
  136.4 167.3 %copy-start.57 = (f32[256]{0:T(256)}, f32[256]{0:T(256)S(1)}, u32[]{:S(2)}) copy-start(f32[256]{0:T(256)S(1)} %dynamic_slice.23) | copy-start | bytes 3076
  202.2 83.8 %copy-start.68 = (f32[128]{0:T(128)}, f32[128]{0:T(128)S(1)}, u32[]{:S(2)}) copy-start(f32[128]{0:T(128)S(1)} %fusion.51) | copy-start | bytes 1540
  210.1 333.3 %reduce-scatter.10.cloned.1.call-start = ((), (), s32[]{:S(2)}) async-start(), calls=%async_computation.18 | async-start | bytes 73728 | tf_op jit(solution)/shard_map/reduce_scatter | solution.py:511
  343.8 203.4 %copy-start.2 = (f32[128,2048]{1,0:T(8,128)}, f32[128,2048]{1,0:T(8,128)S(1)}, u32[]{:S(2)}) copy-start(f32[128,2048]{1,0:T(8,128)S(1)} %get-tuple-element.77) | copy-start | bytes 3145732
  343.9 203.4 %copy-start.61 = (f32[128]{0:T(128)}, f32[128]{0:T(128)S(1)}, u32[]{:S(2)}) copy-start(f32[128]{0:T(128)S(1)} %fusion.76) | copy-start | bytes 1540
  451.6 241.2 %reduce-scatter.12.cloned.1.call-start = ((), (), s32[]{:S(2)}) async-start(), calls=%async_computation.19 | async-start | bytes 3932160 | tf_op jit(solution)/shard_map/reduce_scatter | solution.py:569
  647.4 112.1 %reduce-scatter.20.cloned.1.call-start = ((), (), s32[]{:S(2)}) async-start(), calls=%async_computation.24 | async-start | bytes 10485760 | tf_op jit(solution)/shard_map/reduce_scatter | solution.py:524
  663.4 170.1 %reduce-scatter.16.cloned.1.call-start = ((), (), s32[]{:S(2)}) async-start(), calls=%async_computation.22 | async-start | bytes 10485760 | tf_op jit(solution)/shard_map/reduce_scatter | solution.py:517
  678.0 251.5 %reduce-scatter.18.cloned.1.call-start = ((), (), s32[]{:S(2)}) async-start(), calls=%async_computation.23 | async-start | bytes 10485760 | tf_op jit(solution)/shard_map/reduce_scatter | solution.py:517
  692.2 327.2 %all-gather.13.cloned.1.call-start = ((), (), s32[]{:S(2)}) async-start(), calls=%async_computation.20 | async-start | bytes 4718592 | tf_op jit(solution)/shard_map/all_gather | solution.py:433
  692.8 70.7 %all-to-all-start.3 = ((bf16[8,64,768]{2,1,0:T(8,128)(2,1)}), bf16[8,64,768]{2,1,0:T(8,128)(2,1)S(1)}, u32[]{:S(2)}, u32[]{:S(2)}) async-start(bf16[8,64,768]{2,1,0:T(8,128)(2,1)} %bitcast.265), calls=%async_computation.6 | async-start | bytes 1572864 | tf_op jit(solution)/shard_map/all_to_all | solution.py:570
  697.0 417.9 %reduce-scatter.8.cloned.1.call-start = ((), (), s32[]{:S(2)}) async-start(), calls=%async_computation.17 | async-start | bytes 4718592 | tf_op jit(solution)/shard_map/reduce_scatter | solution.py:500
  764.4 73.1 %all-to-all-start.6 = ((bf16[8,512,256]{2,1,0:T(8,128)(2,1)}), bf16[8,512,256]{2,1,0:T(8,128)(2,1)S(1)}, u32[]{:S(2)}, u32[]{:S(2)}) async-start(bf16[8,512,256]{2,1,0:T(8,128)(2,1)} %bitcast.237), calls=%async_computation.13 | async-start | bytes 4194304 | tf_op jit(solution)/shard_map/all_to_all | solution.py:526
  837.5 85.5 %copy-start.12 = (bf16[8,512,256]{2,1,0:T(8,128)(2,1)}, bf16[8,512,256]{2,1,0:T(8,128)(2,1)S(1)}, u32[]{:S(2)}) copy-start(bf16[8,512,256]{2,1,0:T(8,128)(2,1)S(1)} %all-to-all-done.6) | copy-start | bytes 6291460
  837.5 96.1 %all-to-all-start.4 = ((bf16[8,256,512]{1,2,0:T(8,128)(2,1)}), bf16[8,256,512]{1,2,0:T(8,128)(2,1)}, u32[]{:S(2)}, u32[]{:S(2)}) async-start(bf16[8,256,512]{1,2,0:T(8,128)(2,1)} %copy.213), calls=%async_computation.9 | async-start | bytes 4194304 | tf_op jit(solution)/shard_map/all_to_all | solution.py:518
  933.6 85.7 %copy-start.42 = (bf16[2,128,1024]{2,1,0:T(8,128)(2,1)S(1)}, bf16[2,128,1024]{2,1,0:T(8,128)(2,1)}, u32[]{:S(2)}) copy-start(bf16[2,128,1024]{2,1,0:T(8,128)(2,1)} %copy-done.41) | copy-start | bytes 1572868
  933.6 221.7 %all-to-all-start.5 = ((bf16[8,256,512]{1,2,0:T(8,128)(2,1)}), bf16[8,256,512]{1,2,0:T(8,128)(2,1)}, u32[]{:S(2)}, u32[]{:S(2)}) async-start(bf16[8,256,512]{1,2,0:T(8,128)(2,1)} %copy.215), calls=%async_computation.11 | async-start | bytes 4194304 | tf_op jit(solution)/shard_map/all_to_all | solution.py:518
  959.5 182.3 %reduce-scatter.14.cloned.1.call-start = ((), (), s32[]{:S(2)}) async-start(), calls=%async_computation.21 | async-start | bytes 1310720 | tf_op jit(solution)/shard_map/reduce_scatter | solution.py:543
  1026.8 88.1 %copy-start.3 = (f32[128,2048]{1,0:T(8,128)S(1)}, f32[128,2048]{1,0:T(8,128)}, u32[]{:S(2)}) copy-start(f32[128,2048]{1,0:T(8,128)} %copy-done.2) | copy-start | bytes 3145732
  1026.8 88.1 %copy-start.11 = (f32[128,2048]{1,0:T(8,128)S(1)}, f32[128,2048]{1,0:T(8,128)}, u32[]{:S(2)}) copy-start(f32[128,2048]{1,0:T(8,128)} %copy-done.10) | copy-start | bytes 3145732
  1026.9 88.1 %copy-start.17 = (bf16[1,128,2048]{2,1,0:T(8,128)(2,1)S(1)}, bf16[1,128,2048]{2,1,0:T(8,128)(2,1)}, u32[]{:S(2)}) copy-start(bf16[1,128,2048]{2,1,0:T(8,128)(2,1)} %param.19) | copy-start | bytes 1572868
  1026.9 88.1 %copy-start.47 = (f32[2048]{0:T(1024)S(1)}, f32[2048]{0:T(1024)}, u32[]{:S(2)}) copy-start(f32[2048]{0:T(1024)} %param.27) | copy-start | bytes 24580
  1026.9 88.1 %copy-start.62 = (f32[128]{0:T(128)S(1)}, f32[128]{0:T(128)}, u32[]{:S(2)}) copy-start(f32[128]{0:T(128)} %copy-done.61) | copy-start | bytes 1540
  1026.9 88.1 %copy-start.67 = (f32[128]{0:T(128)S(1)}, f32[128]{0:T(128)}, u32[]{:S(2)}) copy-start(f32[128]{0:T(128)} %copy-done.66) | copy-start | bytes 1540
  (57 other events, 1473.9 us)
Sparse Core Ops, SparseCore 0:
  69.5 57.2 all-gather.8
  129.7 57.5 all-gather.6
  189.4 103.1 all-gather.14
  294.0 56.7 all-gather.10
  451.7 53.0 reduce-scatter.9
  647.6 37.8 reduce-scatter.11
  688.1 71.4 reduce-scatter.19
  762.1 71.3 reduce-scatter.15
  836.1 71.3 reduce-scatter.17
  909.5 109.7 all-gather.12
  1023.6 91.3 reduce-scatter.7
  1117.3 24.4 reduce-scatter.13

commit v3 on v2

--- a/solution.py
+++ b/solution.py
@@ -52,7 +52,12 @@
     pl.semaphore_wait(barrier, count - 1)
 
 
-def gather_kernel(nz, ny, pieces, block, out, own_sem, send_sem, recv_sem):
+def gather_kernel(nz, ny, pieces, *refs):
+    if len(refs) == 5:
+        block, out, own_sem, send_sem, recv_sem = refs
+        note = None
+    else:
+        block, note, out, note_out, own_sem, send_sem, recv_sem, note_send, note_recv = refs
     me = lax.axis_index("group")
     z, y = me // ny, me % ny
     rows = block.shape[0] // pieces
@@ -60,14 +65,24 @@
     def at(z_to, y_to):
         return {"group": z_to * ny + y_to}
 
-    greet(
-        [
-            (z > 0, at(z - 1, y)),
-            (z < nz - 1, at(z + 1, y)),
-            (y > 0, at(z, y - 1)),
-            (y < ny - 1, at(z, y + 1)),
-        ]
-    )
+    def note_copy(k):
+        to = {"group": lax.rem(me + k, nz * ny)}
+        return remote(note, note_out.at[me], note_send.at[k], note_recv.at[k], to)
+
+    if note is None:
+        greet(
+            [
+                (z > 0, at(z - 1, y)),
+                (z < nz - 1, at(z + 1, y)),
+                (y > 0, at(z, y - 1)),
+                (y < ny - 1, at(z, y + 1)),
+            ]
+        )
+    else:
+        greet_all(nz * ny, lambda k: {"group": lax.rem(me + k, nz * ny)})
+        for k in range(1, nz * ny):
+            note_copy(k).start()
+        note_out[me] = note[...]
     own = pltpu.make_async_copy(block, out.at[me], own_sem)
     own.start()
 
@@ -125,20 +140,27 @@
             act(source, distance == 0, inside, start)
         if start:
             own.wait()
-
-
-def gather_rows(block, groups, collective_id, pieces=2):
+    if note is not None:
+        for k in range(1, nz * ny):
+            note_copy(k).wait()
+
+
+def gather_rows(block, groups, collective_id, pieces=2, note=None):
     nz = min(4, groups)
-    return pl.pallas_call(
+    notes = [] if note is None else [note]
+    outs = pl.pallas_call(
         functools.partial(gather_kernel, nz, groups // nz, pieces),
         name="gather_rows",
-        out_shape=jax.ShapeDtypeStruct((groups,) + block.shape, block.dtype),
-        in_specs=[VMEM_SPEC],
-        out_specs=pl.BlockSpec(memory_space=pl.ANY),
-        scratch_shapes=[DMA, DMA((4, groups, pieces)), DMA((groups, pieces))],
+        out_shape=[jax.ShapeDtypeStruct((groups,) + a.shape, a.dtype) for a in [block] + notes],
+        in_specs=[VMEM_SPEC] * (1 + len(notes)),
+        out_specs=[pl.BlockSpec(memory_space=pl.ANY)] + [VMEM_SPEC] * len(notes),
+        scratch_shapes=[DMA, DMA((4, groups, pieces)), DMA((groups, pieces))]
+        + [DMA((groups,))] * 2 * len(notes),
         compiler_params=comm_params(collective_id),
-        cost_estimate=pl.CostEstimate(flops=0, bytes_accessed=100_000_000, transcendentals=0),
-    )(block).reshape(groups * block.shape[0], block.shape[1])
+        cost_estimate=pl.CostEstimate(flops=0, bytes_accessed=200_000_000, transcendentals=0),
+    )(block, *notes)
+    rows = outs[0].reshape(groups * block.shape[0], block.shape[1])
+    return rows if note is None else (rows, outs[1])
 
 
 def reduce_kernel(nz, ny, pieces, parts, out, ybuf, zbuf, ysend, yrecv, zsend, zrecv):
@@ -429,33 +451,33 @@
     part = hidden_size // parts
     score_scale = 1.0 / math.sqrt(head_dim)
 
-    def gather(block):
-        return lax.all_gather(block, "group", axis=0, tiled=True)
-
     def own_cols(matrix, axis):
         return lax.dynamic_slice_in_dim(matrix, me * cols, cols, axis)
 
-    def slices_in(w):
+    def slices(w):
         w = w.reshape(local_experts, w.shape[1], parts, part).transpose(0, 2, 1, 3)
-        w = w.reshape(groups, w.shape[2], part)
-        w = lax.all_to_all(w, "group", 0, 0, tiled=True).reshape(width, part)
+        return w.reshape(groups, w.shape[2], part)
+
+    def exchange(w):
+        return lax.all_to_all(w, "group", 0, 0, tiled=True)
+
+    def row_of_devices(w):
         return lax.all_gather(w, "expert", axis=0, tiled=False)
 
-    gate_w = slices_in(w_gate)
-    up_w = slices_in(w_up)
-    down_w = w_down.reshape(groups, part, cols)
-    down_w = lax.all_to_all(down_w, "group", 0, 0, tiled=True).transpose(1, 0, 2)
-    down_w = lax.all_gather(down_w.reshape(part, width), "expert", axis=0, tiled=False)
+    together = lax.optimization_barrier
+    gate_own = exchange(slices(w_gate))
 
     inputs = layer_in[0].astype(F32)
     normed_b = rms_norm(inputs, attn_gain).astype(BF16)
     expert_ids = jnp.arange(experts, dtype=jnp.int32)
     marks = jnp.any(routing[0][:, :, None] == expert_ids[None, None, :], axis=1).astype(F32)
     marks = jnp.concatenate([marks.T, segment_ids[0].astype(F32)[None]], axis=0)
-    marks = lax.all_gather(marks, "group", axis=1, tiled=True)
+    normed_all, marks = gather_rows(normed_b, groups, 1, note=marks)
+    marks = marks.transpose(1, 0, 2).reshape(experts + 1, length)
     chosen, seg_all = marks[:experts].T > 0.5, marks[experts]
-    normed_all = gather_rows(normed_b, groups, 1)
-    grad_all = gather(out_grad[0])
+    gate_own, up_in, normed_late = together((gate_own, slices(w_up), normed_all))
+    gate_w = row_of_devices(gate_own.reshape(width, part))
+    up_own = exchange(up_in)
     wq, wk, wv = own_cols(w_query, 1), own_cols(w_key, 1), own_cols(w_value, 1)
     query_raw, key_raw = mm(normed_all, wq), mm(normed_all, wk)
     values_b = mm(normed_all, wv).astype(BF16).reshape(length, heads, head_dim)
@@ -483,10 +505,16 @@
     probs = jnp.exp(scores - log_total)
     probs_b = probs.astype(BF16)
     mixed_c = ein("hqk,khd->qhd", probs_b, values_b).reshape(length, cols).astype(BF16)
+    up_own, down_in, mixed_c = together((up_own, w_down.reshape(groups, part, cols), mixed_c))
+    up_w = row_of_devices(up_own.reshape(width, part))
+    down_own = exchange(down_in)
     (mixed_b,) = swap([mixed_c], groups, False, 3)
     resid = inputs + mm(mixed_b, w_out)
     normed_mlp_b = rms_norm(resid, mlp_gain).astype(BF16)
     mlp_all = gather_rows(normed_mlp_b, groups, 4)
+    down_own, grad_in, mlp_late = together((down_own, out_grad[0], mlp_all))
+    down_w = row_of_devices(down_own.transpose(1, 0, 2).reshape(part, width))
+    grad_all = exchange(jnp.broadcast_to(grad_in, (groups, rows, width))).reshape(length, width)
 
     router_all = jax.nn.softmax(mm(mlp_all, w_router), axis=-1)
     picked = jnp.where(chosen, router_all, 0.0).reshape(length, sources, local_experts)
@@ -497,34 +525,37 @@
     hidden = gate_pre * sigma * up_pre
     hidden_b = (hidden * picked).astype(BF16)
     out_part = ein("tef,efd->td", hidden_b, down_w).astype(BF16)
+    out_part, grad_all, mixed_in = together((out_part, grad_all, mixed_b))
     mixture = lax.psum_scatter(out_part, "group", scatter_dimension=0, tiled=True)
+    mixed_all = exchange(jnp.broadcast_to(mixed_in, (groups, rows, width))).reshape(length, width)
     hidden_grad = ein("td,efd->tef", grad_all, down_w)
     picked_grad = jnp.sum(hidden * hidden_grad, axis=2)
     hidden_grad = hidden_grad * picked
     gate_grad_b = (hidden_grad * up_pre * sigma * (1.0 + gate_pre * (1.0 - sigma))).astype(BF16)
     up_grad_b = (hidden_grad * gate_pre * sigma).astype(BF16)
-    slot_part = ein("tef,edf->td", gate_grad_b, gate_w) + ein("tef,edf->td", up_grad_b, up_w)
-    slot_sum = reduce_rows(slot_part.astype(BF16), groups, 5)
     own_expert = jnp.arange(local_experts, dtype=jnp.int32) == me // parts
     full_part = jnp.where(own_expert[None, None, :], picked_grad[:, :, None], 0.0)
     full_part = jnp.where(chosen, full_part.reshape(length, experts), 0.0)
-    router_full_grad = lax.psum_scatter(full_part, "group", scatter_dimension=0, tiled=True)
-    gate_w_part = ein("td,tef->edf", mlp_all, gate_grad_b).astype(BF16)
-    up_w_part = ein("td,tef->edf", mlp_all, up_grad_b).astype(BF16)
+    full_part = full_part.T.reshape(experts, groups, rows).transpose(1, 0, 2)
+    router_full_grad = small_sum(full_part, ("group",), True, 10).T
+    gate_w_part = ein("td,tef->edf", mlp_late, gate_grad_b).astype(BF16)
+    up_w_part = ein("td,tef->edf", mlp_late, up_grad_b).astype(BF16)
     down_w_part = ein("tef,td->efd", hidden_b, grad_all).astype(BF16)
+    up_w_part, down_w_part, gate_grad_b, up_grad_b = together(
+        (up_w_part, down_w_part, gate_grad_b, up_grad_b)
+    )
+
+    def over_row(w):
+        return lax.psum_scatter(w, "expert", scatter_dimension=0, tiled=False)
+
+    gate_sum, up_sum, down_sum = over_row(gate_w_part), over_row(up_w_part), over_row(down_w_part)
+    slot_part = ein("tef,edf->td", gate_grad_b, gate_w) + ein("tef,edf->td", up_grad_b, up_w)
+    slot_part, mixture, mixed_all = together((slot_part.astype(BF16), mixture, mixed_all))
+    slot_sum = reduce_rows(slot_part, groups, 5)
 
     def slices_out(w):
-        w = lax.psum_scatter(w, "expert", scatter_dimension=0, tiled=False)
-        w = lax.all_to_all(w.reshape(groups, cols, part), "group", 0, 0, tiled=True)
         w = w.reshape(local_experts, parts, cols, part).transpose(0, 2, 1, 3)
         return w.reshape(local_experts, cols, hidden_size).astype(F32)
-
-    gate_sum = slices_out(gate_w_part)
-    up_sum = slices_out(up_w_part)
-    down_sum = lax.psum_scatter(down_w_part, "expert", scatter_dimension=0, tiled=False)
-    down_sum = down_sum.reshape(part, groups, cols).transpose(1, 0, 2)
-    down_sum = lax.all_to_all(down_sum, "group", 0, 0, tiled=True)
-    down_sum = down_sum.reshape(local_experts, hidden_size, cols).astype(F32)
 
     result = (resid + mixture.astype(F32)).astype(BF16)
     grad_out = out_grad[0].astype(F32)
@@ -538,11 +569,12 @@
     resid_part, mlp_gain_grad = mlp_back(mlp_in_grad)
     resid_grad = grad_out + resid_part
     attn_grad_b = resid_grad.astype(BF16)
-    attn_grad_all = gather(attn_grad_b)
-    out_w_part = mm_tn(mixed_c, attn_grad_all).astype(BF16)
-    out_w_grad = lax.psum_scatter(out_w_part, "expert", scatter_dimension=0, tiled=True)
     mixed_grad_b = mm_nt(attn_grad_b, w_out).astype(BF16)
-    (mixed_grad_c,) = swap([mixed_grad_b], groups, True, 6)
+    gate_sum, mixed_grad_b, attn_grad_b = together((gate_sum, mixed_grad_b, attn_grad_b))
+    gate_sum = exchange(gate_sum.reshape(groups, cols, part))
+    mixed_grad_c, attn_grad_c = swap([mixed_grad_b, attn_grad_b], groups, True, 6)
+    up_sum, mixed_grad_c, attn_grad_c = together((up_sum, mixed_grad_c, attn_grad_c))
+    out_w_part = mm_tn(mixed_all, attn_grad_c).astype(BF16)
     mixed_grad_c = mixed_grad_c.reshape(length, heads, head_dim)
 
     prob_grad = ein("qhd,khd->hqk", mixed_grad_c, values_b)
@@ -557,7 +589,11 @@
 
     query_turn, key_turn = unturned(query_grad), unturned(key_grad)
     query_mix, key_mix = query_turn * query_gain_c, key_turn * key_gain_c
-    dots = row_sums(query_mix * query_raw, key_mix * key_raw, 7)
+    query_dots, key_dots, gate_sum, up_sum = together(
+        (query_mix * query_raw, key_mix * key_raw, gate_sum, up_sum)
+    )
+    up_sum = exchange(up_sum.reshape(groups, cols, part))
+    dots = row_sums(query_dots, key_dots, 7)
     query_raw_b = (
         query_scale * query_mix - query_raw * query_scale**3 * dots[0]
     ).astype(BF16)
@@ -565,11 +601,17 @@
     query_gain_part = jnp.sum(query_turn * query_raw * query_scale, axis=0)
     key_gain_part = jnp.sum(key_turn * key_raw * key_scale, axis=0)
     raw_grads = jnp.concatenate([query_raw_b, key_raw_b, value_grad_b], axis=1)
-    qkv_part = mm_tn(normed_all, raw_grads).astype(BF16).reshape(groups, sources, -1, 3 * cols)
-    qkv_part = lax.psum_scatter(qkv_part, "expert", scatter_dimension=1, tiled=False)
-    qkv_part = lax.all_to_all(qkv_part, "group", 0, 0, tiled=True)
-    qkv_part = qkv_part.transpose(1, 0, 2).reshape(-1, groups, 3, cols).astype(F32)
+    qkv_part = jnp.concatenate([mm_tn(normed_late, raw_grads).astype(BF16), out_w_part], axis=1)
+    qkv_part = qkv_part.reshape(groups, sources, -1, 4 * cols).transpose(1, 0, 2, 3)
+    qkv_part = qkv_part.reshape(sources, -1, 4 * cols)
+    qkv_part = lax.psum_scatter(qkv_part, "expert", scatter_dimension=0, tiled=False)
+    qkv_part = lax.all_to_all(qkv_part.reshape(groups, -1, 4 * cols), "group", 0, 0, tiled=True)
+    qkv_part = qkv_part.transpose(1, 0, 2).reshape(-1, groups, 4, cols).astype(F32)
     query_own, key_own, value_own = swap([query_raw_b, key_raw_b, value_grad_b], groups, False, 8)
+    query_own, key_own, value_own, up_sum, down_sum = together(
+        (query_own, key_own, value_own, up_sum, down_sum)
+    )
+    down_sum = exchange(down_sum.reshape(part, groups, cols).transpose(1, 0, 2))
     normed_grad = mm_nt(query_own, w_query) + mm_nt(key_own, w_key) + mm_nt(value_own, w_value)
     _, attn_back = jax.vjp(rms_norm, inputs, attn_gain)
     input_part, attn_gain_grad = attn_back(normed_grad)
@@ -594,12 +636,12 @@
         qkv_part[:, :, 2].reshape(-1, width),
         small[experts + 2],
         small[experts + 3],
-        out_w_grad.astype(F32),
+        qkv_part[:, :, 3].reshape(-1, width),
         small[experts],
         small[:experts].T,
-        gate_sum,
-        up_sum,
-        down_sum,
+        slices_out(gate_sum),
+        slices_out(up_sum),
+        down_sum.reshape(local_experts, hidden_size, cols).astype(F32),
     )
 
 

time: 1180 us -> 1110 us (0.941)
  Pallas kernels: 299 us -> 524 us
  blocking collectives: 173 us -> 0 us
  waiting for transfers between devices: 236 us -> 87.5 us
  local copies, waits for them, and re-layouts: 94.3 us -> 109 us
    reduce_scatter x6 -> x4, waiting for transfers between devices: 130 us -> 0.04 us  [the longest x3 0.04 us: over_row(): return lax.psum_scatter(w, 'expert', scatter_dimension=0, tiled=False)]
    pallas_call x3 -> x4, Pallas kernels: 32.2 us -> 148 us  [small_sum(): pl.pallas_call(functools.partial(small_sum_kernel, axes, scatter), name='...]
    all_to_all x2 -> x0, blocking collectives: 107 us -> none  [slices_in(): w = lax.all_to_all(w, 'group', 0, 0, tiled=True).reshape(width, part)]
    pallas_call x3, Pallas kernels: 93.4 us -> 187 us  [swap(): pl.pallas_call(functools.partial(swap_kernel, groups, to_rows), name='swa...]
    all_to_all x5 -> x9, waiting for transfers between devices: 0.01 us -> 69.3 us  [the longest x8 69.3 us: exchange(): return lax.all_to_all(w, 'group', 0, 0, tiled=True)]
    all_gather x1 -> x0, blocking collectives: 65.5 us -> none  [shards(): marks = lax.all_gather(marks, 'group', axis=1, tiled=True)]
    reduce_scatter x1, waiting for transfers between devices: 52.4 us -> 0.02 us  [shards(): lax.psum_scatter(out_part, 'group', scatter_dimension=0, tiled=True)]
    all_gather x5 -> x3, waiting for transfers between devices: 52.3 us -> 17.3 us  [row_of_devices(): return lax.all_gather(w, 'expert', axis=0, tiled=False)]
  transfers between devices with their start and end apart: 17 -> 17, of which waited for: 5 -> 4; matrix products, arithmetic and copies ran while one was open for 24% -> 35% of each run, Pallas kernels for 24% -> 48%
where the time goes in v3:
time: 1110 us; the launch traced here: 1100 us
  Pallas kernels  524 us (47%)
  matrix products  249 us (22%)
  local copies, waits for them, and re-layouts  109 us (10%)
  waiting for transfers between devices  87.5 us (8%)
  other arithmetic  57.7 us (5%)
  starting transfers between devices  55.3 us (5%)
  between operations  15.5 us (1%)
    dot_general x15, matrix products, ein(): return jnp.einsum(spec, *ops, preferred_element_type=F32)  188 us
    pallas_call x3, Pallas kernels, swap(): pl.pallas_call(functools.partial(swap_kernel, groups, to_rows), name='swa...  187 us
    pallas_call x4, Pallas kernels, small_sum(): pl.pallas_call(functools.partial(small_sum_kernel, axes, scatter), name='...  148 us
    pallas_call x2, Pallas kernels, gather_rows(): pl.pallas_call(functools.partial(gather_kernel, nz, groups // nz, pieces)...  138 us
    all_to_all x8, waiting for transfers between devices, exchange(): return lax.all_to_all(w, 'group', 0, 0, tiled=True)  69.3 us
    pallas_call x1, Pallas kernels, reduce_rows(): pl.pallas_call(functools.partial(reduce_kernel, nz, ny, pieces), name='re...  50.8 us
    all_to_all x8, starting transfers between devices, exchange(): return lax.all_to_all(w, 'group', 0, 0, tiled=True)  50.2 us
    dot_general x5, matrix products, mm_nt(): lax.dot_general(left, right, (((1,), (1,)), ((), ())), preferred_element_...  30.7 us
  transfers between devices with their start and end apart: 17, of which 4 were waited for; matrix products, arithmetic and copies ran while one was open for 35% of the time, Pallas kernels for 48%

profile of v3, /device:TPU:0, one launch (start us, length us, event | category | flops | bytes accessed | tf_op | source)
XLA Modules:
  0.0 1097.4 jit_solution(1916806093324102885)
XLA Ops:
  11.5 7.3 all-to-all-start
  21.7 86.7 %gather_rows.2 = (bf16[8,128,2048]{2,1,0:T(8,128)(2,1)}, f32[8,17,128]{2,1,0:T(8,128)}) custom-call(bf16[128,2048]{1,0:T(8,128)(2,1)} %fusion.48.refs_0_, f32[17,128]{1,0:T(8,128)} %pad_maximum_fusion.11.refs_1_), custom_call_target="tpu_custom_call" | custom-call | bytes 200000000 | tf_op jit(solution)/shard_map/gather_rows/pallas_call | solution.py:151
  123.4 10.3 small_sum.4
  170.4 22.4 %all-to-all-done.1 = bf16[8,256,512]{1,2,0:T(8,128)(2,1)} async-done(((bf16[8,256,512]{1,2,0:T(8,128)(2,1)}), bf16[8,256,512]{1,2,0:T(8,128)(2,1)}, u32[]{:S(2)}, u32[]{:S(2)}) %all-to-all-start.1) | async-done | bytes 2097184 | tf_op jit(solution)/shard_map/all_to_all | solution.py:462
  201.5 57.2 %swap.3 = bf16[128,2048]{1,0:T(8,128)(2,1)} custom-call(bf16[8,128,256]{2,1,0:T(8,128)(2,1)} %bitcast.301), custom_call_target="tpu_custom_call" | custom-call | bytes 30000000 | tf_op jit(solution)/shard_map/swap/pallas_call | solution.py:316
  265.6 50.8 %gather_rows.3 = bf16[8,128,2048]{2,1,0:T(8,128)(2,1)} custom-call(bf16[128,2048]{1,0:T(8,128)(2,1)} %multiply_convert_fusion.6.refs_0_), custom_call_target="tpu_custom_call" | custom-call | bytes 200000000 | tf_op jit(solution)/shard_map/gather_rows/pallas_call | solution.py:151
  335.4 15.0 %fusion.105 = f32[1024,4,512]{0,2,1:T(8,128)} fusion(bf16[1024,2048,1]{1,0,2:T(8,128)(2,1)} %bitcast.273, bf16[4,2048,512]{2,1,0:T(8,128)(2,1)} %all-gather.4.cloned.1.call-done), kind=kOutput, calls=%fused_computation.194 | convolution fusion | flops 8589934592 | bytes 20971520 | tf_op jit(solution)/shard_map/td,edf->tef/dot_general | solution.py:417
  350.3 14.6 %fusion.106 = f32[1024,4,512]{0,2,1:T(8,128)} fusion(bf16[1024,2048,1]{1,0,2:T(8,128)(2,1)} %bitcast.274, bf16[4,2048,512]{2,1,0:T(8,128)(2,1)} %all-gather.6.cloned.1.call-done), kind=kOutput, calls=%fused_computation.195 | convolution fusion | flops 8589934592 | bytes 20971520 | tf_op jit(solution)/shard_map/td,edf->tef/dot_general | solution.py:417
  364.9 17.3 %all-gather.8.cloned.1.call-done = bf16[4,512,2048]{2,1,0:T(8,128)(2,1)} async-done(((bf16[1,512,2048]{2,1,0:T(8,128)(2,1)}), bf16[4,512,2048]{2,1,0:T(8,128)(2,1)}) %all-gather.8.cloned.1.call-update) | async-done | bytes 8388624 | tf_op jit(solution)/shard_map/all_gather | solution.py:465
  382.3 17.3 %bitcast_convert_fusion = bf16[1024,2048]{1,0:T(8,128)(2,1)} fusion(bf16[4,512,2048]{2,1,0:T(8,128)(2,1)} %all-gather.8.cloned.1.call-done, f32[1024,4]{0,1:T(4,128)S(1)} %bitcast.327, f32[1024,4,512]{0,2,1:T(8,128)} %fusion.106, f32[1024,4,512]{0,2,1:T(8,128)} %fusion.105), kind=kOutput, calls=%fused_computation.3 | convolution fusion | flops 8606711808 | bytes 29376512 | tf_op jit(solution)/shard_map/tef,efd->td/dot_general | solution.py:417
  399.6 24.1 %all-to-all-done.3 = bf16[8,128,2048]{2,1,0:T(8,128)(2,1)} async-done(((bf16[8,128,2048]{2,1,0:T(8,128)(2,1)}), bf16[8,128,2048]{2,1,0:T(8,128)(2,1)}, u32[]{:S(2)}, u32[]{:S(2)}) %all-to-all-start.3) | async-done | bytes 4194336 | tf_op jit(solution)/shard_map/all_to_all | solution.py:462
  423.7 22.2 %multiply_reduce_fusion.1 = (f32[1024,4]{0,1:T(4,128)S(1)}, bf16[1024,4,512]{0,2,1:T(8,128)(2,1)}, bf16[1024,4,512]{0,2,1:T(8,128)(2,1)}) fusion(f32[1024,4,512]{0,2,1:T(8,128)} %fusion.106, f32[1024,4,512]{0,2,1:T(8,128)} %fusion.105, f32[1024,4]{0,1:T(4,128)S(1)} %bitcast.328, bf16[4,512,2048]{2,1,0:T(8,128)(2,1)} %all-gather.8.cloned.1.call-done, ...), kind=kOutput, calls=%fused_computation.8 | convolution fusion | flops 8627679232 | bytes 37781504 | tf_op jit(solution)/shard_map/td,efd->tef/dot_general | solution.py:417
  445.9 13.5 %convert_bitcast_fusion = bf16[4,2048,512]{1,2,0:T(8,128)(2,1)} fusion(bf16[1024,4,512]{0,2,1:T(8,128)(2,1)} %get-tuple-element.66, bf16[1024,2048]{1,0:T(8,128)(2,1)S(1)} %bitcast.276), kind=kOutput, calls=%fused_computation.7 | convolution fusion | flops 8594128896 | bytes 16777216 | tf_op jit(solution)/shard_map/td,tef->edf/dot_general | solution.py:417
  459.4 16.5 %convolution_convert_fusion = bf16[4,512,2048]{2,1,0:T(8,128)(2,1)} fusion(bf16[1024,2048]{1,0:T(8,128)(2,1)} %bitcast.30, f32[1024,4]{0,1:T(4,128)S(1)} %bitcast.329, f32[1024,4,512]{0,2,1:T(8,128)} %fusion.106, f32[1024,4,512]{0,2,1:T(8,128)} %fusion.105), kind=kOutput, calls=%fused_computation.19 | convolution fusion | flops 8608808960 | bytes 29376512 | tf_op jit(solution)/shard_map/tef,td->efd/dot_general | solution.py:417
  476.0 14.0 %convert_bitcast_fusion.1 = bf16[4,2048,512]{1,2,0:T(8,128)(2,1)} fusion(bf16[1024,4,512]{0,2,1:T(8,128)(2,1)} %get-tuple-element.67, bf16[1024,2048]{1,0:T(8,128)(2,1)} %bitcast.275), kind=kOutput, calls=%fused_computation.10 | convolution fusion | flops 8594128896 | bytes 16777216 | tf_op jit(solution)/shard_map/td,tef->edf/dot_general | solution.py:417
  499.6 103.7 %small_sum.5 = f32[16,128]{1,0:T(8,128)} custom-call(f32[8,16,128]{2,1,0:T(8,128)} %bitcast_bitcast_fusion.1.values), custom_call_target="tpu_custom_call" | custom-call | bytes 10000000 | tf_op jit(solution)/shard_map/small_sum/pallas_call | solution.py:368
  604.8 12.8 %fusion.107 = f32[1024,2048,1]{1,0,2:T(8,128)S(1)} fusion(bf16[1024,4,512]{0,2,1:T(8,128)(2,1)} %get-tuple-element.66, bf16[4,2048,512]{2,1,0:T(8,128)(2,1)} %all-gather.4.cloned.1.call-done), kind=kOutput, calls=%fused_computation.196 | convolution fusion | flops 8589934592 | bytes 20971520 | tf_op jit(solution)/shard_map/tef,edf->td/dot_general | solution.py:417
  617.7 13.0 %fusion.1 = bf16[1024,2048]{1,0:T(8,128)(2,1)} fusion(f32[1024,2048,1]{1,0,2:T(8,128)S(1)} %fusion.107, bf16[1024,4,512]{0,2,1:T(8,128)(2,1)S(1)} %copy-done.64, bf16[4,2048,512]{2,1,0:T(8,128)(2,1)} %all-gather.6.cloned.1.call-done), kind=kOutput, calls=%fused_computation.2 | convolution fusion | flops 8594128896 | bytes 25165824 | tf_op jit(solution)/shard_map/tef,edf->td/dot_general | solution.py:417
  630.7 50.8 %reduce_rows.1 = f32[128,2048]{1,0:T(8,128)} custom-call(bf16[8,128,2048]{2,1,0:T(8,128)(2,1)} %bitcast.290), custom_call_target="tpu_custom_call" | custom-call | bytes 100000000 | tf_op jit(solution)/shard_map/reduce_rows/pallas_call | solution.py:255
  684.5 7.2 convolution_convert_fusion.3.refs_0_
  699.3 64.8 %swap.4 = (bf16[8,128,256]{2,1,0:T(8,128)(2,1)}, bf16[8,128,256]{2,1,0:T(8,128)(2,1)}) custom-call(bf16[128,2048]{1,0:T(8,128)(2,1)} %convolution_convert_fusion.3.refs_0_, bf16[128,2048]{1,0:T(8,128)(2,1)} %copy-done.16), custom_call_target="tpu_custom_call" | custom-call | bytes 30000000 | tf_op jit(solution)/shard_map/swap/pallas_call | solution.py:316
  771.2 15.9 %fusion.40 = f32[1024,2,128]{2,0,1:T(8,128)} fusion(f32[2,1024,1024]{1,2,0:T(8,128)} %fusion.108, f32[2,1024,1024]{1,2,0:T(8,128)} %copy-done.9, f32[2,1024]{1,0:T(2,128)S(1)} %copy-done.50, pred[1024,1024]{0,1:T(8,128)(4,1)} %copy-done.17, bf16[1024,2,64]{2,0,1:T(8,128)(2,1)} %copy-done.25, bf16[1024,2,64]{2,0,1:T(8,128)(2,1)} %copy-done.26), kind=kOutput, calls=%fused_computation.64 | convolution fusion | flops 560991232 | bytes 19406848 | tf_op jit(solution)/shard_map/hqk,khd->qhd/dot_general | solution.py:417
  787.1 15.8 %fusion.43 = f32[1024,2,128]{2,0,1:T(8,128)} fusion(f32[2,1024,1024]{1,2,0:T(8,128)} %fusion.108, f32[2,1024,1024]{1,2,0:T(8,128)} %copy-done.9, f32[2,1024]{1,0:T(2,128)S(1)} %copy-done.50, pred[1024,1024]{0,1:T(8,128)(4,1)} %copy-done.17, bf16[1024,2,64]{2,0,1:T(8,128)(2,1)} %copy-done.24, bf16[1024,2,64]{2,0,1:T(8,128)(2,1)} %copy-done.23), kind=kOutput, calls=%fused_computation.65 | convolution fusion | flops 560991232 | bytes 19406848 | tf_op jit(solution)/shard_map/hqk,qhd->khd/dot_general | solution.py:417
  826.7 6.7 convolution_convert_fusion.4
  836.7 12.9 %small_sum.6 = f32[16,128]{1,0:T(8,128)} custom-call(f32[16,128]{1,0:T(8,128)} %reshape.464.values), custom_call_target="tpu_custom_call" | custom-call | bytes 10000000 | tf_op jit(solution)/shard_map/small_sum/pallas_call | solution.py:368
  862.2 6.4 copy.222
  888.9 65.0 %swap.5 = (bf16[128,2048]{1,0:T(8,128)(2,1)}, bf16[128,2048]{1,0:T(8,128)(2,1)}, bf16[128,2048]{1,0:T(8,128)(2,1)}) custom-call(bf16[8,128,256]{2,1,0:T(8,128)(2,1)} %bitcast.296, bf16[8,128,256]{2,1,0:T(8,128)(2,1)} %bitcast.295, bf16[8,128,256]{2,1,0:T(8,128)(2,1)} %copy.243.refs_2_), custom_call_target="tpu_custom_call" | custom-call | bytes 30000000 | tf_op jit(solution)/shard_map/swap/pallas_call | solution.py:316
  957.0 14.5 %all-to-all-start.8 = ((bf16[8,512,256]{2,1,0:T(8,128)(2,1)}), bf16[8,512,256]{2,1,0:T(8,128)(2,1)}, u32[]{:S(2)}, u32[]{:S(2)}) async-start(bf16[8,512,256]{2,1,0:T(8,128)(2,1)} %bitcast.285), calls=%async_computation.13 | async-start | bytes 4194304 | tf_op jit(solution)/shard_map/all_to_all | solution.py:462
  989.9 7.4 convolution_add_fusion.2
  997.2 22.7 %all-to-all-done.8 = bf16[8,512,256]{2,1,0:T(8,128)(2,1)} async-done(((bf16[8,512,256]{2,1,0:T(8,128)(2,1)}), bf16[8,512,256]{2,1,0:T(8,128)(2,1)}, u32[]{:S(2)}, u32[]{:S(2)}) %all-to-all-start.8) | async-done | bytes 2097184 | tf_op jit(solution)/shard_map/all_to_all | solution.py:462
  1024.3 8.1 fusion.49
  1035.9 21.3 %small_sum.7 = f32[16,128]{1,0:T(8,128)} custom-call(f32[32,16,128]{2,1,0:T(8,128)} %bitcast.309), custom_call_target="tpu_custom_call" | custom-call | bytes 10000000 | tf_op jit(solution)/shard_map/small_sum/pallas_call | solution.py:368
  (300 shorter events, 243.6 us)
Async XLA Ops:
  7.2 323.9 %copy-start = (bf16[2048,16]{0,1:T(8,128)(2,1)S(1)}, bf16[2048,16]{0,1:T(8,128)(2,1)}, u32[]{:S(2)}) copy-start(bf16[2048,16]{0,1:T(8,128)(2,1)} %param.28) | copy-start | bytes 196612
  11.5 100.1 %all-to-all-start = ((bf16[8,256,512]{1,2,0:T(8,128)(2,1)}), bf16[8,256,512]{1,2,0:T(8,128)(2,1)S(1)}, u32[]{:S(2)}, u32[]{:S(2)}) async-start(bf16[8,256,512]{1,2,0:T(8,128)(2,1)} %copy.185), calls=%async_computation | async-start | bytes 4194304 | tf_op jit(solution)/shard_map/all_to_all | solution.py:462
  18.8 316.5 %all-gather.4.cloned.1.call-start = ((), (), s32[]{:S(2)}) async-start(), calls=%async_computation.14 | async-start | bytes 10485760 | tf_op jit(solution)/shard_map/all_gather | solution.py:465
  141.3 51.6 %all-to-all-start.1 = ((bf16[8,256,512]{1,2,0:T(8,128)(2,1)}), bf16[8,256,512]{1,2,0:T(8,128)(2,1)}, u32[]{:S(2)}, u32[]{:S(2)}) async-start(bf16[8,256,512]{1,2,0:T(8,128)(2,1)} %copy.186), calls=%async_computation.1 | async-start | bytes 4194304 | tf_op jit(solution)/shard_map/all_to_all | solution.py:462
  146.1 204.3 %all-gather.6.cloned.1.call-start = ((), (), s32[]{:S(2)}) async-start(), calls=%async_computation.15 | async-start | bytes 10485760 | tf_op jit(solution)/shard_map/all_gather | solution.py:465
  196.8 119.6 %all-to-all-start.2 = ((bf16[8,512,256]{2,1,0:T(8,128)(2,1)}), bf16[8,512,256]{2,1,0:T(8,128)(2,1)S(1)}, u32[]{:S(2)}, u32[]{:S(2)}) async-start(bf16[8,512,256]{2,1,0:T(8,128)(2,1)} %bitcast.297), calls=%async_computation.2 | async-start | bytes 4194304 | tf_op jit(solution)/shard_map/all_to_all | solution.py:462
  200.4 181.8 %all-gather.8.cloned.1.call-start = ((), (), s32[]{:S(2)}) async-start(), calls=%async_computation.16 | async-start | bytes 10485760 | tf_op jit(solution)/shard_map/all_gather | solution.py:465
  201.5 63.2 %copy-start.33 = (f32[2048]{0:T(1024)S(1)}, f32[2048]{0:T(1024)}, u32[]{:S(2)}) copy-start(f32[2048]{0:T(1024)} %param.27) | copy-start | bytes 24580
  263.6 59.1 %copy-start.56 = (f32[128]{0:T(128)}, f32[128]{0:T(128)S(1)}, u32[]{:S(2)}) copy-start(f32[128]{0:T(128)S(1)} %get-tuple-element.152) | copy-start | bytes 1540
  263.6 59.1 %copy-start.47 = (f32[128]{0:T(128)}, f32[128]{0:T(128)S(1)}, u32[]{:S(2)}) copy-start(f32[128]{0:T(128)S(1)} %fusion.83) | copy-start | bytes 1540
  264.6 58.2 %copy-start.13 = (bf16[1,128,2048]{2,1,0:T(8,128)(2,1)S(1)}, bf16[1,128,2048]{2,1,0:T(8,128)(2,1)}, u32[]{:S(2)}) copy-start(bf16[1,128,2048]{2,1,0:T(8,128)(2,1)} %param.19) | copy-start | bytes 1572868
  325.3 98.3 %all-to-all-start.3 = ((bf16[8,128,2048]{2,1,0:T(8,128)(2,1)}), bf16[8,128,2048]{2,1,0:T(8,128)(2,1)}, u32[]{:S(2)}, u32[]{:S(2)}) async-start(bf16[8,128,2048]{2,1,0:T(8,128)(2,1)} %broadcast_in_dim.56), calls=%async_computation.3 | async-start | bytes 8388608 | tf_op jit(solution)/shard_map/all_to_all | solution.py:462
  331.0 299.6 %reduce-scatter.6.cloned.1.call-start = ((), (), s32[]{:S(2)}) async-start(), calls=%async_computation.17 | async-start | bytes 4718592 | tf_op jit(solution)/shard_map/reduce_scatter | solution.py:529
  423.7 268.0 %reduce-scatter.10.cloned.1.call-start = ((), (), s32[]{:S(2)}) async-start(), calls=%async_computation.19 | async-start | bytes 10485760 | tf_op jit(solution)/shard_map/reduce_scatter | solution.py:549
  459.4 304.8 %reduce-scatter.8.cloned.1.call-start = ((), (), s32[]{:S(2)}) async-start(), calls=%async_computation.18 | async-start | bytes 10485760 | tf_op jit(solution)/shard_map/reduce_scatter | solution.py:549
  490.0 464.0 %reduce-scatter.12.cloned.1.call-start = ((), (), s32[]{:S(2)}) async-start(), calls=%async_computation.20 | async-start | bytes 10485760 | tf_op jit(solution)/shard_map/reduce_scatter | solution.py:549
  493.7 137.0 %all-to-all-start.4 = ((bf16[8,128,2048]{2,1,0:T(8,128)(2,1)}), bf16[8,128,2048]{2,1,0:T(8,128)(2,1)}, u32[]{:S(2)}, u32[]{:S(2)}) async-start(bf16[8,128,2048]{2,1,0:T(8,128)(2,1)} %broadcast_in_dim.57), calls=%async_computation.5 | async-start | bytes 8388608 | tf_op jit(solution)/shard_map/all_to_all | solution.py:462
  617.6 63.9 %copy-start.2 = (f32[128,2048]{1,0:T(8,128)S(1)}, f32[128,2048]{1,0:T(8,128)}, u32[]{:S(2)}) copy-start(f32[128,2048]{1,0:T(8,128)} %copy-done.1) | copy-start | bytes 3145732
  617.6 63.9 %copy-start.34 = (f32[2048]{0:T(1024)S(1)}, f32[2048]{0:T(1024)}, u32[]{:S(2)}) copy-start(f32[2048]{0:T(1024)} %param.27) | copy-start | bytes 24580
  617.6 63.9 %copy-start.48 = (f32[128]{0:T(128)S(1)}, f32[128]{0:T(128)}, u32[]{:S(2)}) copy-start(f32[128]{0:T(128)} %copy-done.47) | copy-start | bytes 1540
  630.6 52.7 %copy-start.57 = (f32[128]{0:T(128)S(1)}, f32[128]{0:T(128)}, u32[]{:S(2)}) copy-start(f32[128]{0:T(128)} %copy-done.56) | copy-start | bytes 1540
  630.6 52.7 %copy-start.14 = (bf16[1,128,2048]{2,1,0:T(8,128)(2,1)S(1)}, bf16[1,128,2048]{2,1,0:T(8,128)(2,1)}, u32[]{:S(2)}) copy-start(bf16[1,128,2048]{2,1,0:T(8,128)(2,1)} %param.19) | copy-start | bytes 1572868
  694.7 76.5 %copy-start.50 = (f32[2,1024]{1,0:T(2,128)S(1)}, f32[2,1024]{1,0:T(2,128)}, u32[]{:S(2)}) copy-start(f32[2,1024]{1,0:T(2,128)} %copy-done.49) | copy-start | bytes 24580
  694.7 138.7 %all-to-all-start.5 = ((bf16[8,256,512]{1,2,0:T(8,128)(2,1)}), bf16[8,256,512]{1,2,0:T(8,128)(2,1)}, u32[]{:S(2)}, u32[]{:S(2)}) async-start(bf16[8,256,512]{1,2,0:T(8,128)(2,1)} %bitcast.284), calls=%async_computation.8 | async-start | bytes 4194304 | tf_op jit(solution)/shard_map/all_to_all | solution.py:462
  699.3 320.7 %reduce-scatter.14.cloned.1.call-start = ((), (), s32[]{:S(2)}) async-start(), calls=%async_computation.21 | async-start | bytes 5242880 | tf_op jit(solution)/shard_map/reduce_scatter | solution.py:607
  876.6 77.4 %all-to-all-start.6 = ((bf16[8,256,512]{1,2,0:T(8,128)(2,1)}), bf16[8,256,512]{1,2,0:T(8,128)(2,1)}, u32[]{:S(2)}, u32[]{:S(2)}) async-start(bf16[8,256,512]{1,2,0:T(8,128)(2,1)} %bitcast.286), calls=%async_computation.9 | async-start | bytes 4194304 | tf_op jit(solution)/shard_map/all_to_all | solution.py:462
  957.0 62.9 %all-to-all-start.8 = ((bf16[8,512,256]{2,1,0:T(8,128)(2,1)}), bf16[8,512,256]{2,1,0:T(8,128)(2,1)}, u32[]{:S(2)}, u32[]{:S(2)}) async-start(bf16[8,512,256]{2,1,0:T(8,128)(2,1)} %bitcast.285), calls=%async_computation.13 | async-start | bytes 4194304 | tf_op jit(solution)/shard_map/all_to_all | solution.py:462
  1020.0 56.2 %all-to-all-start.7 = ((bf16[8,64,1024]{2,1,0:T(8,128)(2,1)}), bf16[8,64,1024]{2,1,0:T(8,128)(2,1)}, u32[]{:S(2)}, u32[]{:S(2)}) async-start(bf16[8,64,1024]{2,1,0:T(8,128)(2,1)} %bitcast.308), calls=%async_computation.12 | async-start | bytes 2097152 | tf_op jit(solution)/shard_map/all_to_all | solution.py:608
  1033.9 34.7 %copy-start.59 = (f32[128]{0:T(128)S(1)}, f32[128]{0:T(128)}, u32[]{:S(2)}) copy-start(f32[128]{0:T(128)} %copy-done.58) | copy-start | bytes 1540
  1033.9 34.7 %copy-start.60 = (f32[128]{0:T(128)S(1)}, f32[128]{0:T(128)}, u32[]{:S(2)}) copy-start(f32[128]{0:T(128)} %get-tuple-element.103) | copy-start | bytes 1540
  1033.9 35.3 %copy-start.15 = (bf16[1,128,2048]{2,1,0:T(8,128)(2,1)S(1)}, bf16[1,128,2048]{2,1,0:T(8,128)(2,1)}, u32[]{:S(2)}) copy-start(bf16[1,128,2048]{2,1,0:T(8,128)(2,1)} %param.19) | copy-start | bytes 1572868
  1033.9 35.3 %copy-start.55 = (f32[128]{0:T(128)S(1)}, f32[128]{0:T(128)}, u32[]{:S(2)}) copy-start(f32[128]{0:T(128)} %copy-done.54) | copy-start | bytes 1540
  (50 other events, 551.2 us)
Sparse Core Ops, SparseCore 0:
  114.1 60.4 all-gather.3
  196.9 57.1 all-gather.5
  322.9 59.3 all-gather.7
  423.8 96.3 reduce-scatter.5
  522.6 89.3 reduce-scatter.9
  614.4 71.4 reduce-scatter.7
  688.4 71.4 reduce-scatter.11
  873.7 45.5 reduce-scatter.13

commit v4 on v3

--- a/solution.py
+++ b/solution.py
@@ -52,24 +52,26 @@
     pl.semaphore_wait(barrier, count - 1)
 
 
-def gather_kernel(nz, ny, pieces, *refs):
-    if len(refs) == 5:
-        block, out, own_sem, send_sem, recv_sem = refs
-        note = None
-    else:
-        block, note, out, note_out, own_sem, send_sem, recv_sem, note_send, note_recv = refs
+def gather_kernel(nz, ny, pieces, count, *refs):
+    noted = len(refs) > 2 * count + 3
+    ins, outs, sems = refs[: count + noted], refs[count + noted : -3 - 2 * noted], refs[-3 - 2 * noted :]
+    own_sem, send_sem, recv_sem = sems[:3]
     me = lax.axis_index("group")
     z, y = me // ny, me % ny
-    rows = block.shape[0] // pieces
 
     def at(z_to, y_to):
         return {"group": z_to * ny + y_to}
 
     def note_copy(k):
         to = {"group": lax.rem(me + k, nz * ny)}
-        return remote(note, note_out.at[me], note_send.at[k], note_recv.at[k], to)
-
-    if note is None:
+        return remote(ins[count], outs[count].at[me], sems[3].at[k], sems[4].at[k], to)
+
+    if noted:
+        greet_all(nz * ny, lambda k: {"group": lax.rem(me + k, nz * ny)})
+        for k in range(1, nz * ny):
+            note_copy(k).start()
+        outs[count][me] = ins[count][...]
+    else:
         greet(
             [
                 (z > 0, at(z - 1, y)),
@@ -78,23 +80,20 @@
                 (y < ny - 1, at(z, y + 1)),
             ]
         )
-    else:
-        greet_all(nz * ny, lambda k: {"group": lax.rem(me + k, nz * ny)})
-        for k in range(1, nz * ny):
-            note_copy(k).start()
-        note_out[me] = note[...]
-    own = pltpu.make_async_copy(block, out.at[me], own_sem)
-    own.start()
+    owns = [pltpu.make_async_copy(ins[n], outs[n].at[me], own_sem.at[n]) for n in range(count)]
+    for own in owns:
+        own.start()
 
     def part(ref, c):
+        rows = ref.shape[0] // pieces
         return ref.at[pl.ds(c * rows, rows)]
 
-    def copy(slot, source, c, where, first):
+    def copy(slot, source, n, c, where, first):
         return remote(
-            part(block, c) if first else part(out.at[source], c),
-            part(out.at[source], c),
-            send_sem.at[slot, source, c],
-            recv_sem.at[source, c],
+            part(ins[n], c) if first else part(outs[n].at[source], c),
+            part(outs[n].at[source], c),
+            send_sem.at[n, slot, source, c],
+            recv_sem.at[n, source, c],
             where,
         )
 
@@ -108,19 +107,19 @@
             (go & (sy >= y) & (y > 0), 3, at(z, y - 1)),
         ]
 
-    def act(source, first, go, start):
+    def act(source, n, first, go, start):
         for c in range(pieces):
             if start and not first:
 
                 @pl.when(go)
                 def _():
-                    copy(0, source, c, at(z, y), False).wait_recv()
+                    copy(0, source, n, c, at(z, y), False).wait_recv()
 
             for cond, slot, where in outgoing(source, go):
 
                 @pl.when(cond)
                 def _(slot=slot, where=where):
-                    one = copy(slot, source, c, where, first)
+                    one = copy(slot, source, n, c, where, first)
                     if start:
                         one.start()
                     else:
@@ -137,33 +136,40 @@
     order = sorted(order, key=lambda t: (t[0], -t[1]))
     for start in (True, False):
         for distance, _, source, inside in order:
-            act(source, distance == 0, inside, start)
+            for n in range(count):
+                act(source, n, distance == 0, inside, start)
         if start:
-            own.wait()
-    if note is not None:
+            for own in owns:
+                own.wait()
+    if noted:
         for k in range(1, nz * ny):
             note_copy(k).wait()
 
 
-def gather_rows(block, groups, collective_id, pieces=2, note=None):
+def gather_rows(blocks, groups, collective_id, pieces=2, note=None):
     nz = min(4, groups)
+    count = len(blocks)
     notes = [] if note is None else [note]
     outs = pl.pallas_call(
-        functools.partial(gather_kernel, nz, groups // nz, pieces),
+        functools.partial(gather_kernel, nz, groups // nz, pieces, count),
         name="gather_rows",
-        out_shape=[jax.ShapeDtypeStruct((groups,) + a.shape, a.dtype) for a in [block] + notes],
-        in_specs=[VMEM_SPEC] * (1 + len(notes)),
-        out_specs=[pl.BlockSpec(memory_space=pl.ANY)] + [VMEM_SPEC] * len(notes),
-        scratch_shapes=[DMA, DMA((4, groups, pieces)), DMA((groups, pieces))]
+        out_shape=[jax.ShapeDtypeStruct((groups,) + a.shape, a.dtype) for a in blocks + notes],
+        in_specs=[VMEM_SPEC] * (count + len(notes)),
+        out_specs=[pl.BlockSpec(memory_space=pl.ANY)] * count + [VMEM_SPEC] * len(notes),
+        scratch_shapes=[DMA((count,)), DMA((count, 4, groups, pieces)), DMA((count, groups, pieces))]
         + [DMA((groups,))] * 2 * len(notes),
         compiler_params=comm_params(collective_id),
-        cost_estimate=pl.CostEstimate(flops=0, bytes_accessed=200_000_000, transcendentals=0),
-    )(block, *notes)
-    rows = outs[0].reshape(groups * block.shape[0], block.shape[1])
-    return rows if note is None else (rows, outs[1])
-
-
-def reduce_kernel(nz, ny, pieces, parts, out, ybuf, zbuf, ysend, yrecv, zsend, zrecv):
+        cost_estimate=pl.CostEstimate(
+            flops=0, bytes_accessed=200_000_000 * count, transcendentals=0
+        ),
+    )(*blocks, *notes)
+    rows = [a.reshape(groups * b.shape[0], b.shape[1]) for a, b in zip(outs, blocks)]
+    return rows + list(outs[count:])
+
+
+def reduce_kernel(
+    nz, ny, pieces, parts, note, out, note_out, ybuf, zbuf, landed, ysend, yrecv, zsend, zrecv, nsend, nrecv
+):
     me = lax.axis_index("group")
     z, y = me // ny, me % ny
     rows = parts.shape[1] // pieces
@@ -171,7 +177,14 @@
     def at(z_to, y_to):
         return {"group": z_to * ny + y_to}
 
-    greet([(z > 0, at(z - 1, y)), (z < nz - 1, at(z + 1, y)), (z >= 0, at(z, 1 - y))])
+    def note_copy(k):
+        to = lax.rem(me + k, nz * ny)
+        return remote(note.at[to], landed.at[k], nsend.at[k], nrecv.at[k], {"group": to})
+
+    greet_all(nz * ny, lambda k: {"group": lax.rem(me + k, nz * ny)})
+    for k in range(1, nz * ny):
+        note_copy(k).start()
+    landed[0] = note[me]
 
     def part(ref, c):
         return ref.at[pl.ds(c * rows, rows)]
@@ -244,31 +257,41 @@
 
     for c in range(pieces):
         y_copy(z, c).wait_send()
-
-
-def reduce_rows(parts, groups, collective_id, pieces=2):
+    for k in range(1, nz * ny):
+        note_copy(k).wait()
+    note_out[...] = jnp.sum(landed[...], axis=0)
+
+
+def reduce_rows(parts, note, groups, collective_id, pieces=2):
     nz = min(4, groups)
     ny = groups // nz
     if ny != 2:
-        return lax.psum_scatter(parts, "group", scatter_dimension=0, tiled=True).astype(F32)
+        total = lax.psum_scatter(parts, "group", scatter_dimension=0, tiled=True).astype(F32)
+        return total, lax.psum_scatter(note, "group", scatter_dimension=0, tiled=False)
     rows, width = parts.shape[0] // groups, parts.shape[1]
     return pl.pallas_call(
         functools.partial(reduce_kernel, nz, ny, pieces),
         name="reduce_rows",
-        out_shape=jax.ShapeDtypeStruct((rows, width), F32),
-        in_specs=[VMEM_SPEC],
-        out_specs=VMEM_SPEC,
+        out_shape=[
+            jax.ShapeDtypeStruct((rows, width), F32),
+            jax.ShapeDtypeStruct(note.shape[1:], F32),
+        ],
+        in_specs=[VMEM_SPEC] * 2,
+        out_specs=[VMEM_SPEC] * 2,
         scratch_shapes=[
             pltpu.VMEM((nz, rows, width), BF16),
             pltpu.VMEM((2, nz, rows, width), BF16),
+            pltpu.VMEM(note.shape, F32),
             DMA((nz, pieces)),
             DMA((nz, pieces)),
             DMA((nz, pieces)),
             DMA((2, nz, pieces)),
+            DMA((groups,)),
+            DMA((groups,)),
         ],
         compiler_params=comm_params(collective_id),
-        cost_estimate=pl.CostEstimate(flops=0, bytes_accessed=100_000_000, transcendentals=0),
-    )(parts.reshape(groups, rows, width))
+        cost_estimate=pl.CostEstimate(flops=0, bytes_accessed=200_000_000, transcendentals=0),
+    )(parts.reshape(groups, rows, width), note)
 
 
 def swap_kernel(groups, to_rows, *refs):
@@ -472,12 +495,13 @@
     expert_ids = jnp.arange(experts, dtype=jnp.int32)
     marks = jnp.any(routing[0][:, :, None] == expert_ids[None, None, :], axis=1).astype(F32)
     marks = jnp.concatenate([marks.T, segment_ids[0].astype(F32)[None]], axis=0)
-    normed_all, marks = gather_rows(normed_b, groups, 1, note=marks)
+    normed_all, grad_all, marks = gather_rows([normed_b, out_grad[0]], groups, 1, note=marks)
     marks = marks.transpose(1, 0, 2).reshape(experts + 1, length)
     chosen, seg_all = marks[:experts].T > 0.5, marks[experts]
-    gate_own, up_in, normed_late = together((gate_own, slices(w_up), normed_all))
+    down_in = w_down.reshape(groups, part, cols)
+    gate_own, down_in, normed_late = together((gate_own, down_in, normed_all))
     gate_w = row_of_devices(gate_own.reshape(width, part))
-    up_own = exchange(up_in)
+    down_own = exchange(down_in)
     wq, wk, wv = own_cols(w_query, 1), own_cols(w_key, 1), own_cols(w_value, 1)
     query_raw, key_raw = mm(normed_all, wq), mm(normed_all, wk)
     values_b = mm(normed_all, wv).astype(BF16).reshape(length, heads, head_dim)
@@ -505,16 +529,16 @@
     probs = jnp.exp(scores - log_total)
     probs_b = probs.astype(BF16)
     mixed_c = ein("hqk,khd->qhd", probs_b, values_b).reshape(length, cols).astype(BF16)
-    up_own, down_in, mixed_c = together((up_own, w_down.reshape(groups, part, cols), mixed_c))
-    up_w = row_of_devices(up_own.reshape(width, part))
-    down_own = exchange(down_in)
-    (mixed_b,) = swap([mixed_c], groups, False, 3)
+    down_own, mixed_in = together((down_own, mixed_c))
+    down_w = row_of_devices(down_own.transpose(1, 0, 2).reshape(part, width))
+    (mixed_b,) = swap([mixed_in], groups, False, 3)
+    up_in, mixed_b = together((slices(w_up), mixed_b))
+    up_own = exchange(up_in)
     resid = inputs + mm(mixed_b, w_out)
     normed_mlp_b = rms_norm(resid, mlp_gain).astype(BF16)
-    mlp_all = gather_rows(normed_mlp_b, groups, 4)
-    down_own, grad_in, mlp_late = together((down_own, out_grad[0], mlp_all))
-    down_w = row_of_devices(down_own.transpose(1, 0, 2).reshape(part, width))
-    grad_all = exchange(jnp.broadcast_to(grad_in, (groups, rows, width))).reshape(length, width)
+    (mlp_all,) = gather_rows([normed_mlp_b], groups, 4)
+    up_own, down_w, mlp_late = together((up_own, down_w, mlp_all))
+    up_w = row_of_devices(up_own.reshape(width, part))
 
     router_all = jax.nn.softmax(mm(mlp_all, w_router), axis=-1)
     picked = jnp.where(chosen, router_all, 0.0).reshape(length, sources, local_experts)
@@ -525,9 +549,7 @@
     hidden = gate_pre * sigma * up_pre
     hidden_b = (hidden * picked).astype(BF16)
     out_part = ein("tef,efd->td", hidden_b, down_w).astype(BF16)
-    out_part, grad_all, mixed_in = together((out_part, grad_all, mixed_b))
     mixture = lax.psum_scatter(out_part, "group", scatter_dimension=0, tiled=True)
-    mixed_all = exchange(jnp.broadcast_to(mixed_in, (groups, rows, width))).reshape(length, width)
     hidden_grad = ein("td,efd->tef", grad_all, down_w)
     picked_grad = jnp.sum(hidden * hidden_grad, axis=2)
     hidden_grad = hidden_grad * picked
@@ -537,7 +559,6 @@
     full_part = jnp.where(own_expert[None, None, :], picked_grad[:, :, None], 0.0)
     full_part = jnp.where(chosen, full_part.reshape(length, experts), 0.0)
     full_part = full_part.T.reshape(experts, groups, rows).transpose(1, 0, 2)
-    router_full_grad = small_sum(full_part, ("group",), True, 10).T
     gate_w_part = ein("td,tef->edf", mlp_late, gate_grad_b).astype(BF16)
     up_w_part = ein("td,tef->edf", mlp_late, up_grad_b).astype(BF16)
     down_w_part = ein("tef,td->efd", hidden_b, grad_all).astype(BF16)
@@ -550,8 +571,9 @@
 
     gate_sum, up_sum, down_sum = over_row(gate_w_part), over_row(up_w_part), over_row(down_w_part)
     slot_part = ein("tef,edf->td", gate_grad_b, gate_w) + ein("tef,edf->td", up_grad_b, up_w)
-    slot_part, mixture, mixed_all = together((slot_part.astype(BF16), mixture, mixed_all))
-    slot_sum = reduce_rows(slot_part, groups, 5)
+    slot_part, mixture = together((slot_part.astype(BF16), mixture))
+    slot_sum, router_full_grad = reduce_rows(slot_part, full_part, groups, 5)
+    router_full_grad = router_full_grad.T
 
     def slices_out(w):
         w = w.reshape(local_experts, parts, cols, part).transpose(0, 2, 1, 3)
@@ -569,12 +591,11 @@
     resid_part, mlp_gain_grad = mlp_back(mlp_in_grad)
     resid_grad = grad_out + resid_part
     attn_grad_b = resid_grad.astype(BF16)
-    mixed_grad_b = mm_nt(attn_grad_b, w_out).astype(BF16)
-    gate_sum, mixed_grad_b, attn_grad_b = together((gate_sum, mixed_grad_b, attn_grad_b))
-    gate_sum = exchange(gate_sum.reshape(groups, cols, part))
-    mixed_grad_c, attn_grad_c = swap([mixed_grad_b, attn_grad_b], groups, True, 6)
-    up_sum, mixed_grad_c, attn_grad_c = together((up_sum, mixed_grad_c, attn_grad_c))
-    out_w_part = mm_tn(mixed_all, attn_grad_c).astype(BF16)
+    (attn_grad_all,) = gather_rows([attn_grad_b], groups, 6)
+    gate_sum, up_sum, attn_grad_late = together((gate_sum, up_sum, attn_grad_all))
+    gate_up_sum = jnp.concatenate([gate_sum, up_sum], axis=1).reshape(groups, cols, 2 * part)
+    gate_up_sum = exchange(gate_up_sum)
+    mixed_grad_c = mm_nt(attn_grad_all, own_cols(w_out, 0)).astype(BF16)
     mixed_grad_c = mixed_grad_c.reshape(length, heads, head_dim)
 
     prob_grad = ein("qhd,khd->hqk", mixed_grad_c, values_b)
@@ -589,29 +610,25 @@
 
     query_turn, key_turn = unturned(query_grad), unturned(key_grad)
     query_mix, key_mix = query_turn * query_gain_c, key_turn * key_gain_c
-    query_dots, key_dots, gate_sum, up_sum = together(
-        (query_mix * query_raw, key_mix * key_raw, gate_sum, up_sum)
-    )
-    up_sum = exchange(up_sum.reshape(groups, cols, part))
-    dots = row_sums(query_dots, key_dots, 7)
+    dots = row_sums(query_mix * query_raw, key_mix * key_raw, 7)
     query_raw_b = (
         query_scale * query_mix - query_raw * query_scale**3 * dots[0]
     ).astype(BF16)
     key_raw_b = (key_scale * key_mix - key_raw * key_scale**3 * dots[1]).astype(BF16)
     query_gain_part = jnp.sum(query_turn * query_raw * query_scale, axis=0)
     key_gain_part = jnp.sum(key_turn * key_raw * key_scale, axis=0)
-    raw_grads = jnp.concatenate([query_raw_b, key_raw_b, value_grad_b], axis=1)
-    qkv_part = jnp.concatenate([mm_tn(normed_late, raw_grads).astype(BF16), out_w_part], axis=1)
-    qkv_part = qkv_part.reshape(groups, sources, -1, 4 * cols).transpose(1, 0, 2, 3)
-    qkv_part = qkv_part.reshape(sources, -1, 4 * cols)
-    qkv_part = lax.psum_scatter(qkv_part, "expert", scatter_dimension=0, tiled=False)
-    qkv_part = lax.all_to_all(qkv_part.reshape(groups, -1, 4 * cols), "group", 0, 0, tiled=True)
-    qkv_part = qkv_part.transpose(1, 0, 2).reshape(-1, groups, 4, cols).astype(F32)
-    query_own, key_own, value_own = swap([query_raw_b, key_raw_b, value_grad_b], groups, False, 8)
-    query_own, key_own, value_own, up_sum, down_sum = together(
-        (query_own, key_own, value_own, up_sum, down_sum)
+    raw_grads = [query_raw_b, key_raw_b, value_grad_b]
+    (query_own, key_own, value_own), raw_grads, gate_up_sum, down_sum = together(
+        (swap(raw_grads, groups, False, 8), raw_grads, gate_up_sum, down_sum)
     )
     down_sum = exchange(down_sum.reshape(part, groups, cols).transpose(1, 0, 2))
+    out_w_part = mm_tn(mixed_c, attn_grad_late).astype(BF16)
+    out_w_grad = lax.psum_scatter(out_w_part, "expert", scatter_dimension=0, tiled=True)
+    qkv_part = mm_tn(normed_late, jnp.concatenate(raw_grads, axis=1)).astype(BF16)
+    qkv_part = qkv_part.reshape(groups, sources, -1, 3 * cols).transpose(1, 0, 2, 3)
+    qkv_part = over_row(qkv_part.reshape(sources, -1, 3 * cols)).reshape(groups, -1, 3 * cols)
+    qkv_part = exchange(qkv_part)
+    qkv_part = qkv_part.transpose(1, 0, 2).reshape(-1, groups, 3, cols).astype(F32)
     normed_grad = mm_nt(query_own, w_query) + mm_nt(key_own, w_key) + mm_nt(value_own, w_value)
     _, attn_back = jax.vjp(rms_norm, inputs, attn_gain)
     input_part, attn_gain_grad = attn_back(normed_grad)
@@ -636,11 +653,11 @@
         qkv_part[:, :, 2].reshape(-1, width),
         small[experts + 2],
         small[experts + 3],
-        qkv_part[:, :, 3].reshape(-1, width),
+        out_w_grad.astype(F32),
         small[experts],
         small[:experts].T,
-        slices_out(gate_sum),
-        slices_out(up_sum),
+        slices_out(gate_up_sum[:, :, :part]),
+        slices_out(gate_up_sum[:, :, part:]),
         down_sum.reshape(local_experts, hidden_size, cols).astype(F32),
     )
 

time: 1110 us -> 966 us (0.87)
  Pallas kernels: 524 us -> 414 us
  local copies, waits for them, and re-layouts: 109 us -> 82.7 us
  waiting for transfers between devices: 87.5 us -> 110 us
    pallas_call x3 -> x2, Pallas kernels: 187 us -> 44.2 us  [swap(): pl.pallas_call(functools.partial(swap_kernel, groups, to_rows), name='swa...]
    pallas_call x2 -> x3, Pallas kernels: 138 us -> 244 us  [gather_rows(): pl.pallas_call(functools.partial(gather_kernel, nz, groups // nz, pieces,...]
    pallas_call x4 -> x3, Pallas kernels: 148 us -> 70.9 us  [small_sum(): pl.pallas_call(functools.partial(small_sum_kernel, axes, scatter), name='...]
    all_to_all x8 -> x6, waiting for transfers between devices: 69.3 us -> 36 us  [exchange(): return lax.all_to_all(w, 'group', 0, 0, tiled=True)]
    reduce_scatter x3 -> x4, waiting for transfers between devices: 0.04 us -> 31.5 us  [over_row(): return lax.psum_scatter(w, 'expert', scatter_dimension=0, tiled=False)]
    all_gather x3, waiting for transfers between devices: 17.3 us -> 42.2 us  [row_of_devices(): return lax.all_gather(w, 'expert', axis=0, tiled=False)]
    all_to_all x8 -> x6, starting transfers between devices: 50.2 us -> 43.8 us  [exchange(): return lax.all_to_all(w, 'group', 0, 0, tiled=True)]
  transfers between devices with their start and end apart: 17 -> 15, of which waited for: 4 -> 4; matrix products, arithmetic and copies ran while one was open for 35% -> 33% of each run, Pallas kernels for 48% -> 43%
where the time goes in v4:
time: 966 us; the launch traced here: 958 us
  Pallas kernels  414 us (43%)
  matrix products  239 us (25%)
  waiting for transfers between devices  110 us (11%)
  local copies, waits for them, and re-layouts  82.7 us (9%)
  other arithmetic  51.1 us (5%)
  starting transfers between devices  44.8 us (5%)
  between operations  15.4 us (2%)
    pallas_call x3, Pallas kernels, gather_rows(): pl.pallas_call(functools.partial(gather_kernel, nz, groups // nz, pieces,...  244 us
    dot_general x15, matrix products, ein(): return jnp.einsum(spec, *ops, preferred_element_type=F32)  186 us
    pallas_call x3, Pallas kernels, small_sum(): pl.pallas_call(functools.partial(small_sum_kernel, axes, scatter), name='...  70.9 us
    pallas_call x1, Pallas kernels, reduce_rows(): pl.pallas_call(functools.partial(reduce_kernel, nz, ny, pieces), name='re...  55.5 us
    pallas_call x2, Pallas kernels, swap(): pl.pallas_call(functools.partial(swap_kernel, groups, to_rows), name='swa...  44.2 us
    all_to_all x6, starting transfers between devices, exchange(): return lax.all_to_all(w, 'group', 0, 0, tiled=True)  43.8 us
    all_gather x3, waiting for transfers between devices, row_of_devices(): return lax.all_gather(w, 'expert', axis=0, tiled=False)  42.2 us
    all_to_all x6, waiting for transfers between devices, exchange(): return lax.all_to_all(w, 'group', 0, 0, tiled=True)  36 us
  transfers between devices with their start and end apart: 15, of which 4 were waited for; matrix products, arithmetic and copies ran while one was open for 33% of the time, Pallas kernels for 43%

profile of v4, /device:TPU:0, one launch (start us, length us, event | category | flops | bytes accessed | tf_op | source)
XLA Modules:
  0.0 958.2 jit_solution(17193589831347856647)
XLA Ops:
  11.5 7.3 all-to-all-start
  22.2 115.2 %gather_rows.3 = (bf16[8,128,2048]{2,1,0:T(8,128)(2,1)}, bf16[8,128,2048]{2,1,0:T(8,128)(2,1)}, f32[8,17,128]{2,1,0:T(8,128)}) custom-call(bf16[128,2048]{1,0:T(8,128)(2,1)} %fusion.45.refs_0_, bf16[128,2048]{1,0:T(8,128)(2,1)} %bitcast.278, f32[17,128]{1,0:T(8,128)} %pad_maximum_fusion.11.refs_2_), custom_call_target="tpu_custom_call" | custom-call | bytes 400000000 | tf_op jit(solution)/shard_map/gather_rows/pallas_call | solution.py:153
  145.0 15.9 %small_sum.3 = f32[16,128]{1,0:T(8,128)} custom-call(f32[16,128]{1,0:T(8,128)} %reshape.439.values), custom_call_target="tpu_custom_call" | custom-call | bytes 10000000 | tf_op jit(solution)/shard_map/small_sum/pallas_call | solution.py:391
  193.1 22.8 %all-to-all-done.1 = bf16[8,512,256]{2,1,0:T(8,128)(2,1)} async-done(((bf16[8,512,256]{2,1,0:T(8,128)(2,1)}), bf16[8,512,256]{2,1,0:T(8,128)(2,1)}, u32[]{:S(2)}, u32[]{:S(2)}) %all-to-all-start.1) | async-done | bytes 2097184 | tf_op jit(solution)/shard_map/all_to_all | solution.py:485
  226.7 13.5 %swap.2 = bf16[128,2048]{1,0:T(8,128)(2,1)} custom-call(bf16[8,128,256]{2,1,0:T(8,128)(2,1)} %bitcast.289), custom_call_target="tpu_custom_call" | custom-call | bytes 30000000 | tf_op jit(solution)/shard_map/swap/pallas_call | solution.py:339
  242.6 7.6 all-to-all-start.2
  257.4 79.1 %gather_rows.4 = bf16[8,128,2048]{2,1,0:T(8,128)(2,1)} custom-call(bf16[128,2048]{1,0:T(8,128)(2,1)} %multiply_convert_fusion.6.refs_0_), custom_call_target="tpu_custom_call" | custom-call | bytes 200000000 | tf_op jit(solution)/shard_map/gather_rows/pallas_call | solution.py:153
  342.6 14.7 %fusion.103 = f32[1024,4,512]{0,2,1:T(8,128)} fusion(bf16[1024,2048,1]{1,0,2:T(8,128)(2,1)} %bitcast.259, bf16[4,2048,512]{2,1,0:T(8,128)(2,1)} %all-gather.6.cloned.1.call-done), kind=kOutput, calls=%fused_computation.192 | convolution fusion | flops 8589934592 | bytes 20971520 | tf_op jit(solution)/shard_map/td,edf->tef/dot_general | solution.py:440
  357.3 42.1 %all-gather.8.cloned.1.call-done = bf16[4,2048,512]{2,1,0:T(8,128)(2,1)} async-done(((bf16[1,2048,512]{2,1,0:T(8,128)(2,1)}), bf16[4,2048,512]{2,1,0:T(8,128)(2,1)}) %all-gather.8.cloned.1.call-update) | async-done | bytes 8388624 | tf_op jit(solution)/shard_map/all_gather | solution.py:488
  399.4 14.7 %fusion.104 = f32[1024,4,512]{0,2,1:T(8,128)} fusion(bf16[1024,2048,1]{1,0,2:T(8,128)(2,1)} %bitcast.260, bf16[4,2048,512]{2,1,0:T(8,128)(2,1)} %all-gather.8.cloned.1.call-done), kind=kOutput, calls=%fused_computation.193 | convolution fusion | flops 8589934592 | bytes 20971520 | tf_op jit(solution)/shard_map/td,edf->tef/dot_general | solution.py:440
  414.2 16.7 %bitcast_convert_fusion = bf16[1024,2048]{1,0:T(8,128)(2,1)} fusion(bf16[4,512,2048]{2,1,0:T(8,128)(2,1)} %all-gather.4.cloned.1.call-done, f32[1024,4]{0,1:T(4,128)S(1)} %bitcast.317, f32[1024,4,512]{0,2,1:T(8,128)} %fusion.104, f32[1024,4,512]{0,2,1:T(8,128)S(1)} %copy-done.67), kind=kOutput, calls=%fused_computation.1 | convolution fusion | flops 8606711808 | bytes 29376512 | tf_op jit(solution)/shard_map/tef,efd->td/dot_general | solution.py:440
  431.0 21.8 %multiply_reduce_fusion.1 = (f32[1024,4]{0,1:T(4,128)S(1)}, bf16[1024,4,512]{0,2,1:T(8,128)(2,1)}, bf16[1024,4,512]{0,2,1:T(8,128)(2,1)}) fusion(f32[1024,4,512]{0,2,1:T(8,128)} %fusion.104, f32[1024,4,512]{0,2,1:T(8,128)} %fusion.103, f32[1024,4]{0,1:T(4,128)S(1)} %bitcast.318, bf16[1024,2048,1]{1,0,2:T(8,128)(2,1)} %bitcast.330, ...), kind=kOutput, calls=%fused_computation.8 | convolution fusion | flops 8627679232 | bytes 37781504 | tf_op jit(solution)/shard_map/td,efd->tef/dot_general | solution.py:440
  452.8 13.4 %convert_bitcast_fusion = bf16[4,2048,512]{1,2,0:T(8,128)(2,1)} fusion(bf16[1024,4,512]{0,2,1:T(8,128)(2,1)} %get-tuple-element.61, bf16[1024,2048]{1,0:T(8,128)(2,1)S(1)} %bitcast.262), kind=kOutput, calls=%fused_computation.4 | convolution fusion | flops 8594128896 | bytes 16777216 | tf_op jit(solution)/shard_map/td,tef->edf/dot_general | solution.py:440
  466.2 16.3 %convolution_convert_fusion = bf16[4,512,2048]{2,1,0:T(8,128)(2,1)} fusion(bf16[1024,2048,1]{1,0,2:T(8,128)(2,1)} %bitcast.331, f32[1024,4]{0,1:T(4,128)S(1)} %bitcast.319, f32[1024,4,512]{0,2,1:T(8,128)} %fusion.104, f32[1024,4,512]{0,2,1:T(8,128)} %fusion.103), kind=kOutput, calls=%fused_computation.19 | convolution fusion | flops 8608808960 | bytes 29376512 | tf_op jit(solution)/shard_map/tef,td->efd/dot_general | solution.py:440
  482.6 14.1 %convert_bitcast_fusion.1 = bf16[4,2048,512]{1,2,0:T(8,128)(2,1)} fusion(bf16[1024,4,512]{0,2,1:T(8,128)(2,1)} %get-tuple-element.62, bf16[1024,2048]{1,0:T(8,128)(2,1)} %bitcast.261), kind=kOutput, calls=%fused_computation.12 | convolution fusion | flops 8594128896 | bytes 16777216 | tf_op jit(solution)/shard_map/td,tef->edf/dot_general | solution.py:440
  498.8 13.2 %fusion.105 = f32[1024,2048,1]{1,0,2:T(8,128)S(1)} fusion(bf16[1024,4,512]{0,2,1:T(8,128)(2,1)} %get-tuple-element.61, bf16[4,2048,512]{2,1,0:T(8,128)(2,1)} %all-gather.6.cloned.1.call-done), kind=kOutput, calls=%fused_computation.194 | convolution fusion | flops 8589934592 | bytes 20971520 | tf_op jit(solution)/shard_map/tef,edf->td/dot_general | solution.py:440
  512.1 12.9 %fusion.1 = bf16[1024,2048]{1,0:T(8,128)(2,1)} fusion(f32[1024,2048,1]{1,0,2:T(8,128)S(1)} %fusion.105, bf16[1024,4,512]{0,2,1:T(8,128)(2,1)S(1)} %copy-done.68, bf16[4,2048,512]{2,1,0:T(8,128)(2,1)} %all-gather.8.cloned.1.call-done), kind=kOutput, calls=%fused_computation.3 | convolution fusion | flops 8594128896 | bytes 25165824 | tf_op jit(solution)/shard_map/tef,edf->td/dot_general | solution.py:440
  525.0 55.5 %reduce_rows.1 = (f32[128,2048]{1,0:T(8,128)}, f32[16,128]{1,0:T(8,128)}) custom-call(bf16[8,128,2048]{2,1,0:T(8,128)(2,1)} %bitcast.281, f32[8,16,128]{2,1,0:T(8,128)} %bitcast_bitcast_fusion.1.note), custom_call_target="tpu_custom_call" | custom-call | bytes 200000000 | tf_op jit(solution)/shard_map/reduce_rows/pallas_call | solution.py:272
  585.9 49.4 %gather_rows.5 = bf16[8,128,2048]{2,1,0:T(8,128)(2,1)} custom-call(bf16[128,2048]{1,0:T(8,128)(2,1)} %fusion.95.refs_0_), custom_call_target="tpu_custom_call" | custom-call | bytes 200000000 | tf_op jit(solution)/shard_map/gather_rows/pallas_call | solution.py:153
  635.3 31.4 %reduce-scatter.11.cloned.1.call-done = bf16[1,2048,512]{1,2,0:T(8,128)(2,1)} async-done(((bf16[4,2048,512]{1,2,0:T(8,128)(2,1)}), bf16[1,2048,512]{1,2,0:T(8,128)(2,1)}) %reduce-scatter.11.cloned.1.call-update) | async-done | bytes 2097168 | tf_op jit(solution)/shard_map/reduce_scatter | solution.py:570
  682.8 6.4 convolution_convert_fusion.3
  691.3 6.1 fusion.106
  697.4 15.8 %fusion.37 = f32[1024,2,128]{2,0,1:T(8,128)} fusion(f32[2,1024,1024]{1,2,0:T(8,128)} %fusion.106, f32[2,1024,1024]{1,2,0:T(8,128)} %copy-done.14, f32[2,1024]{1,0:T(2,128)S(1)} %copy-done.56, pred[1024,1024]{0,1:T(8,128)(4,1)S(1)} %copy-done.20, bf16[1024,2,64]{2,0,1:T(8,128)(2,1)S(1)} %copy-done.27, bf16[1024,2,64]{2,0,1:T(8,128)(2,1)S(1)} %copy-done.29), kind=kOutput, calls=%fused_computation.59 | convolution fusion | flops 560991232 | bytes 19406848 | tf_op jit(solution)/shard_map/hqk,khd->qhd/dot_general | solution.py:440
  713.2 15.2 %fusion.40 = f32[1024,2,128]{2,0,1:T(8,128)} fusion(f32[2,1024,1024]{1,2,0:T(8,128)} %fusion.106, f32[2,1024,1024]{1,2,0:T(8,128)} %copy-done.14, f32[2,1024]{1,0:T(2,128)S(1)} %copy-done.56, pred[1024,1024]{0,1:T(8,128)(4,1)S(1)} %copy-done.20, bf16[1024,2,64]{2,0,1:T(8,128)(2,1)} %copy-done.25, bf16[1024,2,64]{2,0,1:T(8,128)(2,1)} %copy-done.24), kind=kOutput, calls=%fused_computation.60 | convolution fusion | flops 560991232 | bytes 19406848 | tf_op jit(solution)/shard_map/hqk,qhd->khd/dot_general | solution.py:440
  749.4 23.9 %small_sum.4 = f32[16,128]{1,0:T(8,128)} custom-call(f32[16,128]{1,0:T(8,128)} %reshape.452.values), custom_call_target="tpu_custom_call" | custom-call | bytes 10000000 | tf_op jit(solution)/shard_map/small_sum/pallas_call | solution.py:391
  780.8 30.6 %swap.3 = (bf16[128,2048]{1,0:T(8,128)(2,1)}, bf16[128,2048]{1,0:T(8,128)(2,1)}, bf16[128,2048]{1,0:T(8,128)(2,1)}) custom-call(bf16[8,128,256]{2,1,0:T(8,128)(2,1)} %bitcast.286, bf16[8,128,256]{2,1,0:T(8,128)(2,1)} %bitcast.285, bf16[8,128,256]{2,1,0:T(8,128)(2,1)} %copy.311.refs_2_), custom_call_target="tpu_custom_call" | custom-call | bytes 30000000 | tf_op jit(solution)/shard_map/swap/pallas_call | solution.py:339
  811.5 6.0 convolution_convert_fusion.1
  822.5 14.1 %all-to-all-start.5 = ((bf16[8,512,256]{2,1,0:T(8,128)(2,1)}), bf16[8,512,256]{2,1,0:T(8,128)(2,1)}, u32[]{:S(2)}, u32[]{:S(2)}) async-start(bf16[8,512,256]{2,1,0:T(8,128)(2,1)} %bitcast.271), calls=%async_computation.11 | async-start | bytes 4194304 | tf_op jit(solution)/shard_map/all_to_all | solution.py:485
  841.1 6.4 fusion.107
  847.5 6.4 convolution_add_fusion.2
  859.1 31.1 %small_sum.5 = f32[16,128]{1,0:T(8,128)} custom-call(f32[32,16,128]{2,1,0:T(8,128)} %bitcast.297), custom_call_target="tpu_custom_call" | custom-call | bytes 10000000 | tf_op jit(solution)/shard_map/small_sum/pallas_call | solution.py:391
  925.3 13.2 %all-to-all-done.4 = bf16[8,64,768]{2,1,0:T(8,128)(2,1)} async-done(((bf16[8,64,768]{2,1,0:T(8,128)(2,1)}), bf16[8,64,768]{2,1,0:T(8,128)(2,1)}, u32[]{:S(2)}, u32[]{:S(2)}) %all-to-all-start.4) | async-done | bytes 786464 | tf_op jit(solution)/shard_map/all_to_all | solution.py:485
  (304 shorter events, 189.6 us)
Async XLA Ops:
  7.2 331.9 %copy-start = (bf16[2048,16]{0,1:T(8,128)(2,1)S(1)}, bf16[2048,16]{0,1:T(8,128)(2,1)}, u32[]{:S(2)}) copy-start(bf16[2048,16]{0,1:T(8,128)(2,1)} %param.28) | copy-start | bytes 196612
  11.5 152.9 %all-to-all-start = ((bf16[8,256,512]{1,2,0:T(8,128)(2,1)}), bf16[8,256,512]{1,2,0:T(8,128)(2,1)}, u32[]{:S(2)}, u32[]{:S(2)}) async-start(bf16[8,256,512]{1,2,0:T(8,128)(2,1)} %copy.256), calls=%async_computation | async-start | bytes 4194304 | tf_op jit(solution)/shard_map/all_to_all | solution.py:485
  19.6 142.0 %copy-start.49 = (f32[256]{0:T(256)}, f32[256]{0:T(256)S(1)}, u32[]{:S(2)}) copy-start(f32[256]{0:T(256)S(1)} %dynamic_slice.25) | copy-start | bytes 3076
  20.4 142.7 %copy-start.51 = (f32[256]{0:T(256)}, f32[256]{0:T(256)S(1)}, u32[]{:S(2)}) copy-start(f32[256]{0:T(256)S(1)} %dynamic_slice.26) | copy-start | bytes 3076
  21.2 116.3 %copy-start.62 = (f32[128]{0:T(128)}, f32[128]{0:T(128)S(1)}, u32[]{:S(2)}) copy-start(f32[128]{0:T(128)S(1)} %fusion.50) | copy-start | bytes 1540
  21.2 123.2 %copy-start.57 = (f32[128]{0:T(128)}, f32[128]{0:T(128)S(1)}, u32[]{:S(2)}) copy-start(f32[128]{0:T(128)S(1)} %fusion.79) | copy-start | bytes 1540
  141.5 21.9 %copy-start.8 = (f32[1024,256]{0,1:T(8,128)}, f32[1024,256]{0,1:T(8,128)S(1)}, u32[]{:S(2)}) copy-start(f32[1024,256]{0,1:T(8,128)S(1)} %get-tuple-element.136) | copy-start | bytes 3145732
  144.4 30.1 %copy-start.6 = (f32[1024,256]{0,1:T(8,128)}, f32[1024,256]{0,1:T(8,128)S(1)}, u32[]{:S(2)}) copy-start(f32[1024,256]{0,1:T(8,128)S(1)} %get-tuple-element.138) | copy-start | bytes 3145732
  144.4 25.0 %copy-start.37 = (f32[8,17,128]{2,1,0:T(8,128)S(1)}, f32[8,17,128]{2,1,0:T(8,128)}, u32[]{:S(2)}) copy-start(f32[8,17,128]{2,1,0:T(8,128)} %get-tuple-element.51) | copy-start | bytes 208900
  164.4 51.5 %all-to-all-start.1 = ((bf16[8,512,256]{2,1,0:T(8,128)(2,1)}), bf16[8,512,256]{2,1,0:T(8,128)(2,1)}, u32[]{:S(2)}, u32[]{:S(2)}) async-start(bf16[8,512,256]{2,1,0:T(8,128)(2,1)} %bitcast.287), calls=%async_computation.1 | async-start | bytes 4194304 | tf_op jit(solution)/shard_map/all_to_all | solution.py:485
  169.2 167.4 %all-gather.4.cloned.1.call-start = ((), (), s32[]{:S(2)}) async-start(), calls=%async_computation.12 | async-start | bytes 10485760 | tf_op jit(solution)/shard_map/all_gather | solution.py:488
  193.1 32.6 %copy-start.34 = (bf16[2,128,1024]{2,1,0:T(8,128)(2,1)}, bf16[2,128,1024]{2,1,0:T(8,128)(2,1)S(1)}, u32[]{:S(2)}) copy-start(bf16[2,128,1024]{2,1,0:T(8,128)(2,1)S(1)} %convolution_convert_fusion.4) | copy-start | bytes 1572868
  221.2 121.4 %all-gather.6.cloned.1.call-start = ((), (), s32[]{:S(2)}) async-start(), calls=%async_computation.13 | async-start | bytes 10485760 | tf_op jit(solution)/shard_map/all_gather | solution.py:488
  242.6 93.9 %all-to-all-start.2 = ((bf16[8,256,512]{1,2,0:T(8,128)(2,1)}), bf16[8,256,512]{1,2,0:T(8,128)(2,1)S(1)}, u32[]{:S(2)}, u32[]{:S(2)}) async-start(bf16[8,256,512]{1,2,0:T(8,128)(2,1)} %copy.263), calls=%async_computation.2 | async-start | bytes 4194304 | tf_op jit(solution)/shard_map/all_to_all | solution.py:485
  250.3 149.2 %all-gather.8.cloned.1.call-start = ((), (), s32[]{:S(2)}) async-start(), calls=%async_computation.14 | async-start | bytes 10485760 | tf_op jit(solution)/shard_map/all_gather | solution.py:488
  256.0 86.4 %copy-start.53 = (f32[128]{0:T(128)}, f32[128]{0:T(128)S(1)}, u32[]{:S(2)}) copy-start(f32[128]{0:T(128)S(1)} %fusion.80) | copy-start | bytes 1540
  339.0 186.0 %reduce-scatter.7.cloned.1.call-start = ((), (), s32[]{:S(2)}) async-start(), calls=%async_computation.15 | async-start | bytes 4718592 | tf_op jit(solution)/shard_map/reduce_scatter | solution.py:552
  430.9 204.4 %reduce-scatter.9.cloned.1.call-start = ((), (), s32[]{:S(2)}) async-start(), calls=%async_computation.16 | async-start | bytes 10485760 | tf_op jit(solution)/shard_map/reduce_scatter | solution.py:570
  431.0 21.8 %copy-start.3 = (bf16[8,128,2048]{2,1,0:T(8,128)(2,1)S(1)}, bf16[8,128,2048]{2,1,0:T(8,128)(2,1)}, u32[]{:S(2)}) copy-start(bf16[8,128,2048]{2,1,0:T(8,128)(2,1)} %gather_rows.4) | copy-start | bytes 12582916
  466.2 200.5 %reduce-scatter.11.cloned.1.call-start = ((), (), s32[]{:S(2)}) async-start(), calls=%async_computation.17 | async-start | bytes 10485760 | tf_op jit(solution)/shard_map/reduce_scatter | solution.py:570
  496.7 314.8 %reduce-scatter.13.cloned.1.call-start = ((), (), s32[]{:S(2)}) async-start(), calls=%async_computation.18 | async-start | bytes 10485760 | tf_op jit(solution)/shard_map/reduce_scatter | solution.py:570
  512.0 69.9 %copy-start.2 = (f32[128,2048]{1,0:T(8,128)S(1)}, f32[128,2048]{1,0:T(8,128)}, u32[]{:S(2)}) copy-start(f32[128,2048]{1,0:T(8,128)} %copy-done.1) | copy-start | bytes 3145732
  512.0 69.9 %copy-start.40 = (f32[2048]{0:T(1024)S(1)}, f32[2048]{0:T(1024)}, u32[]{:S(2)}) copy-start(f32[2048]{0:T(1024)} %param.27) | copy-start | bytes 24580
  512.0 69.9 %copy-start.54 = (f32[128]{0:T(128)S(1)}, f32[128]{0:T(128)}, u32[]{:S(2)}) copy-start(f32[128]{0:T(128)} %copy-done.53) | copy-start | bytes 1540
  512.0 71.7 %copy-start.61 = (f32[128]{0:T(128)S(1)}, f32[128]{0:T(128)}, u32[]{:S(2)}) copy-start(f32[128]{0:T(128)} %copy-done.60) | copy-start | bytes 1540
  512.1 72.7 %copy-start.17 = (bf16[1,128,2048]{2,1,0:T(8,128)(2,1)S(1)}, bf16[1,128,2048]{2,1,0:T(8,128)(2,1)}, u32[]{:S(2)}) copy-start(bf16[1,128,2048]{2,1,0:T(8,128)(2,1)} %param.19) | copy-start | bytes 1572868
  671.8 139.6 %all-to-all-start.3 = ((bf16[8,256,1024]{1,2,0:T(8,128)(2,1)}), bf16[8,256,1024]{1,2,0:T(8,128)(2,1)}, u32[]{:S(2)}, u32[]{:S(2)}) async-start(bf16[8,256,1024]{1,2,0:T(8,128)(2,1)} %bitcast.263), calls=%async_computation.6 | async-start | bytes 8388608 | tf_op jit(solution)/shard_map/all_to_all | solution.py:485
  677.5 161.8 %reduce-scatter.17.cloned.1.call-start = ((), (), s32[]{:S(2)}) async-start(), calls=%async_computation.20 | async-start | bytes 1310720 | tf_op jit(solution)/shard_map/reduce_scatter | solution.py:626
  746.6 166.8 %reduce-scatter.15.cloned.1.call-start = ((), (), s32[]{:S(2)}) async-start(), calls=%async_computation.19 | async-start | bytes 3932160 | tf_op jit(solution)/shard_map/reduce_scatter | solution.py:570
  822.5 25.0 %copy-start.36 = (bf16[128,2048]{1,0:T(8,128)(2,1)S(1)}, bf16[128,2048]{1,0:T(8,128)(2,1)}, u32[]{:S(2)}) copy-start(bf16[128,2048]{1,0:T(8,128)(2,1)} %get-tuple-element.75) | copy-start | bytes 1572868
  822.5 90.9 %all-to-all-start.5 = ((bf16[8,512,256]{2,1,0:T(8,128)(2,1)}), bf16[8,512,256]{2,1,0:T(8,128)(2,1)}, u32[]{:S(2)}, u32[]{:S(2)}) async-start(bf16[8,512,256]{2,1,0:T(8,128)(2,1)} %bitcast.271), calls=%async_computation.11 | async-start | bytes 4194304 | tf_op jit(solution)/shard_map/all_to_all | solution.py:485
  913.4 25.1 %all-to-all-start.4 = ((bf16[8,64,768]{2,1,0:T(8,128)(2,1)}), bf16[8,64,768]{2,1,0:T(8,128)(2,1)}, u32[]{:S(2)}, u32[]{:S(2)}) async-start(bf16[8,64,768]{2,1,0:T(8,128)(2,1)} %bitcast.298), calls=%async_computation.9 | async-start | bytes 1572864 | tf_op jit(solution)/shard_map/all_to_all | solution.py:485
  (54 other events, 472.8 us)
Sparse Core Ops, SparseCore 0:
  221.3 57.1 all-gather.3
  280.7 58.2 all-gather.5
  341.1 58.2 all-gather.7
  431.0 88.2 reduce-scatter.6
  521.8 71.0 reduce-scatter.8
  595.3 71.3 reduce-scatter.10
  669.3 71.3 reduce-scatter.12
  746.7 25.3 reduce-scatter.16
  819.5 46.3 reduce-scatter.14

commit v5 on v4

--- a/solution.py
+++ b/solution.py
@@ -495,7 +495,7 @@
     expert_ids = jnp.arange(experts, dtype=jnp.int32)
     marks = jnp.any(routing[0][:, :, None] == expert_ids[None, None, :], axis=1).astype(F32)
     marks = jnp.concatenate([marks.T, segment_ids[0].astype(F32)[None]], axis=0)
-    normed_all, grad_all, marks = gather_rows([normed_b, out_grad[0]], groups, 1, note=marks)
+    normed_all, marks = gather_rows([normed_b], groups, 1, note=marks)
     marks = marks.transpose(1, 0, 2).reshape(experts + 1, length)
     chosen, seg_all = marks[:experts].T > 0.5, marks[experts]
     down_in = w_down.reshape(groups, part, cols)
@@ -537,8 +537,10 @@
     resid = inputs + mm(mixed_b, w_out)
     normed_mlp_b = rms_norm(resid, mlp_gain).astype(BF16)
     (mlp_all,) = gather_rows([normed_mlp_b], groups, 4)
-    up_own, down_w, mlp_late = together((up_own, down_w, mlp_all))
+    up_own, down_w, mlp_late, grad_in = together((up_own, down_w, mlp_all, out_grad[0]))
     up_w = row_of_devices(up_own.reshape(width, part))
+    (grad_all,) = gather_rows([grad_in], groups, 10)
+    up_w, grad_all = together((up_w, grad_all))
 
     router_all = jax.nn.softmax(mm(mlp_all, w_router), axis=-1)
     picked = jnp.where(chosen, router_all, 0.0).reshape(length, sources, local_experts)
@@ -592,17 +594,19 @@
     resid_grad = grad_out + resid_part
     attn_grad_b = resid_grad.astype(BF16)
     (attn_grad_all,) = gather_rows([attn_grad_b], groups, 6)
-    gate_sum, up_sum, attn_grad_late = together((gate_sum, up_sum, attn_grad_all))
-    gate_up_sum = jnp.concatenate([gate_sum, up_sum], axis=1).reshape(groups, cols, 2 * part)
-    gate_up_sum = exchange(gate_up_sum)
+    gate_sum, attn_grad_late = together((gate_sum, attn_grad_all))
+    gate_sum = exchange(gate_sum.reshape(groups, cols, part))
     mixed_grad_c = mm_nt(attn_grad_all, own_cols(w_out, 0)).astype(BF16)
     mixed_grad_c = mixed_grad_c.reshape(length, heads, head_dim)
 
     prob_grad = ein("qhd,khd->hqk", mixed_grad_c, values_b)
     delta = jnp.sum(probs * prob_grad, axis=-1, keepdims=True)
     score_grad_b = (probs * (prob_grad - delta) * score_scale).astype(BF16)
+    score_grad_b, probs_b = together((score_grad_b, probs_b))
     query_grad = ein("hqk,khd->qhd", score_grad_b, keys_b)
     key_grad = ein("hqk,qhd->khd", score_grad_b, queries_b)
+    gate_sum, up_sum, query_grad, key_grad = together((gate_sum, up_sum, query_grad, key_grad))
+    up_sum = exchange(up_sum.reshape(groups, cols, part))
     value_grad_b = ein("hqk,qhd->khd", probs_b, mixed_grad_c).astype(BF16).reshape(length, cols)
 
     def unturned(grad):
@@ -618,8 +622,8 @@
     query_gain_part = jnp.sum(query_turn * query_raw * query_scale, axis=0)
     key_gain_part = jnp.sum(key_turn * key_raw * key_scale, axis=0)
     raw_grads = [query_raw_b, key_raw_b, value_grad_b]
-    (query_own, key_own, value_own), raw_grads, gate_up_sum, down_sum = together(
-        (swap(raw_grads, groups, False, 8), raw_grads, gate_up_sum, down_sum)
+    (query_own, key_own, value_own), raw_grads, up_sum, down_sum = together(
+        (swap(raw_grads, groups, False, 8), raw_grads, up_sum, down_sum)
     )
     down_sum = exchange(down_sum.reshape(part, groups, cols).transpose(1, 0, 2))
     out_w_part = mm_tn(mixed_c, attn_grad_late).astype(BF16)
@@ -627,8 +631,6 @@
     qkv_part = mm_tn(normed_late, jnp.concatenate(raw_grads, axis=1)).astype(BF16)
     qkv_part = qkv_part.reshape(groups, sources, -1, 3 * cols).transpose(1, 0, 2, 3)
     qkv_part = over_row(qkv_part.reshape(sources, -1, 3 * cols)).reshape(groups, -1, 3 * cols)
-    qkv_part = exchange(qkv_part)
-    qkv_part = qkv_part.transpose(1, 0, 2).reshape(-1, groups, 3, cols).astype(F32)
     normed_grad = mm_nt(query_own, w_query) + mm_nt(key_own, w_key) + mm_nt(value_own, w_value)
     _, attn_back = jax.vjp(rms_norm, inputs, attn_gain)
     input_part, attn_gain_grad = attn_back(normed_grad)
@@ -642,6 +644,9 @@
     small = small.reshape(-1, devices, width // devices).transpose(1, 0, 2).reshape(devices, -1)
     used = small.shape[1]
     small = jnp.pad(small, ((0, 0), (0, -used % 1024))).reshape(devices, -1, 128)
+    small, qkv_part, down_sum = together((small, qkv_part, down_sum))
+    qkv_part = exchange(qkv_part)
+    qkv_part = qkv_part.transpose(1, 0, 2).reshape(-1, groups, 3, cols).astype(F32)
     small = small_sum(small, ("group", "expert"), True, 9).reshape(-1)[:used]
     small = small.reshape(-1, width // devices)
     return (
@@ -656,8 +661,8 @@
         out_w_grad.astype(F32),
         small[experts],
         small[:experts].T,
-        slices_out(gate_up_sum[:, :, :part]),
-        slices_out(gate_up_sum[:, :, part:]),
+        slices_out(gate_sum),
+        slices_out(up_sum),
         down_sum.reshape(local_experts, hidden_size, cols).astype(F32),
     )
 

time: 966 us -> 895 us (0.927)
  waiting for transfers between devices: 110 us -> 44.6 us
  matrix products: 239 us -> 222 us
    all_gather x3, waiting for transfers between devices: 42.2 us -> 0.06 us  [row_of_devices(): return lax.all_gather(w, 'expert', axis=0, tiled=False)]
    dot_general x15 -> x14, matrix products: 186 us -> 154 us  [ein(): return jnp.einsum(spec, *ops, preferred_element_type=F32)]
    reduce_scatter x4, waiting for transfers between devices: 31.5 us -> 0.04 us  [over_row(): return lax.psum_scatter(w, 'expert', scatter_dimension=0, tiled=False)]
    pallas_call x3 -> x4, Pallas kernels: 244 us -> 263 us  [gather_rows(): pl.pallas_call(functools.partial(gather_kernel, nz, groups // nz, pieces,...]
    sub x0 -> x1, matrix products: none -> 14.3 us  [shards(): score_grad_b = (probs * (prob_grad - delta) * score_scale).astype(BF16)]
    pallas_call x3, Pallas kernels: 70.9 us -> 56.8 us  [small_sum(): pl.pallas_call(functools.partial(small_sum_kernel, axes, scatter), name='...]
    all_to_all x6 -> x7, waiting for transfers between devices: 36 us -> 43.8 us  [exchange(): return lax.all_to_all(w, 'group', 0, 0, tiled=True)]
    all_to_all x6 -> x7, starting transfers between devices: 43.8 us -> 47.2 us  [exchange(): return lax.all_to_all(w, 'group', 0, 0, tiled=True)]
  transfers between devices with their start and end apart: 15 -> 16, of which waited for: 4 -> 3; matrix products, arithmetic and copies ran while one was open for 33% -> 34% of each run, Pallas kernels for 43% -> 47%
where the time goes in v5:
time: 895 us; the launch traced here: 887 us
  Pallas kernels  419 us (47%)
  matrix products  222 us (25%)
  local copies, waits for them, and re-layouts  82.8 us (9%)
  other arithmetic  54.9 us (6%)
  starting transfers between devices  49.3 us (6%)
  waiting for transfers between devices  44.6 us (5%)
  between operations  15.5 us (2%)
    pallas_call x4, Pallas kernels, gather_rows(): pl.pallas_call(functools.partial(gather_kernel, nz, groups // nz, pieces,...  263 us
    dot_general x14, matrix products, ein(): return jnp.einsum(spec, *ops, preferred_element_type=F32)  154 us
    pallas_call x3, Pallas kernels, small_sum(): pl.pallas_call(functools.partial(small_sum_kernel, axes, scatter), name='...  56.8 us
    pallas_call x1, Pallas kernels, reduce_rows(): pl.pallas_call(functools.partial(reduce_kernel, nz, ny, pieces), name='re...  54.5 us
    all_to_all x7, starting transfers between devices, exchange(): return lax.all_to_all(w, 'group', 0, 0, tiled=True)  47.2 us
    pallas_call x2, Pallas kernels, swap(): pl.pallas_call(functools.partial(swap_kernel, groups, to_rows), name='swa...  44.3 us
    all_to_all x7, waiting for transfers between devices, exchange(): return lax.all_to_all(w, 'group', 0, 0, tiled=True)  43.8 us
    dot_general x5, matrix products, mm_nt(): lax.dot_general(left, right, (((1,), (1,)), ((), ())), preferred_element_...  23.3 us
  transfers between devices with their start and end apart: 16, of which 3 were waited for; matrix products, arithmetic and copies ran while one was open for 34% of the time, Pallas kernels for 47%

profile of v5, /device:TPU:0, one launch (start us, length us, event | category | flops | bytes accessed | tf_op | source)
XLA Modules:
  0.0 887.3 jit_solution(16065765623659301656)
XLA Ops:
  11.5 7.3 all-to-all-start
  22.2 86.2 %gather_rows.4 = (bf16[8,128,2048]{2,1,0:T(8,128)(2,1)}, f32[8,17,128]{2,1,0:T(8,128)}) custom-call(bf16[128,2048]{1,0:T(8,128)(2,1)} %fusion.24.refs_0_, f32[17,128]{1,0:T(8,128)} %pad_maximum_fusion.10.refs_1_), custom_call_target="tpu_custom_call" | custom-call | bytes 200000000 | tf_op jit(solution)/shard_map/gather_rows/pallas_call | solution.py:153
  116.0 10.2 %small_sum.3 = f32[16,128]{1,0:T(8,128)} custom-call(f32[16,128]{1,0:T(8,128)} %reshape.442.values), custom_call_target="tpu_custom_call" | custom-call | bytes 10000000 | tf_op jit(solution)/shard_map/small_sum/pallas_call | solution.py:391
  163.8 20.6 %all-to-all-done.1 = bf16[8,512,256]{2,1,0:T(8,128)(2,1)} async-done(((bf16[8,512,256]{2,1,0:T(8,128)(2,1)}), bf16[8,512,256]{2,1,0:T(8,128)(2,1)}, u32[]{:S(2)}, u32[]{:S(2)}) %all-to-all-start.1) | async-done | bytes 2097184 | tf_op jit(solution)/shard_map/all_to_all | solution.py:485
  196.5 13.5 %swap.2 = bf16[128,2048]{1,0:T(8,128)(2,1)} custom-call(bf16[8,128,256]{2,1,0:T(8,128)(2,1)} %bitcast.307), custom_call_target="tpu_custom_call" | custom-call | bytes 30000000 | tf_op jit(solution)/shard_map/swap/pallas_call | solution.py:339
  210.1 7.7 all-to-all-start.2
  224.8 79.3 %gather_rows.5 = bf16[8,128,2048]{2,1,0:T(8,128)(2,1)} custom-call(bf16[128,2048]{1,0:T(8,128)(2,1)} %multiply_convert_fusion.6.refs_0_), custom_call_target="tpu_custom_call" | custom-call | bytes 200000000 | tf_op jit(solution)/shard_map/gather_rows/pallas_call | solution.py:153
  309.2 14.6 %fusion.73 = f32[1024,4,512]{0,2,1:T(8,128)} fusion(bf16[1024,2048,1]{1,0,2:T(8,128)(2,1)} %bitcast.272, bf16[4,2048,512]{2,1,0:T(8,128)(2,1)} %all-gather.8.cloned.1.call-done), kind=kOutput, calls=%fused_computation.185 | convolution fusion | flops 8589934592 | bytes 20971520 | tf_op jit(solution)/shard_map/td,edf->tef/dot_general | solution.py:440
  323.9 49.6 %gather_rows.6 = bf16[8,128,2048]{2,1,0:T(8,128)(2,1)} custom-call(bf16[128,2048]{1,0:T(8,128)(2,1)} %bitcast.288), custom_call_target="tpu_custom_call" | custom-call | bytes 200000000 | tf_op jit(solution)/shard_map/gather_rows/pallas_call | solution.py:153
  373.5 14.8 %fusion.74 = f32[1024,4,512]{0,2,1:T(8,128)} fusion(bf16[1024,2048,1]{1,0,2:T(8,128)(2,1)} %bitcast.273, bf16[4,2048,512]{2,1,0:T(8,128)(2,1)} %all-gather.6.cloned.1.call-done), kind=kOutput, calls=%fused_computation.186 | convolution fusion | flops 8589934592 | bytes 20971520 | tf_op jit(solution)/shard_map/td,edf->tef/dot_general | solution.py:440
  388.3 16.7 %bitcast_convert_fusion = bf16[1024,2048]{1,0:T(8,128)(2,1)} fusion(bf16[4,512,2048]{2,1,0:T(8,128)(2,1)} %all-gather.4.cloned.1.call-done, f32[1024,4]{0,1:T(4,128)S(1)} %bitcast.329, f32[1024,4,512]{0,2,1:T(8,128)} %fusion.74, f32[1024,4,512]{0,2,1:T(8,128)S(1)} %copy-done.67), kind=kOutput, calls=%fused_computation.1 | convolution fusion | flops 8606711808 | bytes 29376512 | tf_op jit(solution)/shard_map/tef,efd->td/dot_general | solution.py:440
  405.3 21.8 %multiply_reduce_fusion.1 = (f32[1024,4]{0,1:T(4,128)S(1)}, bf16[1024,4,512]{0,2,1:T(8,128)(2,1)}, bf16[1024,4,512]{0,2,1:T(8,128)(2,1)}) fusion(f32[1024,4,512]{0,2,1:T(8,128)} %fusion.74, f32[1024,4,512]{0,2,1:T(8,128)} %fusion.73, f32[1024,4]{0,1:T(4,128)S(1)} %bitcast.330, bf16[4,512,2048]{2,1,0:T(8,128)(2,1)} %all-gather.4.cloned.1.call-done, ...), kind=kOutput, calls=%fused_computation.8 | convolution fusion | flops 8627679232 | bytes 37781504 | tf_op jit(solution)/shard_map/td,efd->tef/dot_general | solution.py:440
  427.1 13.4 %convert_bitcast_fusion = bf16[4,2048,512]{1,2,0:T(8,128)(2,1)} fusion(bf16[1024,4,512]{0,2,1:T(8,128)(2,1)} %get-tuple-element.73, bf16[1024,2048]{1,0:T(8,128)(2,1)S(1)} %bitcast.275), kind=kOutput, calls=%fused_computation.7 | convolution fusion | flops 8594128896 | bytes 16777216 | tf_op jit(solution)/shard_map/td,tef->edf/dot_general | solution.py:440
  441.1 16.2 %convolution_convert_fusion = bf16[4,512,2048]{2,1,0:T(8,128)(2,1)} fusion(bf16[1024,2048]{1,0:T(8,128)(2,1)} %bitcast.292, f32[1024,4]{0,1:T(4,128)S(1)} %bitcast.331, f32[1024,4,512]{0,2,1:T(8,128)} %fusion.74, f32[1024,4,512]{0,2,1:T(8,128)} %fusion.73), kind=kOutput, calls=%fused_computation.19 | convolution fusion | flops 8608808960 | bytes 29376512 | tf_op jit(solution)/shard_map/tef,td->efd/dot_general | solution.py:440
  457.3 14.2 %convert_bitcast_fusion.1 = bf16[4,2048,512]{1,2,0:T(8,128)(2,1)} fusion(bf16[1024,4,512]{0,2,1:T(8,128)(2,1)} %get-tuple-element.74, bf16[1024,2048]{1,0:T(8,128)(2,1)} %bitcast.274), kind=kOutput, calls=%fused_computation.12 | convolution fusion | flops 8594128896 | bytes 16777216 | tf_op jit(solution)/shard_map/td,tef->edf/dot_general | solution.py:440
  473.5 13.1 %fusion.75 = f32[1024,2048,1]{1,0,2:T(8,128)S(1)} fusion(bf16[1024,4,512]{0,2,1:T(8,128)(2,1)} %get-tuple-element.73, bf16[4,2048,512]{2,1,0:T(8,128)(2,1)} %all-gather.8.cloned.1.call-done), kind=kOutput, calls=%fused_computation.187 | convolution fusion | flops 8589934592 | bytes 20971520 | tf_op jit(solution)/shard_map/tef,edf->td/dot_general | solution.py:440
  486.7 12.9 %fusion.1 = bf16[1024,2048]{1,0:T(8,128)(2,1)} fusion(f32[1024,2048,1]{1,0,2:T(8,128)S(1)} %fusion.75, bf16[1024,4,512]{0,2,1:T(8,128)(2,1)S(1)} %copy-done.68, bf16[4,2048,512]{2,1,0:T(8,128)(2,1)} %all-gather.6.cloned.1.call-done), kind=kOutput, calls=%fused_computation.3 | convolution fusion | flops 8594128896 | bytes 25165824 | tf_op jit(solution)/shard_map/tef,edf->td/dot_general | solution.py:440
  499.6 54.5 %reduce_rows.1 = (f32[128,2048]{1,0:T(8,128)}, f32[16,128]{1,0:T(8,128)}) custom-call(bf16[8,128,2048]{2,1,0:T(8,128)(2,1)} %bitcast.293, f32[8,16,128]{2,1,0:T(8,128)} %bitcast_bitcast_fusion.1.note), custom_call_target="tpu_custom_call" | custom-call | bytes 200000000 | tf_op jit(solution)/shard_map/reduce_rows/pallas_call | solution.py:272
  559.4 47.8 %gather_rows.7 = bf16[8,128,2048]{2,1,0:T(8,128)(2,1)} custom-call(bf16[128,2048]{1,0:T(8,128)(2,1)} %fusion.66.refs_0_), custom_call_target="tpu_custom_call" | custom-call | bytes 200000000 | tf_op jit(solution)/shard_map/gather_rows/pallas_call | solution.py:153
  619.4 14.3 %multiply_convert_fusion = bf16[2,1024,1024]{1,2,0:T(8,128)(2,1)} fusion(f32[2,1024,1024]{1,2,0:T(8,128)} %copy-done.2, f32[2,1024]{1,0:T(2,128)S(1)} %copy-done.50, pred[1024,1024]{0,1:T(8,128)(4,1)S(1)} %copy-done.9, bf16[1024,2,128]{0,2,1:T(8,128)(2,1)} %bitcast.317, bf16[1024,2,128]{0,2,1:T(8,128)(2,1)} %bitcast.316), kind=kOutput, calls=%fused_computation.4 | convolution fusion | flops 1096813568 | bytes 14688256 | tf_op jit(solution)/shard_map/sub | solution.py:604
  633.7 5.5 convolution_bitcast_fusion.1
  643.8 17.1 %all-to-all-done.3 = bf16[8,256,512]{1,2,0:T(8,128)(2,1)} async-done(((bf16[8,256,512]{1,2,0:T(8,128)(2,1)}), bf16[8,256,512]{1,2,0:T(8,128)(2,1)}, u32[]{:S(2)}, u32[]{:S(2)}) %all-to-all-start.3) | async-done | bytes 2097184 | tf_op jit(solution)/shard_map/all_to_all | solution.py:485
  696.0 22.9 %small_sum.4 = f32[16,128]{1,0:T(8,128)} custom-call(f32[16,128]{1,0:T(8,128)} %reshape.456.values), custom_call_target="tpu_custom_call" | custom-call | bytes 10000000 | tf_op jit(solution)/shard_map/small_sum/pallas_call | solution.py:391
  726.3 30.7 %swap.3 = (bf16[128,2048]{1,0:T(8,128)(2,1)}, bf16[128,2048]{1,0:T(8,128)(2,1)}, bf16[128,2048]{1,0:T(8,128)(2,1)}) custom-call(bf16[8,128,256]{2,1,0:T(8,128)(2,1)} %bitcast.302, bf16[8,128,256]{2,1,0:T(8,128)(2,1)} %bitcast.301, bf16[8,128,256]{2,1,0:T(8,128)(2,1)} %copy.306.refs_2_), custom_call_target="tpu_custom_call" | custom-call | bytes 30000000 | tf_op jit(solution)/shard_map/swap/pallas_call | solution.py:339
  757.1 6.0 convolution_convert_fusion.1
  768.1 14.2 %all-to-all-start.5 = ((bf16[8,512,256]{2,1,0:T(8,128)(2,1)}), bf16[8,512,256]{2,1,0:T(8,128)(2,1)}, u32[]{:S(2)}, u32[]{:S(2)}) async-start(bf16[8,512,256]{2,1,0:T(8,128)(2,1)} %bitcast.283), calls=%async_computation.10 | async-start | bytes 4194304 | tf_op jit(solution)/shard_map/all_to_all | solution.py:485
  790.7 5.4 copy.307
  796.2 6.4 fusion.76
  802.6 6.5 convolution_add_fusion.2
  818.3 5.3 copy.308
  823.6 6.0 all-to-all-done.5
  837.1 23.8 %small_sum.5 = f32[16,128]{1,0:T(8,128)} custom-call(f32[32,16,128]{2,1,0:T(8,128)} %bitcast.313), custom_call_target="tpu_custom_call" | custom-call | bytes 10000000 | tf_op jit(solution)/shard_map/small_sum/pallas_call | solution.py:391
  (305 shorter events, 193.2 us)
Async XLA Ops:
  7.2 298.4 %copy-start = (bf16[2048,16]{0,1:T(8,128)(2,1)S(1)}, bf16[2048,16]{0,1:T(8,128)(2,1)}, u32[]{:S(2)}) copy-start(bf16[2048,16]{0,1:T(8,128)(2,1)} %param.28) | copy-start | bytes 196612
  11.5 121.3 %all-to-all-start = ((bf16[8,256,512]{1,2,0:T(8,128)(2,1)}), bf16[8,256,512]{1,2,0:T(8,128)(2,1)}, u32[]{:S(2)}, u32[]{:S(2)}) async-start(bf16[8,256,512]{1,2,0:T(8,128)(2,1)} %copy.252), calls=%async_computation | async-start | bytes 4194304 | tf_op jit(solution)/shard_map/all_to_all | solution.py:485
  19.6 107.4 %copy-start.51 = (f32[256]{0:T(256)}, f32[256]{0:T(256)S(1)}, u32[]{:S(2)}) copy-start(f32[256]{0:T(256)S(1)} %dynamic_slice.25) | copy-start | bytes 3076
  20.4 111.3 %copy-start.53 = (f32[256]{0:T(256)}, f32[256]{0:T(256)S(1)}, u32[]{:S(2)}) copy-start(f32[256]{0:T(256)S(1)} %dynamic_slice.26) | copy-start | bytes 3076
  21.2 87.3 %copy-start.62 = (f32[128]{0:T(128)}, f32[128]{0:T(128)S(1)}, u32[]{:S(2)}) copy-start(f32[128]{0:T(128)S(1)} %fusion.29) | copy-start | bytes 1540
  21.2 94.2 %copy-start.57 = (f32[128]{0:T(128)}, f32[128]{0:T(128)S(1)}, u32[]{:S(2)}) copy-start(f32[128]{0:T(128)S(1)} %fusion.58) | copy-start | bytes 1540
  132.8 51.6 %all-to-all-start.1 = ((bf16[8,512,256]{2,1,0:T(8,128)(2,1)}), bf16[8,512,256]{2,1,0:T(8,128)(2,1)}, u32[]{:S(2)}, u32[]{:S(2)}) async-start(bf16[8,512,256]{2,1,0:T(8,128)(2,1)} %bitcast.303), calls=%async_computation.1 | async-start | bytes 4194304 | tf_op jit(solution)/shard_map/all_to_all | solution.py:485
  137.6 166.6 %all-gather.4.cloned.1.call-start = ((), (), s32[]{:S(2)}) async-start(), calls=%async_computation.13 | async-start | bytes 10485760 | tf_op jit(solution)/shard_map/all_gather | solution.py:488
  163.7 31.8 %copy-start.28 = (bf16[2,128,1024]{2,1,0:T(8,128)(2,1)}, bf16[2,128,1024]{2,1,0:T(8,128)(2,1)S(1)}, u32[]{:S(2)}) copy-start(bf16[2,128,1024]{2,1,0:T(8,128)(2,1)S(1)} %convolution_convert_fusion.4) | copy-start | bytes 1572868
  189.8 119.5 %all-gather.8.cloned.1.call-start = ((), (), s32[]{:S(2)}) async-start(), calls=%async_computation.15 | async-start | bytes 10485760 | tf_op jit(solution)/shard_map/all_gather | solution.py:488
  210.1 94.1 %all-to-all-start.2 = ((bf16[8,256,512]{2,1,0:T(8,128)(2,1)}), bf16[8,256,512]{2,1,0:T(8,128)(2,1)S(1)}, u32[]{:S(2)}, u32[]{:S(2)}) async-start(bf16[8,256,512]{2,1,0:T(8,128)(2,1)} %bitcast.285), calls=%async_computation.2 | async-start | bytes 4194304 | tf_op jit(solution)/shard_map/all_to_all | solution.py:485
  217.8 155.7 %all-gather.6.cloned.1.call-start = ((), (), s32[]{:S(2)}) async-start(), calls=%async_computation.14 | async-start | bytes 10485760 | tf_op jit(solution)/shard_map/all_gather | solution.py:488
  222.9 101.0 %copy-start.60 = (f32[128]{0:T(128)}, f32[128]{0:T(128)S(1)}, u32[]{:S(2)}) copy-start(f32[128]{0:T(128)S(1)} %get-tuple-element.159) | copy-start | bytes 1540
  222.9 100.9 %copy-start.55 = (f32[128]{0:T(128)}, f32[128]{0:T(128)S(1)}, u32[]{:S(2)}) copy-start(f32[128]{0:T(128)S(1)} %fusion.59) | copy-start | bytes 1540
  305.5 194.1 %reduce-scatter.7.cloned.1.call-start = ((), (), s32[]{:S(2)}) async-start(), calls=%async_computation.16 | async-start | bytes 4718592 | tf_op jit(solution)/shard_map/reduce_scatter | solution.py:554
  405.0 202.3 %reduce-scatter.9.cloned.1.call-start = ((), (), s32[]{:S(2)}) async-start(), calls=%async_computation.17 | async-start | bytes 10485760 | tf_op jit(solution)/shard_map/reduce_scatter | solution.py:572
  440.6 203.2 %reduce-scatter.11.cloned.1.call-start = ((), (), s32[]{:S(2)}) async-start(), calls=%async_computation.18 | async-start | bytes 10485760 | tf_op jit(solution)/shard_map/reduce_scatter | solution.py:572
  471.4 285.7 %reduce-scatter.13.cloned.1.call-start = ((), (), s32[]{:S(2)}) async-start(), calls=%async_computation.19 | async-start | bytes 10485760 | tf_op jit(solution)/shard_map/reduce_scatter | solution.py:572
  486.6 68.9 %copy-start.4 = (f32[128,2048]{1,0:T(8,128)S(1)}, f32[128,2048]{1,0:T(8,128)}, u32[]{:S(2)}) copy-start(f32[128,2048]{1,0:T(8,128)} %copy-done.3) | copy-start | bytes 3145732
  486.6 68.9 %copy-start.40 = (f32[2048]{0:T(1024)S(1)}, f32[2048]{0:T(1024)}, u32[]{:S(2)}) copy-start(f32[2048]{0:T(1024)} %param.27) | copy-start | bytes 24580
  486.6 68.9 %copy-start.56 = (f32[128]{0:T(128)S(1)}, f32[128]{0:T(128)}, u32[]{:S(2)}) copy-start(f32[128]{0:T(128)} %copy-done.55) | copy-start | bytes 1540
  486.7 70.6 %copy-start.61 = (f32[128]{0:T(128)S(1)}, f32[128]{0:T(128)}, u32[]{:S(2)}) copy-start(f32[128]{0:T(128)} %copy-done.60) | copy-start | bytes 1540
  486.7 71.6 %copy-start.20 = (bf16[1,128,2048]{2,1,0:T(8,128)(2,1)S(1)}, bf16[1,128,2048]{2,1,0:T(8,128)(2,1)}, u32[]{:S(2)}) copy-start(bf16[1,128,2048]{2,1,0:T(8,128)(2,1)} %param.19) | copy-start | bytes 1572868
  610.4 50.5 %all-to-all-start.3 = ((bf16[8,256,512]{1,2,0:T(8,128)(2,1)}), bf16[8,256,512]{1,2,0:T(8,128)(2,1)}, u32[]{:S(2)}, u32[]{:S(2)}) async-start(bf16[8,256,512]{1,2,0:T(8,128)(2,1)} %bitcast.284), calls=%async_computation.5 | async-start | bytes 4194304 | tf_op jit(solution)/shard_map/all_to_all | solution.py:485
  639.2 29.6 %copy-start.44 = (f32[16,128]{1,0:T(8,128)S(1)}, f32[16,128]{1,0:T(8,128)}, u32[]{:S(2)}) copy-start(f32[16,128]{1,0:T(8,128)} %copy-done.43) | copy-start | bytes 24580
  639.2 29.6 %copy-start.35 = (bf16[1024,256]{0,1:T(8,128)(2,1)S(1)}, bf16[1024,256]{0,1:T(8,128)(2,1)}, u32[]{:S(2)}) copy-start(bf16[1024,256]{0,1:T(8,128)(2,1)} %convolution_convert_fusion.5) | copy-start | bytes 1572868
  643.8 30.8 %copy-start.29 = (bf16[2,128,1024]{2,1,0:T(8,128)(2,1)S(1)}, bf16[2,128,1024]{2,1,0:T(8,128)(2,1)}, u32[]{:S(2)}) copy-start(bf16[2,128,1024]{2,1,0:T(8,128)(2,1)} %copy-done.28) | copy-start | bytes 1572868
  664.0 93.1 %all-to-all-start.4 = ((bf16[8,256,512]{1,2,0:T(8,128)(2,1)}), bf16[8,256,512]{1,2,0:T(8,128)(2,1)}, u32[]{:S(2)}, u32[]{:S(2)}) async-start(bf16[8,256,512]{1,2,0:T(8,128)(2,1)} %bitcast.266), calls=%async_computation.7 | async-start | bytes 4194304 | tf_op jit(solution)/shard_map/all_to_all | solution.py:485
  668.3 114.5 %reduce-scatter.17.cloned.1.call-start = ((), (), s32[]{:S(2)}) async-start(), calls=%async_computation.21 | async-start | bytes 1310720 | tf_op jit(solution)/shard_map/reduce_scatter | solution.py:630
  679.0 150.6 %reduce-scatter.15.cloned.1.call-start = ((), (), s32[]{:S(2)}) async-start(), calls=%async_computation.20 | async-start | bytes 3932160 | tf_op jit(solution)/shard_map/reduce_scatter | solution.py:572
  768.1 61.6 %all-to-all-start.5 = ((bf16[8,512,256]{2,1,0:T(8,128)(2,1)}), bf16[8,512,256]{2,1,0:T(8,128)(2,1)}, u32[]{:S(2)}, u32[]{:S(2)}) async-start(bf16[8,512,256]{2,1,0:T(8,128)(2,1)} %bitcast.283), calls=%async_computation.10 | async-start | bytes 4194304 | tf_op jit(solution)/shard_map/all_to_all | solution.py:485
  829.7 37.9 %all-to-all-start.6 = ((bf16[8,64,768]{2,1,0:T(8,128)(2,1)}), bf16[8,64,768]{2,1,0:T(8,128)(2,1)}, u32[]{:S(2)}, u32[]{:S(2)}) async-start(bf16[8,64,768]{2,1,0:T(8,128)(2,1)} %bitcast.314), calls=%async_computation.11 | async-start | bytes 1572864 | tf_op jit(solution)/shard_map/all_to_all | solution.py:485
  (55 other events, 595.9 us)
Sparse Core Ops, SparseCore 0:
  189.9 57.1 all-gather.3
  249.2 58.2 all-gather.7
  309.7 58.2 all-gather.5
  405.1 90.0 reduce-scatter.6
  497.6 71.0 reduce-scatter.8
  571.1 71.4 reduce-scatter.10
  645.2 71.4 reduce-scatter.12
  719.2 24.8 reduce-scatter.16
  765.2 47.2 reduce-scatter.14

commit v6 on v5

--- a/solution.py
+++ b/solution.py
@@ -494,9 +494,12 @@
     normed_b = rms_norm(inputs, attn_gain).astype(BF16)
     expert_ids = jnp.arange(experts, dtype=jnp.int32)
     marks = jnp.any(routing[0][:, :, None] == expert_ids[None, None, :], axis=1).astype(F32)
-    marks = jnp.concatenate([marks.T, segment_ids[0].astype(F32)[None]], axis=0)
+    own_scales = [
+        lax.rsqrt(jnp.mean(jnp.square(mm(normed_b, w)), axis=1) + EPSILON)[None] for w in (w_query, w_key)
+    ]
+    marks = jnp.concatenate([marks.T, segment_ids[0].astype(F32)[None]] + own_scales, axis=0)
     normed_all, marks = gather_rows([normed_b], groups, 1, note=marks)
-    marks = marks.transpose(1, 0, 2).reshape(experts + 1, length)
+    marks = marks.transpose(1, 0, 2).reshape(experts + 3, length)
     chosen, seg_all = marks[:experts].T > 0.5, marks[experts]
     down_in = w_down.reshape(groups, part, cols)
     gate_own, down_in, normed_late = together((gate_own, down_in, normed_all))
@@ -511,8 +514,7 @@
         sums = small_sum(sums.reshape(-1, 128), ("group",), False, collective_id)
         return sums.reshape(2, length, 1) / width
 
-    scales = lax.rsqrt(row_sums(query_raw * query_raw, key_raw * key_raw, 2) + EPSILON)
-    query_scale, key_scale = scales[0], scales[1]
+    query_scale, key_scale = marks[experts + 1][:, None], marks[experts + 2][:, None]
     query_gain_c, key_gain_c = own_cols(query_gain, 0), own_cols(key_gain, 0)
     cosine, sine = angles(length, head_dim)
 
@@ -529,10 +531,10 @@
     probs = jnp.exp(scores - log_total)
     probs_b = probs.astype(BF16)
     mixed_c = ein("hqk,khd->qhd", probs_b, values_b).reshape(length, cols).astype(BF16)
-    down_own, mixed_in = together((down_own, mixed_c))
+    down_own, gate_w, mixed_in = together((down_own, gate_w, mixed_c))
+    (mixed_b,) = swap([mixed_in], groups, False, 3)
+    up_in, down_own, mixed_b = together((slices(w_up), down_own, mixed_b))
     down_w = row_of_devices(down_own.transpose(1, 0, 2).reshape(part, width))
-    (mixed_b,) = swap([mixed_in], groups, False, 3)
-    up_in, mixed_b = together((slices(w_up), mixed_b))
     up_own = exchange(up_in)
     resid = inputs + mm(mixed_b, w_out)
     normed_mlp_b = rms_norm(resid, mlp_gain).astype(BF16)
@@ -551,6 +553,7 @@
     hidden = gate_pre * sigma * up_pre
     hidden_b = (hidden * picked).astype(BF16)
     out_part = ein("tef,efd->td", hidden_b, down_w).astype(BF16)
+    out_part, grad_all = together((out_part, grad_all))
     mixture = lax.psum_scatter(out_part, "group", scatter_dimension=0, tiled=True)
     hidden_grad = ein("td,efd->tef", grad_all, down_w)
     picked_grad = jnp.sum(hidden * hidden_grad, axis=2)
@@ -563,15 +566,12 @@
     full_part = full_part.T.reshape(experts, groups, rows).transpose(1, 0, 2)
     gate_w_part = ein("td,tef->edf", mlp_late, gate_grad_b).astype(BF16)
     up_w_part = ein("td,tef->edf", mlp_late, up_grad_b).astype(BF16)
-    down_w_part = ein("tef,td->efd", hidden_b, grad_all).astype(BF16)
-    up_w_part, down_w_part, gate_grad_b, up_grad_b = together(
-        (up_w_part, down_w_part, gate_grad_b, up_grad_b)
-    )
+    up_w_part, gate_grad_b, up_grad_b = together((up_w_part, gate_grad_b, up_grad_b))
 
     def over_row(w):
         return lax.psum_scatter(w, "expert", scatter_dimension=0, tiled=False)
 
-    gate_sum, up_sum, down_sum = over_row(gate_w_part), over_row(up_w_part), over_row(down_w_part)
+    gate_sum, up_sum = over_row(gate_w_part), over_row(up_w_part)
     slot_part = ein("tef,edf->td", gate_grad_b, gate_w) + ein("tef,edf->td", up_grad_b, up_w)
     slot_part, mixture = together((slot_part.astype(BF16), mixture))
     slot_sum, router_full_grad = reduce_rows(slot_part, full_part, groups, 5)
@@ -596,7 +596,7 @@
     (attn_grad_all,) = gather_rows([attn_grad_b], groups, 6)
     gate_sum, attn_grad_late = together((gate_sum, attn_grad_all))
     gate_sum = exchange(gate_sum.reshape(groups, cols, part))
-    mixed_grad_c = mm_nt(attn_grad_all, own_cols(w_out, 0)).astype(BF16)
+    mixed_grad_c = mm_nt(attn_grad_late, own_cols(w_out, 0)).astype(BF16)
     mixed_grad_c = mixed_grad_c.reshape(length, heads, head_dim)
 
     prob_grad = ein("qhd,khd->hqk", mixed_grad_c, values_b)
@@ -605,7 +605,12 @@
     score_grad_b, probs_b = together((score_grad_b, probs_b))
     query_grad = ein("hqk,khd->qhd", score_grad_b, keys_b)
     key_grad = ein("hqk,qhd->khd", score_grad_b, queries_b)
-    gate_sum, up_sum, query_grad, key_grad = together((gate_sum, up_sum, query_grad, key_grad))
+    query_grad, key_grad, hidden_b = together((query_grad, key_grad, hidden_b))
+    down_w_part = ein("tef,td->efd", hidden_b, grad_all).astype(BF16)
+    gate_sum, up_sum, query_grad, key_grad, probs_b, down_w_part = together(
+        (gate_sum, up_sum, query_grad, key_grad, probs_b, down_w_part)
+    )
+    down_sum = over_row(down_w_part)
     up_sum = exchange(up_sum.reshape(groups, cols, part))
     value_grad_b = ein("hqk,qhd->khd", probs_b, mixed_grad_c).astype(BF16).reshape(length, cols)
 
@@ -622,10 +627,11 @@
     query_gain_part = jnp.sum(query_turn * query_raw * query_scale, axis=0)
     key_gain_part = jnp.sum(key_turn * key_raw * key_scale, axis=0)
     raw_grads = [query_raw_b, key_raw_b, value_grad_b]
+    down_sum = down_sum.reshape(part, groups, cols).transpose(1, 0, 2)
     (query_own, key_own, value_own), raw_grads, up_sum, down_sum = together(
         (swap(raw_grads, groups, False, 8), raw_grads, up_sum, down_sum)
     )
-    down_sum = exchange(down_sum.reshape(part, groups, cols).transpose(1, 0, 2))
+    down_sum = exchange(down_sum)
     out_w_part = mm_tn(mixed_c, attn_grad_late).astype(BF16)
     out_w_grad = lax.psum_scatter(out_w_part, "expert", scatter_dimension=0, tiled=True)
     qkv_part = mm_tn(normed_late, jnp.concatenate(raw_grads, axis=1)).astype(BF16)

time: 895 us -> 906 us (1.012)
  waiting for transfers between devices: 44.6 us -> 54.8 us
    reduce_scatter x1, waiting for transfers between devices: 0.01 us -> 13.8 us  [shards(): lax.psum_scatter(out_part, 'group', scatter_dimension=0, tiled=True)]
    dot_general x6 -> x8, matrix products: 18.9 us -> 28.9 us  [mm(): return jnp.dot(left, right, preferred_element_type=F32)]
    pallas_call x3 -> x2, Pallas kernels: 56.8 us -> 62.3 us  [small_sum(): pl.pallas_call(functools.partial(small_sum_kernel, axes, scatter), name='...]
    unnamed x153 -> x174, local copies, waits for them, and re-layouts: 18 us -> 20.7 us
  transfers between devices with their start and end apart: 16 -> 16, of which waited for: 3 -> 4; matrix products, arithmetic and copies ran while one was open for 34% -> 32% of each run, Pallas kernels for 47% -> 45%
where the time goes in v6:
time: 906 us; the launch traced here: 895 us
  Pallas kernels  417 us (46%)
  matrix products  228 us (25%)
  local copies, waits for them, and re-layouts  81.4 us (9%)
  waiting for transfers between devices  54.8 us (6%)
  starting transfers between devices  51.2 us (6%)
  other arithmetic  47.6 us (5%)
  between operations  15.6 us (2%)
    pallas_call x4, Pallas kernels, gather_rows(): pl.pallas_call(functools.partial(gather_kernel, nz, groups // nz, pieces,...  256 us
    dot_general x14, matrix products, ein(): return jnp.einsum(spec, *ops, preferred_element_type=F32)  150 us
    pallas_call x2, Pallas kernels, small_sum(): pl.pallas_call(functools.partial(small_sum_kernel, axes, scatter), name='...  62.3 us
    pallas_call x1, Pallas kernels, reduce_rows(): pl.pallas_call(functools.partial(reduce_kernel, nz, ny, pieces), name='re...  53.7 us
    all_to_all x7, starting transfers between devices, exchange(): return lax.all_to_all(w, 'group', 0, 0, tiled=True)  49.1 us
    pallas_call x2, Pallas kernels, swap(): pl.pallas_call(functools.partial(swap_kernel, groups, to_rows), name='swa...  44.1 us
    all_to_all x7, waiting for transfers between devices, exchange(): return lax.all_to_all(w, 'group', 0, 0, tiled=True)  40.8 us
    dot_general x8, matrix products, mm(): return jnp.dot(left, right, preferred_element_type=F32)  28.9 us
  transfers between devices with their start and end apart: 16, of which 4 were waited for; matrix products, arithmetic and copies ran while one was open for 32% of the time, Pallas kernels for 45%

profile of v6, /device:TPU:0, one launch (start us, length us, event | category | flops | bytes accessed | tf_op | source)
XLA Modules:
  0.0 894.9 jit_solution(13061663424779491175)
XLA Ops:
  10.4 7.3 all-to-all-start
  27.1 80.4 %gather_rows.4 = (bf16[8,128,2048]{2,1,0:T(8,128)(2,1)}, f32[8,19,128]{2,1,0:T(8,128)}) custom-call(bf16[128,2048]{1,0:T(8,128)(2,1)} %copy-done.7, f32[19,128]{1,0:T(8,128)} %pad_maximum_fusion.8.refs_1_), custom_call_target="tpu_custom_call" | custom-call | bytes 200000000 | tf_op jit(solution)/shard_map/gather_rows/pallas_call | solution.py:153
  116.6 5.8 multiply_multiply_fusion.1
  135.7 6.5 all-to-all-start.1
  162.1 27.9 %all-to-all-done.1 = bf16[8,512,256]{2,1,0:T(8,128)(2,1)S(1)} async-done(((bf16[8,512,256]{2,1,0:T(8,128)(2,1)}), bf16[8,512,256]{2,1,0:T(8,128)(2,1)S(1)}, u32[]{:S(2)}, u32[]{:S(2)}) %all-to-all-start.1) | async-done | bytes 2097184 | tf_op jit(solution)/shard_map/all_to_all | solution.py:485
  191.0 13.5 %swap.2 = bf16[128,2048]{1,0:T(8,128)(2,1)} custom-call(bf16[8,128,256]{2,1,0:T(8,128)(2,1)} %bitcast.313), custom_call_target="tpu_custom_call" | custom-call | bytes 30000000 | tf_op jit(solution)/shard_map/swap/pallas_call | solution.py:339
  210.9 7.9 all-to-all-start.2
  218.8 5.8 multiply_reduce_fusion.6
  226.6 78.5 %gather_rows.5 = bf16[8,128,2048]{2,1,0:T(8,128)(2,1)} custom-call(bf16[128,2048]{1,0:T(8,128)(2,1)} %multiply_convert_fusion.4.refs_0_), custom_call_target="tpu_custom_call" | custom-call | bytes 200000000 | tf_op jit(solution)/shard_map/gather_rows/pallas_call | solution.py:153
  310.2 14.7 %fusion.76 = f32[1024,4,512]{0,2,1:T(8,128)} fusion(bf16[1024,2048,1]{1,0,2:T(8,128)(2,1)} %bitcast.280, bf16[4,2048,512]{2,1,0:T(8,128)(2,1)} %all-gather.4.cloned.1.call-done), kind=kOutput, calls=%fused_computation.186 | convolution fusion | flops 8589934592 | bytes 20971520 | tf_op jit(solution)/shard_map/td,edf->tef/dot_general | solution.py:440
  324.9 48.4 %gather_rows.6 = bf16[8,128,2048]{2,1,0:T(8,128)(2,1)} custom-call(bf16[128,2048]{1,0:T(8,128)(2,1)} %bitcast.296), custom_call_target="tpu_custom_call" | custom-call | bytes 200000000 | tf_op jit(solution)/shard_map/gather_rows/pallas_call | solution.py:153
  373.4 17.9 %multiply_convert_fusion.3 = (bf16[1024,4,512]{0,2,1:T(8,128)(2,1)}, f32[1024,4,512]{0,2,1:T(8,128)}) fusion(f32[1024,4]{0,1:T(4,128)S(1)} %bitcast.343, f32[1024,4,512]{0,2,1:T(8,128)} %fusion.76, bf16[1024,2048,1]{1,0,2:T(8,128)(2,1)} %bitcast.281, bf16[4,2048,512]{2,1,0:T(8,128)(2,1)} %all-gather.8.cloned.1.call-done), kind=kOutput, calls=%fused_computation.12 | convolution fusion | flops 8604614656 | bytes 33570816 | tf_op jit(solution)/shard_map/td,edf->tef/dot_general | solution.py:440
  391.3 14.1 %bitcast_convert_fusion = bf16[1024,2048]{1,0:T(8,128)(2,1)} fusion(bf16[1024,4,512]{0,2,1:T(8,128)(2,1)} %get-tuple-element.98, bf16[4,512,2048]{2,1,0:T(8,128)(2,1)} %all-gather.6.cloned.1.call-done), kind=kOutput, calls=%fused_computation.3 | convolution fusion | flops 8592031744 | bytes 16777216 | tf_op jit(solution)/shard_map/tef,efd->td/dot_general | solution.py:440
  405.7 21.8 %multiply_reduce_fusion.1 = (f32[1024,4]{0,1:T(4,128)S(1)}, bf16[1024,4,512]{0,2,1:T(8,128)(2,1)}, bf16[1024,4,512]{0,2,1:T(8,128)(2,1)}) fusion(f32[1024,4,512]{0,2,1:T(8,128)} %get-tuple-element.179, f32[1024,4,512]{0,2,1:T(8,128)} %fusion.76, f32[1024,4]{0,1:T(4,128)S(1)} %bitcast.344, bf16[4,512,2048]{2,1,0:T(8,128)(2,1)} %all-gather.6.cloned.1.call-done, ...), kind=kOutput, calls=%fused_computation.8 | convolution fusion | flops 8627679232 | bytes 37781504 | tf_op jit(solution)/shard_map/td,efd->tef/dot_general | solution.py:440
  427.5 13.4 %convert_bitcast_fusion = bf16[4,2048,512]{1,2,0:T(8,128)(2,1)} fusion(bf16[1024,4,512]{0,2,1:T(8,128)(2,1)} %get-tuple-element.84, bf16[1024,2048]{1,0:T(8,128)(2,1)S(1)} %bitcast.283), kind=kOutput, calls=%fused_computation.7 | convolution fusion | flops 8594128896 | bytes 16777216 | tf_op jit(solution)/shard_map/td,tef->edf/dot_general | solution.py:440
  441.4 14.1 %convert_bitcast_fusion.1 = bf16[4,2048,512]{1,2,0:T(8,128)(2,1)} fusion(bf16[1024,4,512]{0,2,1:T(8,128)(2,1)} %get-tuple-element.85, bf16[1024,2048]{1,0:T(8,128)(2,1)} %bitcast.282), kind=kOutput, calls=%fused_computation.10 | convolution fusion | flops 8594128896 | bytes 16777216 | tf_op jit(solution)/shard_map/td,tef->edf/dot_general | solution.py:440
  457.6 12.9 %fusion.77 = f32[1024,2048,1]{1,0,2:T(8,128)S(1)} fusion(bf16[1024,4,512]{0,2,1:T(8,128)(2,1)} %get-tuple-element.84, bf16[4,2048,512]{2,1,0:T(8,128)(2,1)} %all-gather.4.cloned.1.call-done), kind=kOutput, calls=%fused_computation.187 | convolution fusion | flops 8589934592 | bytes 20971520 | tf_op jit(solution)/shard_map/tef,edf->td/dot_general | solution.py:440
  470.5 12.9 %fusion.1 = bf16[1024,2048]{1,0:T(8,128)(2,1)} fusion(f32[1024,2048,1]{1,0,2:T(8,128)S(1)} %fusion.77, bf16[1024,4,512]{0,2,1:T(8,128)(2,1)S(1)} %copy-done.78, bf16[4,2048,512]{2,1,0:T(8,128)(2,1)} %all-gather.8.cloned.1.call-done), kind=kOutput, calls=%fused_computation.2 | convolution fusion | flops 8594128896 | bytes 25165824 | tf_op jit(solution)/shard_map/tef,edf->td/dot_general | solution.py:440
  483.4 13.8 %reduce-scatter.7.cloned.1.call-done = bf16[128,2048]{1,0:T(8,128)(2,1)} async-done(((bf16[1024,2048]{1,0:T(8,128)(2,1)}), bf16[128,2048]{1,0:T(8,128)(2,1)}) %reduce-scatter.7.cloned.1.call-update) | async-done | bytes 524304 | tf_op jit(solution)/shard_map/reduce_scatter | solution.py:557
  497.2 53.7 %reduce_rows.1 = (f32[128,2048]{1,0:T(8,128)}, f32[16,128]{1,0:T(8,128)}) custom-call(bf16[8,128,2048]{2,1,0:T(8,128)(2,1)} %bitcast.303, f32[8,16,128]{2,1,0:T(8,128)} %bitcast_bitcast_fusion.note), custom_call_target="tpu_custom_call" | custom-call | bytes 200000000 | tf_op jit(solution)/shard_map/reduce_rows/pallas_call | solution.py:272
  556.3 49.2 %gather_rows.7 = bf16[8,128,2048]{2,1,0:T(8,128)(2,1)} custom-call(bf16[128,2048]{1,0:T(8,128)(2,1)} %fusion.68.refs_0_), custom_call_target="tpu_custom_call" | custom-call | bytes 200000000 | tf_op jit(solution)/shard_map/gather_rows/pallas_call | solution.py:153
  617.7 14.4 %multiply_convert_fusion = bf16[2,1024,1024]{1,2,0:T(8,128)(2,1)} fusion(f32[2,1024,1024]{1,2,0:T(8,128)} %copy-done.2, f32[2,1024]{1,0:T(2,128)S(1)} %copy-done.61, pred[1024,1024]{0,1:T(8,128)(4,1)S(1)} %copy-done.11, bf16[1024,2,128]{0,2,1:T(8,128)(2,1)} %bitcast.323, bf16[1024,2,128]{0,2,1:T(8,128)(2,1)} %bitcast.322), kind=kOutput, calls=%fused_computation.4 | convolution fusion | flops 1096813568 | bytes 14688256 | tf_op jit(solution)/shard_map/sub | solution.py:604
  639.8 13.4 %convolution_convert_fusion = bf16[4,512,2048]{2,1,0:T(8,128)(2,1)} fusion(bf16[1024,4,512]{0,2,1:T(8,128)(2,1)} %get-tuple-element.98, bf16[1024,2048]{1,0:T(8,128)(2,1)S(1)} %bitcast.300), kind=kOutput, calls=%fused_computation.19 | convolution fusion | flops 8594128896 | bytes 16777216 | tf_op jit(solution)/shard_map/tef,td->efd/dot_general | solution.py:440
  653.2 7.1 all-to-all-done.3
  679.7 38.6 %small_sum.2 = f32[16,128]{1,0:T(8,128)} custom-call(f32[16,128]{1,0:T(8,128)} %reshape.459.values), custom_call_target="tpu_custom_call" | custom-call | bytes 10000000 | tf_op jit(solution)/shard_map/small_sum/pallas_call | solution.py:391
  733.2 30.5 %swap.3 = (bf16[128,2048]{1,0:T(8,128)(2,1)}, bf16[128,2048]{1,0:T(8,128)(2,1)}, bf16[128,2048]{1,0:T(8,128)(2,1)}) custom-call(bf16[8,128,256]{2,1,0:T(8,128)(2,1)} %bitcast.305, bf16[8,128,256]{2,1,0:T(8,128)(2,1)} %bitcast.306, bf16[8,128,256]{2,1,0:T(8,128)(2,1)} %copy.253.refs_2_), custom_call_target="tpu_custom_call" | custom-call | bytes 30000000 | tf_op jit(solution)/shard_map/swap/pallas_call | solution.py:339
  768.0 5.7 convolution_convert_fusion.1
  775.7 14.3 %all-to-all-start.5 = ((bf16[8,512,256]{2,1,0:T(8,128)(2,1)}), bf16[8,512,256]{2,1,0:T(8,128)(2,1)}, u32[]{:S(2)}, u32[]{:S(2)}) async-start(bf16[8,512,256]{2,1,0:T(8,128)(2,1)} %bitcast.290), calls=%async_computation.10 | async-start | bytes 4194304 | tf_op jit(solution)/shard_map/all_to_all | solution.py:485
  803.9 6.4 fusion.78
  810.4 6.5 convolution_add_fusion.2
  831.6 5.8 all-to-all-done.5
  844.8 23.8 %small_sum.3 = f32[16,128]{1,0:T(8,128)} custom-call(f32[32,16,128]{2,1,0:T(8,128)} %bitcast.319), custom_call_target="tpu_custom_call" | custom-call | bytes 10000000 | tf_op jit(solution)/shard_map/small_sum/pallas_call | solution.py:391
  (320 shorter events, 192.5 us)
Async XLA Ops:
  7.2 299.5 %copy-start = (bf16[2048,16]{0,1:T(8,128)(2,1)S(1)}, bf16[2048,16]{0,1:T(8,128)(2,1)}, u32[]{:S(2)}) copy-start(bf16[2048,16]{0,1:T(8,128)(2,1)} %param.28) | copy-start | bytes 196612
  10.4 97.1 %all-to-all-start = ((bf16[8,256,512]{2,1,0:T(8,128)(2,1)}), bf16[8,256,512]{2,1,0:T(8,128)(2,1)S(1)}, u32[]{:S(2)}, u32[]{:S(2)}) async-start(bf16[8,256,512]{2,1,0:T(8,128)(2,1)} %bitcast.293), calls=%async_computation | async-start | bytes 4194304 | tf_op jit(solution)/shard_map/all_to_all | solution.py:485
  17.7 172.3 %all-gather.4.cloned.1.call-start = ((), (), s32[]{:S(2)}) async-start(), calls=%async_computation.13 | async-start | bytes 10485760 | tf_op jit(solution)/shard_map/all_gather | solution.py:488
  127.6 18.9 %copy-start.20 = (f32[1024,64]{1,0:T(8,128)}, f32[1024,64]{1,0:T(8,128)S(1)}, u32[]{:S(2)}) copy-start(f32[1024,64]{1,0:T(8,128)S(1)} %get-tuple-element.167) | copy-start | bytes 786436
  135.7 54.3 %all-to-all-start.1 = ((bf16[8,512,256]{2,1,0:T(8,128)(2,1)}), bf16[8,512,256]{2,1,0:T(8,128)(2,1)S(1)}, u32[]{:S(2)}, u32[]{:S(2)}) async-start(bf16[8,512,256]{2,1,0:T(8,128)(2,1)} %bitcast.309), calls=%async_computation.1 | async-start | bytes 4194304 | tf_op jit(solution)/shard_map/all_to_all | solution.py:485
  142.2 163.0 %all-gather.6.cloned.1.call-start = ((), (), s32[]{:S(2)}) async-start(), calls=%async_computation.14 | async-start | bytes 10485760 | tf_op jit(solution)/shard_map/all_gather | solution.py:488
  162.0 44.9 %copy-start.44 = (bf16[2,128,1024]{2,1,0:T(8,128)(2,1)}, bf16[2,128,1024]{2,1,0:T(8,128)(2,1)S(1)}, u32[]{:S(2)}) copy-start(bf16[2,128,1024]{2,1,0:T(8,128)(2,1)S(1)} %convolution_convert_fusion.4) | copy-start | bytes 1572868
  210.9 94.2 %all-to-all-start.2 = ((bf16[8,256,512]{2,1,0:T(8,128)(2,1)}), bf16[8,256,512]{2,1,0:T(8,128)(2,1)S(1)}, u32[]{:S(2)}, u32[]{:S(2)}) async-start(bf16[8,256,512]{2,1,0:T(8,128)(2,1)} %bitcast.292), calls=%async_computation.2 | async-start | bytes 4194304 | tf_op jit(solution)/shard_map/all_to_all | solution.py:485
  218.7 154.6 %all-gather.8.cloned.1.call-start = ((), (), s32[]{:S(2)}) async-start(), calls=%async_computation.15 | async-start | bytes 10485760 | tf_op jit(solution)/shard_map/all_gather | solution.py:488
  306.5 190.8 %reduce-scatter.7.cloned.1.call-start = ((), (), s32[]{:S(2)}) async-start(), calls=%async_computation.16 | async-start | bytes 4718592 | tf_op jit(solution)/shard_map/reduce_scatter | solution.py:557
  405.4 200.1 %reduce-scatter.9.cloned.1.call-start = ((), (), s32[]{:S(2)}) async-start(), calls=%async_computation.17 | async-start | bytes 10485760 | tf_op jit(solution)/shard_map/reduce_scatter | solution.py:572
  405.7 21.8 %copy-start.5 = (bf16[8,128,2048]{2,1,0:T(8,128)(2,1)S(1)}, bf16[8,128,2048]{2,1,0:T(8,128)(2,1)}, u32[]{:S(2)}) copy-start(bf16[8,128,2048]{2,1,0:T(8,128)(2,1)} %gather_rows.5) | copy-start | bytes 12582916
  441.0 212.3 %reduce-scatter.11.cloned.1.call-start = ((), (), s32[]{:S(2)}) async-start(), calls=%async_computation.18 | async-start | bytes 10485760 | tf_op jit(solution)/shard_map/reduce_scatter | solution.py:572
  483.4 68.9 %copy-start.4 = (f32[128,2048]{1,0:T(8,128)S(1)}, f32[128,2048]{1,0:T(8,128)}, u32[]{:S(2)}) copy-start(f32[128,2048]{1,0:T(8,128)} %copy-done.3) | copy-start | bytes 3145732
  483.4 68.9 %copy-start.53 = (f32[2048]{0:T(1024)S(1)}, f32[2048]{0:T(1024)}, u32[]{:S(2)}) copy-start(f32[2048]{0:T(1024)} %param.27) | copy-start | bytes 24580
  483.4 68.9 %copy-start.68 = (f32[128]{0:T(128)S(1)}, f32[128]{0:T(128)}, u32[]{:S(2)}) copy-start(f32[128]{0:T(128)} %copy-done.67) | copy-start | bytes 1540
  483.4 70.7 %copy-start.73 = (f32[128]{0:T(128)S(1)}, f32[128]{0:T(128)}, u32[]{:S(2)}) copy-start(f32[128]{0:T(128)} %copy-done.72) | copy-start | bytes 1540
  483.4 71.7 %copy-start.21 = (bf16[1,128,2048]{2,1,0:T(8,128)(2,1)S(1)}, bf16[1,128,2048]{2,1,0:T(8,128)(2,1)}, u32[]{:S(2)}) copy-start(bf16[1,128,2048]{2,1,0:T(8,128)(2,1)} %param.19) | copy-start | bytes 1572868
  608.6 51.8 %all-to-all-start.3 = ((bf16[8,256,512]{1,2,0:T(8,128)(2,1)}), bf16[8,256,512]{1,2,0:T(8,128)(2,1)}, u32[]{:S(2)}, u32[]{:S(2)}) async-start(bf16[8,256,512]{1,2,0:T(8,128)(2,1)} %bitcast.272), calls=%async_computation.5 | async-start | bytes 4194304 | tf_op jit(solution)/shard_map/all_to_all | solution.py:485
  613.0 150.8 %reduce-scatter.13.cloned.1.call-start = ((), (), s32[]{:S(2)}) async-start(), calls=%async_computation.19 | async-start | bytes 10485760 | tf_op jit(solution)/shard_map/reduce_scatter | solution.py:572
  617.7 14.4 %copy-start.38 = (bf16[1024,2,64]{2,0,1:T(8,128)(2,1)S(1)}, bf16[1024,2,64]{2,0,1:T(8,128)(2,1)}, u32[]{:S(2)}) copy-start(bf16[1024,2,64]{2,0,1:T(8,128)(2,1)} %copy-done.37) | copy-start | bytes 786436
  617.7 14.4 %copy-start.40 = (bf16[1024,2,64]{2,0,1:T(8,128)(2,1)S(1)}, bf16[1024,2,64]{2,0,1:T(8,128)(2,1)}, u32[]{:S(2)}) copy-start(bf16[1024,2,64]{2,0,1:T(8,128)(2,1)} %copy-done.39) | copy-start | bytes 786436
  663.5 104.5 %all-to-all-start.4 = ((bf16[8,256,512]{1,2,0:T(8,128)(2,1)}), bf16[8,256,512]{1,2,0:T(8,128)(2,1)}, u32[]{:S(2)}, u32[]{:S(2)}) async-start(bf16[8,256,512]{1,2,0:T(8,128)(2,1)} %bitcast.271), calls=%async_computation.7 | async-start | bytes 4194304 | tf_op jit(solution)/shard_map/all_to_all | solution.py:485
  667.8 122.7 %reduce-scatter.17.cloned.1.call-start = ((), (), s32[]{:S(2)}) async-start(), calls=%async_computation.21 | async-start | bytes 1310720 | tf_op jit(solution)/shard_map/reduce_scatter | solution.py:636
  673.6 163.8 %reduce-scatter.15.cloned.1.call-start = ((), (), s32[]{:S(2)}) async-start(), calls=%async_computation.20 | async-start | bytes 3932160 | tf_op jit(solution)/shard_map/reduce_scatter | solution.py:572
  775.6 14.4 %copy-start.17 = (bf16[128,2048]{1,0:T(8,128)(2,1)S(1)}, bf16[128,2048]{1,0:T(8,128)(2,1)}, u32[]{:S(2)}) copy-start(bf16[128,2048]{1,0:T(8,128)(2,1)} %multiply_convert_fusion.4.refs_0_) | copy-start | bytes 1572868
  775.7 61.7 %all-to-all-start.5 = ((bf16[8,512,256]{2,1,0:T(8,128)(2,1)}), bf16[8,512,256]{2,1,0:T(8,128)(2,1)}, u32[]{:S(2)}, u32[]{:S(2)}) async-start(bf16[8,512,256]{2,1,0:T(8,128)(2,1)} %bitcast.290), calls=%async_computation.10 | async-start | bytes 4194304 | tf_op jit(solution)/shard_map/all_to_all | solution.py:485
  803.9 13.0 %slice-start.2 = ((s8[8388608]{0:T(1024)(128)(4,1)}), s8[4194304]{0:T(1024)(128)(4,1)S(1)}, s32[]{:S(2)}) async-start(s8[8388608]{0:T(1024)(128)(4,1)} %bitcast.287), calls=%async_computation.24 | async-start | bytes 8388608
  826.1 15.7 %copy-start.75 = (f32[128]{0:T(128)S(1)}, f32[128]{0:T(128)}, u32[]{:S(2)}) copy-start(f32[128]{0:T(128)} %copy-done.74) | copy-start | bytes 1540
  826.1 15.7 %copy-start.15 = (f32[128,2048]{1,0:T(8,128)S(1)}, f32[128,2048]{1,0:T(8,128)}, u32[]{:S(2)}) copy-start(f32[128,2048]{1,0:T(8,128)} %copy-done.14) | copy-start | bytes 3145732
  826.1 15.7 %copy-start.22 = (bf16[1,128,2048]{2,1,0:T(8,128)(2,1)S(1)}, bf16[1,128,2048]{2,1,0:T(8,128)(2,1)}, u32[]{:S(2)}) copy-start(bf16[1,128,2048]{2,1,0:T(8,128)(2,1)} %param.19) | copy-start | bytes 1572868
  837.3 37.9 %all-to-all-start.6 = ((bf16[8,64,768]{2,1,0:T(8,128)(2,1)}), bf16[8,64,768]{2,1,0:T(8,128)(2,1)}, u32[]{:S(2)}, u32[]{:S(2)}) async-start(bf16[8,64,768]{2,1,0:T(8,128)(2,1)} %bitcast.320), calls=%async_computation.11 | async-start | bytes 1572864 | tf_op jit(solution)/shard_map/all_to_all | solution.py:485
  (67 other events, 316.0 us)
Sparse Core Ops, SparseCore 0:
  109.0 60.4 all-gather.3
  211.0 61.4 all-gather.5
  306.6 59.8 all-gather.7
  405.5 91.6 reduce-scatter.6
  499.6 71.0 reduce-scatter.8
  573.2 71.3 reduce-scatter.10
  660.5 70.3 reduce-scatter.12
  733.4 24.8 reduce-scatter.16
  775.8 47.1 reduce-scatter.14

commit v7 on v6

--- a/solution.py
+++ b/solution.py
@@ -523,6 +523,7 @@
 
     queries_b = turned(query_raw, query_scale, query_gain_c).astype(BF16)
     keys_b = turned(key_raw, key_scale, key_gain_c).astype(BF16)
+    down_own, queries_b, keys_b = together((down_own, queries_b, keys_b))
     place = jnp.arange(length, dtype=jnp.int32)
     allowed = (seg_all[:, None] == seg_all[None, :]) & (place[None, :] <= place[:, None])
     scores = jnp.where(allowed[None], ein("qhd,khd->hqk", queries_b, keys_b) * score_scale, MASKED)
@@ -531,7 +532,7 @@
     probs = jnp.exp(scores - log_total)
     probs_b = probs.astype(BF16)
     mixed_c = ein("hqk,khd->qhd", probs_b, values_b).reshape(length, cols).astype(BF16)
-    down_own, gate_w, mixed_in = together((down_own, gate_w, mixed_c))
+    gate_w, mixed_in = together((gate_w, mixed_c))
     (mixed_b,) = swap([mixed_in], groups, False, 3)
     up_in, down_own, mixed_b = together((slices(w_up), down_own, mixed_b))
     down_w = row_of_devices(down_own.transpose(1, 0, 2).reshape(part, width))
@@ -619,7 +620,10 @@
 
     query_turn, key_turn = unturned(query_grad), unturned(key_grad)
     query_mix, key_mix = query_turn * query_gain_c, key_turn * key_gain_c
-    dots = row_sums(query_mix * query_raw, key_mix * key_raw, 7)
+    query_dots, key_dots, value_grad_b = together(
+        (query_mix * query_raw, key_mix * key_raw, value_grad_b)
+    )
+    dots = row_sums(query_dots, key_dots, 7)
     query_raw_b = (
         query_scale * query_mix - query_raw * query_scale**3 * dots[0]
     ).astype(BF16)
@@ -650,10 +654,11 @@
     small = small.reshape(-1, devices, width // devices).transpose(1, 0, 2).reshape(devices, -1)
     used = small.shape[1]
     small = jnp.pad(small, ((0, 0), (0, -used % 1024))).reshape(devices, -1, 128)
+    small = small_sum(small, ("group", "expert"), True, 9)
     small, qkv_part, down_sum = together((small, qkv_part, down_sum))
     qkv_part = exchange(qkv_part)
     qkv_part = qkv_part.transpose(1, 0, 2).reshape(-1, groups, 3, cols).astype(F32)
-    small = small_sum(small, ("group", "expert"), True, 9).reshape(-1)[:used]
+    small = small.reshape(-1)[:used]
     small = small.reshape(-1, width // devices)
     return (
         result[None],

time: 906 us -> 878 us (0.969)
  Pallas kernels: 417 us -> 397 us
  local copies, waits for them, and re-layouts: 81.4 us -> 68 us
    pallas_call x2, Pallas kernels: 62.3 us -> 43.1 us  [small_sum(): pl.pallas_call(functools.partial(small_sum_kernel, axes, scatter), name='...]
    unnamed x174 -> x145, local copies, waits for them, and re-layouts: 20.7 us -> 18.6 us
  transfers between devices with their start and end apart: 16 -> 16, of which waited for: 4 -> 4; matrix products, arithmetic and copies ran while one was open for 32% -> 32% of each run, Pallas kernels for 45% -> 44%
where the time goes in v7:
time: 878 us; the launch traced here: 872 us
  Pallas kernels  397 us (45%)
  matrix products  226 us (26%)
  local copies, waits for them, and re-layouts  68 us (8%)
  waiting for transfers between devices  60.7 us (7%)
  other arithmetic  53.4 us (6%)
  starting transfers between devices  50.8 us (6%)
  between operations  15.6 us (2%)
    pallas_call x4, Pallas kernels, gather_rows(): pl.pallas_call(functools.partial(gather_kernel, nz, groups // nz, pieces,...  256 us
    dot_general x14, matrix products, ein(): return jnp.einsum(spec, *ops, preferred_element_type=F32)  147 us
    pallas_call x1, Pallas kernels, reduce_rows(): pl.pallas_call(functools.partial(reduce_kernel, nz, ny, pieces), name='re...  53.6 us
    all_to_all x7, starting transfers between devices, exchange(): return lax.all_to_all(w, 'group', 0, 0, tiled=True)  49.6 us
    all_to_all x7, waiting for transfers between devices, exchange(): return lax.all_to_all(w, 'group', 0, 0, tiled=True)  46.6 us
    pallas_call x2, Pallas kernels, swap(): pl.pallas_call(functools.partial(swap_kernel, groups, to_rows), name='swa...  44.1 us
    pallas_call x2, Pallas kernels, small_sum(): pl.pallas_call(functools.partial(small_sum_kernel, axes, scatter), name='...  43.1 us
    dot_general x8, matrix products, mm(): return jnp.dot(left, right, preferred_element_type=F32)  29.5 us
  transfers between devices with their start and end apart: 16, of which 4 were waited for; matrix products, arithmetic and copies ran while one was open for 32% of the time, Pallas kernels for 44%

profile of v7, /device:TPU:0, one launch (start us, length us, event | category | flops | bytes accessed | tf_op | source)
XLA Modules:
  0.0 871.6 jit_solution(7075467067047072922)
XLA Ops:
  10.4 7.3 all-to-all-start
  27.1 80.4 %gather_rows.4 = (bf16[8,128,2048]{2,1,0:T(8,128)(2,1)}, f32[8,19,128]{2,1,0:T(8,128)}) custom-call(bf16[128,2048]{1,0:T(8,128)(2,1)} %copy-done.7, f32[19,128]{1,0:T(8,128)} %pad_maximum_fusion.6.refs_1_), custom_call_target="tpu_custom_call" | custom-call | bytes 200000000 | tf_op jit(solution)/shard_map/gather_rows/pallas_call | solution.py:153
  108.9 6.8 all-to-all-start.1
  138.8 24.7 %all-to-all-done.1 = bf16[8,512,256]{2,1,0:T(8,128)(2,1)} async-done(((bf16[8,512,256]{2,1,0:T(8,128)(2,1)}), bf16[8,512,256]{2,1,0:T(8,128)(2,1)}, u32[]{:S(2)}, u32[]{:S(2)}) %all-to-all-start.1) | async-done | bytes 2097184 | tf_op jit(solution)/shard_map/all_to_all | solution.py:485
  174.6 13.6 %swap.2 = bf16[128,2048]{1,0:T(8,128)(2,1)} custom-call(bf16[8,128,256]{2,1,0:T(8,128)(2,1)} %bitcast.293), custom_call_target="tpu_custom_call" | custom-call | bytes 30000000 | tf_op jit(solution)/shard_map/swap/pallas_call | solution.py:339
  193.5 7.9 all-to-all-start.2
  201.7 5.9 multiply_reduce_fusion.6
  209.6 78.1 %gather_rows.5 = bf16[8,128,2048]{2,1,0:T(8,128)(2,1)} custom-call(bf16[128,2048]{1,0:T(8,128)(2,1)} %multiply_convert_fusion.4.refs_0_), custom_call_target="tpu_custom_call" | custom-call | bytes 200000000 | tf_op jit(solution)/shard_map/gather_rows/pallas_call | solution.py:153
  292.7 14.6 %fusion.66 = f32[1024,4,512]{0,2,1:T(8,128)} fusion(bf16[1024,2048,1]{1,0,2:T(8,128)(2,1)} %bitcast.254, bf16[4,2048,512]{2,1,0:T(8,128)(2,1)} %all-gather.4.cloned.1.call-done), kind=kOutput, calls=%fused_computation.174 | convolution fusion | flops 8589934592 | bytes 20971520 | tf_op jit(solution)/shard_map/td,edf->tef/dot_general | solution.py:440
  307.3 48.4 %gather_rows.6 = bf16[8,128,2048]{2,1,0:T(8,128)(2,1)} custom-call(bf16[128,2048]{1,0:T(8,128)(2,1)} %bitcast.272), custom_call_target="tpu_custom_call" | custom-call | bytes 200000000 | tf_op jit(solution)/shard_map/gather_rows/pallas_call | solution.py:153
  355.8 17.9 %multiply_convert_fusion.3 = (bf16[1024,4,512]{0,2,1:T(8,128)(2,1)}, f32[1024,4,512]{0,2,1:T(8,128)}) fusion(f32[1024,4]{0,1:T(4,128)S(1)} %bitcast.320, f32[1024,4,512]{0,2,1:T(8,128)} %fusion.66, bf16[1024,2048,1]{1,0,2:T(8,128)(2,1)} %bitcast.255, bf16[4,2048,512]{2,1,0:T(8,128)(2,1)} %all-gather.8.cloned.1.call-done), kind=kOutput, calls=%fused_computation.12 | convolution fusion | flops 8604614656 | bytes 33570816 | tf_op jit(solution)/shard_map/td,edf->tef/dot_general | solution.py:440
  373.7 14.1 %bitcast_convert_fusion = bf16[1024,2048]{1,0:T(8,128)(2,1)} fusion(bf16[1024,4,512]{0,2,1:T(8,128)(2,1)} %get-tuple-element.105, bf16[4,512,2048]{2,1,0:T(8,128)(2,1)} %all-gather.6.cloned.1.call-done), kind=kOutput, calls=%fused_computation.3 | convolution fusion | flops 8592031744 | bytes 16777216 | tf_op jit(solution)/shard_map/tef,efd->td/dot_general | solution.py:440
  388.1 21.8 %multiply_reduce_fusion.1 = (f32[1024,4]{0,1:T(4,128)S(1)}, bf16[1024,4,512]{0,2,1:T(8,128)(2,1)}, bf16[1024,4,512]{0,2,1:T(8,128)(2,1)}) fusion(f32[1024,4,512]{0,2,1:T(8,128)} %get-tuple-element.185, f32[1024,4,512]{0,2,1:T(8,128)} %fusion.66, f32[1024,4]{0,1:T(4,128)S(1)} %bitcast.321, bf16[4,512,2048]{2,1,0:T(8,128)(2,1)} %all-gather.6.cloned.1.call-done, ...), kind=kOutput, calls=%fused_computation.8 | convolution fusion | flops 8627679232 | bytes 37781504 | tf_op jit(solution)/shard_map/td,efd->tef/dot_general | solution.py:440
  409.9 13.4 %convert_bitcast_fusion = bf16[4,2048,512]{1,2,0:T(8,128)(2,1)} fusion(bf16[1024,4,512]{0,2,1:T(8,128)(2,1)} %get-tuple-element.91, bf16[1024,2048]{1,0:T(8,128)(2,1)S(1)} %bitcast.257), kind=kOutput, calls=%fused_computation.7 | convolution fusion | flops 8594128896 | bytes 16777216 | tf_op jit(solution)/shard_map/td,tef->edf/dot_general | solution.py:440
  423.6 14.1 %convert_bitcast_fusion.1 = bf16[4,2048,512]{1,2,0:T(8,128)(2,1)} fusion(bf16[1024,4,512]{0,2,1:T(8,128)(2,1)} %get-tuple-element.92, bf16[1024,2048]{1,0:T(8,128)(2,1)} %bitcast.256), kind=kOutput, calls=%fused_computation.10 | convolution fusion | flops 8594128896 | bytes 16777216 | tf_op jit(solution)/shard_map/td,tef->edf/dot_general | solution.py:440
  439.8 12.9 %fusion.67 = f32[1024,2048,1]{1,0,2:T(8,128)S(1)} fusion(bf16[1024,4,512]{0,2,1:T(8,128)(2,1)} %get-tuple-element.91, bf16[4,2048,512]{2,1,0:T(8,128)(2,1)} %all-gather.4.cloned.1.call-done), kind=kOutput, calls=%fused_computation.175 | convolution fusion | flops 8589934592 | bytes 20971520 | tf_op jit(solution)/shard_map/tef,edf->td/dot_general | solution.py:440
  452.6 13.1 %fusion.1 = bf16[1024,2048]{1,0:T(8,128)(2,1)} fusion(f32[1024,2048,1]{1,0,2:T(8,128)S(1)} %fusion.67, bf16[1024,4,512]{0,2,1:T(8,128)(2,1)S(1)} %copy-done.64, bf16[4,2048,512]{2,1,0:T(8,128)(2,1)} %all-gather.8.cloned.1.call-done), kind=kOutput, calls=%fused_computation.2 | convolution fusion | flops 8594128896 | bytes 25165824 | tf_op jit(solution)/shard_map/tef,edf->td/dot_general | solution.py:440
  465.8 13.8 %reduce-scatter.7.cloned.1.call-done = bf16[128,2048]{1,0:T(8,128)(2,1)} async-done(((bf16[1024,2048]{1,0:T(8,128)(2,1)}), bf16[128,2048]{1,0:T(8,128)(2,1)}) %reduce-scatter.7.cloned.1.call-update) | async-done | bytes 524304 | tf_op jit(solution)/shard_map/reduce_scatter | solution.py:558
  479.6 53.6 %reduce_rows.1 = (f32[128,2048]{1,0:T(8,128)}, f32[16,128]{1,0:T(8,128)}) custom-call(bf16[8,128,2048]{2,1,0:T(8,128)(2,1)} %bitcast.279, f32[8,16,128]{2,1,0:T(8,128)} %bitcast_bitcast_fusion.note), custom_call_target="tpu_custom_call" | custom-call | bytes 200000000 | tf_op jit(solution)/shard_map/reduce_rows/pallas_call | solution.py:272
  537.6 49.1 %gather_rows.7 = bf16[8,128,2048]{2,1,0:T(8,128)(2,1)} custom-call(bf16[128,2048]{1,0:T(8,128)(2,1)} %fusion.60.refs_0_), custom_call_target="tpu_custom_call" | custom-call | bytes 200000000 | tf_op jit(solution)/shard_map/gather_rows/pallas_call | solution.py:153
  599.0 14.4 %multiply_convert_fusion = bf16[2,1024,1024]{1,2,0:T(8,128)(2,1)} fusion(f32[2,1024,1024]{1,2,0:T(8,128)} %copy-done.2, f32[2,1024]{1,0:T(2,128)S(1)} %copy-done.44, pred[1024,1024]{0,1:T(8,128)(4,1)S(1)} %copy-done.11, bf16[1024,2,128]{0,2,1:T(8,128)(2,1)} %bitcast.302, bf16[1024,2,128]{0,2,1:T(8,128)(2,1)} %bitcast.301), kind=kOutput, calls=%fused_computation.4 | convolution fusion | flops 1096813568 | bytes 14688256 | tf_op jit(solution)/shard_map/sub | solution.py:605
  620.7 11.2 %convolution_convert_fusion = bf16[4,512,2048]{2,1,0:T(8,128)(2,1)} fusion(bf16[1024,4,512]{0,2,1:T(8,128)(2,1)S(1)} %copy-done.63, bf16[1024,2048]{1,0:T(8,128)(2,1)S(1)} %bitcast.276), kind=kOutput, calls=%fused_computation.19 | convolution fusion | flops 8594128896 | bytes 16777216 | tf_op jit(solution)/shard_map/tef,td->efd/dot_general | solution.py:440
  631.9 9.5 %all-to-all-done.3 = bf16[8,256,512]{1,2,0:T(8,128)(2,1)} async-done(((bf16[8,256,512]{1,2,0:T(8,128)(2,1)}), bf16[8,256,512]{1,2,0:T(8,128)(2,1)}, u32[]{:S(2)}, u32[]{:S(2)}) %all-to-all-start.3) | async-done | bytes 2097184 | tf_op jit(solution)/shard_map/all_to_all | solution.py:485
  649.0 5.9 convolution_convert_fusion.2
  678.3 21.1 %small_sum.2 = f32[16,128]{1,0:T(8,128)} custom-call(f32[16,128]{1,0:T(8,128)} %reshape.463.values), custom_call_target="tpu_custom_call" | custom-call | bytes 10000000 | tf_op jit(solution)/shard_map/small_sum/pallas_call | solution.py:391
  705.4 30.5 %swap.3 = (bf16[128,2048]{1,0:T(8,128)(2,1)}, bf16[128,2048]{1,0:T(8,128)(2,1)}, bf16[128,2048]{1,0:T(8,128)(2,1)}) custom-call(bf16[8,128,256]{2,1,0:T(8,128)(2,1)} %bitcast.292, bf16[8,128,256]{2,1,0:T(8,128)(2,1)} %bitcast.291, bf16[8,128,256]{2,1,0:T(8,128)(2,1)} %bitcast.285), custom_call_target="tpu_custom_call" | custom-call | bytes 30000000 | tf_op jit(solution)/shard_map/swap/pallas_call | solution.py:339
  740.1 5.8 convolution_convert_fusion.1
  748.0 14.4 %all-to-all-start.5 = ((bf16[8,512,256]{2,1,0:T(8,128)(2,1)}), bf16[8,512,256]{2,1,0:T(8,128)(2,1)}, u32[]{:S(2)}, u32[]{:S(2)}) async-start(bf16[8,512,256]{2,1,0:T(8,128)(2,1)} %bitcast.265), calls=%async_computation.10 | async-start | bytes 4194304 | tf_op jit(solution)/shard_map/all_to_all | solution.py:485
  776.3 6.4 fusion.68
  782.8 6.5 convolution_add_fusion.2
  795.0 22.0 %small_sum.3 = f32[16,128]{1,0:T(8,128)} custom-call(f32[32,16,128]{2,1,0:T(8,128)} %bitcast.298), custom_call_target="tpu_custom_call" | custom-call | bytes 10000000 | tf_op jit(solution)/shard_map/small_sum/pallas_call | solution.py:391
  839.3 12.4 %all-to-all-done.6 = bf16[8,64,768]{2,1,0:T(8,128)(2,1)} async-done(((bf16[8,64,768]{2,1,0:T(8,128)(2,1)}), bf16[8,64,768]{2,1,0:T(8,128)(2,1)}, u32[]{:S(2)}, u32[]{:S(2)}) %all-to-all-start.6) | async-done | bytes 786464 | tf_op jit(solution)/shard_map/all_to_all | solution.py:485
  (296 shorter events, 184.3 us)
Async XLA Ops:
  7.2 281.9 %copy-start = (bf16[2048,16]{0,1:T(8,128)(2,1)S(1)}, bf16[2048,16]{0,1:T(8,128)(2,1)}, u32[]{:S(2)}) copy-start(bf16[2048,16]{0,1:T(8,128)(2,1)} %param.28) | copy-start | bytes 196612
  10.4 97.1 %all-to-all-start = ((bf16[8,256,512]{2,1,0:T(8,128)(2,1)}), bf16[8,256,512]{2,1,0:T(8,128)(2,1)S(1)}, u32[]{:S(2)}, u32[]{:S(2)}) async-start(bf16[8,256,512]{2,1,0:T(8,128)(2,1)} %bitcast.268), calls=%async_computation | async-start | bytes 4194304 | tf_op jit(solution)/shard_map/all_to_all | solution.py:485
  17.7 155.9 %all-gather.4.cloned.1.call-start = ((), (), s32[]{:S(2)}) async-start(), calls=%async_computation.13 | async-start | bytes 10485760 | tf_op jit(solution)/shard_map/all_gather | solution.py:488
  108.9 54.6 %all-to-all-start.1 = ((bf16[8,512,256]{2,1,0:T(8,128)(2,1)}), bf16[8,512,256]{2,1,0:T(8,128)(2,1)}, u32[]{:S(2)}, u32[]{:S(2)}) async-start(bf16[8,512,256]{2,1,0:T(8,128)(2,1)} %bitcast.287), calls=%async_computation.1 | async-start | bytes 4194304 | tf_op jit(solution)/shard_map/all_to_all | solution.py:485
  115.7 172.1 %all-gather.6.cloned.1.call-start = ((), (), s32[]{:S(2)}) async-start(), calls=%async_computation.14 | async-start | bytes 10485760 | tf_op jit(solution)/shard_map/all_gather | solution.py:488
  132.3 31.2 %copy-start.16 = (bf16[1024,2,128]{0,2,1:T(8,128)(2,1)}, bf16[1024,2,128]{0,2,1:T(8,128)(2,1)S(1)}, u32[]{:S(2)}) copy-start(bf16[1024,2,128]{0,2,1:T(8,128)(2,1)S(1)} %pad_maximum_fusion.5) | copy-start | bytes 1572868
  132.7 30.9 %copy-start.28 = (bf16[1024,2,128]{0,2,1:T(8,128)(2,1)}, bf16[1024,2,128]{0,2,1:T(8,128)(2,1)S(1)}, u32[]{:S(2)}) copy-start(bf16[1024,2,128]{0,2,1:T(8,128)(2,1)S(1)} %pad_maximum_fusion.4) | copy-start | bytes 1572868
  135.9 31.7 %copy-start.10 = (pred[1024,1024]{0,1:T(8,128)(4,1)}, pred[1024,1024]{0,1:T(8,128)(4,1)S(1)}, u32[]{:S(2)}) copy-start(pred[1024,1024]{0,1:T(8,128)(4,1)S(1)} %fusion.15) | copy-start | bytes 3145732
  138.8 32.1 %copy-start.29 = (bf16[1024,256]{0,1:T(8,128)(2,1)}, bf16[1024,256]{0,1:T(8,128)(2,1)S(1)}, u32[]{:S(2)}) copy-start(bf16[1024,256]{0,1:T(8,128)(2,1)S(1)} %convolution_convert_fusion.6) | copy-start | bytes 1572868
  173.6 17.5 %copy-start.24 = (bf16[2,128,1024]{2,1,0:T(8,128)(2,1)}, bf16[2,128,1024]{2,1,0:T(8,128)(2,1)S(1)}, u32[]{:S(2)}) copy-start(bf16[2,128,1024]{2,1,0:T(8,128)(2,1)S(1)} %convolution_convert_fusion.4) | copy-start | bytes 1572868
  193.5 94.2 %all-to-all-start.2 = ((bf16[8,256,512]{2,1,0:T(8,128)(2,1)}), bf16[8,256,512]{2,1,0:T(8,128)(2,1)S(1)}, u32[]{:S(2)}, u32[]{:S(2)}) async-start(bf16[8,256,512]{2,1,0:T(8,128)(2,1)} %bitcast.267), calls=%async_computation.2 | async-start | bytes 4194304 | tf_op jit(solution)/shard_map/all_to_all | solution.py:485
  201.4 154.4 %all-gather.8.cloned.1.call-start = ((), (), s32[]{:S(2)}) async-start(), calls=%async_computation.15 | async-start | bytes 10485760 | tf_op jit(solution)/shard_map/all_gather | solution.py:488
  289.1 190.5 %reduce-scatter.7.cloned.1.call-start = ((), (), s32[]{:S(2)}) async-start(), calls=%async_computation.16 | async-start | bytes 4718592 | tf_op jit(solution)/shard_map/reduce_scatter | solution.py:558
  387.8 198.9 %reduce-scatter.9.cloned.1.call-start = ((), (), s32[]{:S(2)}) async-start(), calls=%async_computation.17 | async-start | bytes 10485760 | tf_op jit(solution)/shard_map/reduce_scatter | solution.py:573
  388.0 21.8 %copy-start.5 = (bf16[8,128,2048]{2,1,0:T(8,128)(2,1)S(1)}, bf16[8,128,2048]{2,1,0:T(8,128)(2,1)}, u32[]{:S(2)}) copy-start(bf16[8,128,2048]{2,1,0:T(8,128)(2,1)} %gather_rows.5) | copy-start | bytes 12582916
  423.3 208.6 %reduce-scatter.11.cloned.1.call-start = ((), (), s32[]{:S(2)}) async-start(), calls=%async_computation.18 | async-start | bytes 10485760 | tf_op jit(solution)/shard_map/reduce_scatter | solution.py:573
  439.8 12.9 %copy-start.64 = (bf16[1024,4,512]{0,2,1:T(8,128)(2,1)S(1)}, bf16[1024,4,512]{0,2,1:T(8,128)(2,1)}, u32[]{:S(2)}) copy-start(bf16[1024,4,512]{0,2,1:T(8,128)(2,1)} %get-tuple-element.92) | copy-start | bytes 12582916
  465.8 68.8 %copy-start.4 = (f32[128,2048]{1,0:T(8,128)S(1)}, f32[128,2048]{1,0:T(8,128)}, u32[]{:S(2)}) copy-start(f32[128,2048]{1,0:T(8,128)} %copy-done.3) | copy-start | bytes 3145732
  465.8 68.8 %copy-start.35 = (f32[2048]{0:T(1024)S(1)}, f32[2048]{0:T(1024)}, u32[]{:S(2)}) copy-start(f32[2048]{0:T(1024)} %param.27) | copy-start | bytes 24580
  465.8 68.8 %copy-start.50 = (f32[128]{0:T(128)S(1)}, f32[128]{0:T(128)}, u32[]{:S(2)}) copy-start(f32[128]{0:T(128)} %copy-done.49) | copy-start | bytes 1540
  465.8 70.6 %copy-start.57 = (f32[128]{0:T(128)S(1)}, f32[128]{0:T(128)}, u32[]{:S(2)}) copy-start(f32[128]{0:T(128)} %copy-done.56) | copy-start | bytes 1540
  465.8 70.6 %copy-start.18 = (bf16[1,128,2048]{2,1,0:T(8,128)(2,1)S(1)}, bf16[1,128,2048]{2,1,0:T(8,128)(2,1)}, u32[]{:S(2)}) copy-start(bf16[1,128,2048]{2,1,0:T(8,128)(2,1)} %param.19) | copy-start | bytes 1572868
  536.4 53.5 %copy-start.54 = (f32[128]{0:T(128)}, f32[128]{0:T(128)S(1)}, u32[]{:S(2)}) copy-start(f32[128]{0:T(128)S(1)} %multiply_multiply_fusion.8) | copy-start | bytes 1540
  589.9 51.5 %all-to-all-start.3 = ((bf16[8,256,512]{1,2,0:T(8,128)(2,1)}), bf16[8,256,512]{1,2,0:T(8,128)(2,1)}, u32[]{:S(2)}, u32[]{:S(2)}) async-start(bf16[8,256,512]{1,2,0:T(8,128)(2,1)} %bitcast.269), calls=%async_computation.5 | async-start | bytes 4194304 | tf_op jit(solution)/shard_map/all_to_all | solution.py:485
  594.3 141.6 %reduce-scatter.13.cloned.1.call-start = ((), (), s32[]{:S(2)}) async-start(), calls=%async_computation.19 | async-start | bytes 10485760 | tf_op jit(solution)/shard_map/reduce_scatter | solution.py:573
  644.5 95.6 %all-to-all-start.4 = ((bf16[8,256,512]{1,2,0:T(8,128)(2,1)}), bf16[8,256,512]{1,2,0:T(8,128)(2,1)}, u32[]{:S(2)}, u32[]{:S(2)}) async-start(bf16[8,256,512]{1,2,0:T(8,128)(2,1)} %bitcast.264), calls=%async_computation.7 | async-start | bytes 4194304 | tf_op jit(solution)/shard_map/all_to_all | solution.py:485
  648.9 114.0 %reduce-scatter.17.cloned.1.call-start = ((), (), s32[]{:S(2)}) async-start(), calls=%async_computation.21 | async-start | bytes 1310720 | tf_op jit(solution)/shard_map/reduce_scatter | solution.py:640
  654.9 171.5 %reduce-scatter.15.cloned.1.call-start = ((), (), s32[]{:S(2)}) async-start(), calls=%async_computation.20 | async-start | bytes 3932160 | tf_op jit(solution)/shard_map/reduce_scatter | solution.py:573
  747.9 14.4 %copy-start.13 = (bf16[128,2048]{1,0:T(8,128)(2,1)S(1)}, bf16[128,2048]{1,0:T(8,128)(2,1)}, u32[]{:S(2)}) copy-start(bf16[128,2048]{1,0:T(8,128)(2,1)} %multiply_convert_fusion.4.refs_0_) | copy-start | bytes 1572868
  748.0 78.4 %all-to-all-start.5 = ((bf16[8,512,256]{2,1,0:T(8,128)(2,1)}), bf16[8,512,256]{2,1,0:T(8,128)(2,1)}, u32[]{:S(2)}, u32[]{:S(2)}) async-start(bf16[8,512,256]{2,1,0:T(8,128)(2,1)} %bitcast.265), calls=%async_computation.10 | async-start | bytes 4194304 | tf_op jit(solution)/shard_map/all_to_all | solution.py:485
  776.3 13.0 %slice-start.2 = ((s8[8388608]{0:T(1024)(128)(4,1)}), s8[4194304]{0:T(1024)(128)(4,1)S(1)}, s32[]{:S(2)}) async-start(s8[8388608]{0:T(1024)(128)(4,1)} %bitcast.261), calls=%async_computation.24 | async-start | bytes 8388608
  826.4 25.2 %all-to-all-start.6 = ((bf16[8,64,768]{2,1,0:T(8,128)(2,1)}), bf16[8,64,768]{2,1,0:T(8,128)(2,1)}, u32[]{:S(2)}, u32[]{:S(2)}) async-start(bf16[8,64,768]{2,1,0:T(8,128)(2,1)} %bitcast.299), calls=%async_computation.11 | async-start | bytes 1572864 | tf_op jit(solution)/shard_map/all_to_all | solution.py:485
  (53 other events, 284.6 us)
Sparse Core Ops, SparseCore 0:
  109.0 60.4 all-gather.3
  193.6 61.3 all-gather.5
  289.2 59.8 all-gather.7
  387.9 91.5 reduce-scatter.6
  482.0 71.0 reduce-scatter.8
  555.5 71.3 reduce-scatter.10
  641.6 70.6 reduce-scatter.12
  714.8 24.7 reduce-scatter.16
  748.1 47.4 reduce-scatter.14

commit v8 on v7

--- a/solution.py
+++ b/solution.py
@@ -620,16 +620,16 @@
 
     query_turn, key_turn = unturned(query_grad), unturned(key_grad)
     query_mix, key_mix = query_turn * query_gain_c, key_turn * key_gain_c
-    query_dots, key_dots, value_grad_b = together(
-        (query_mix * query_raw, key_mix * key_raw, value_grad_b)
+    query_gain_part = jnp.sum(query_turn * query_raw * query_scale, axis=0)
+    key_gain_part = jnp.sum(key_turn * key_raw * key_scale, axis=0)
+    query_dots, key_dots, value_grad_b, query_gain_part, key_gain_part = together(
+        (query_mix * query_raw, key_mix * key_raw, value_grad_b, query_gain_part, key_gain_part)
     )
     dots = row_sums(query_dots, key_dots, 7)
     query_raw_b = (
         query_scale * query_mix - query_raw * query_scale**3 * dots[0]
     ).astype(BF16)
     key_raw_b = (key_scale * key_mix - key_raw * key_scale**3 * dots[1]).astype(BF16)
-    query_gain_part = jnp.sum(query_turn * query_raw * query_scale, axis=0)
-    key_gain_part = jnp.sum(key_turn * key_raw * key_scale, axis=0)
     raw_grads = [query_raw_b, key_raw_b, value_grad_b]
     down_sum = down_sum.reshape(part, groups, cols).transpose(1, 0, 2)
     (query_own, key_own, value_own), raw_grads, up_sum, down_sum = together(
@@ -654,12 +654,13 @@
     small = small.reshape(-1, devices, width // devices).transpose(1, 0, 2).reshape(devices, -1)
     used = small.shape[1]
     small = jnp.pad(small, ((0, 0), (0, -used % 1024))).reshape(devices, -1, 128)
+    small, up_out, down_sum = together((small, slices_out(up_sum), down_sum))
     small = small_sum(small, ("group", "expert"), True, 9)
-    small, qkv_part, down_sum = together((small, qkv_part, down_sum))
+    small, qkv_part = together((small, qkv_part))
     qkv_part = exchange(qkv_part)
+    small = small.reshape(-1)[:used].reshape(-1, width // devices)
+    qkv_part, small = together((qkv_part, small))
     qkv_part = qkv_part.transpose(1, 0, 2).reshape(-1, groups, 3, cols).astype(F32)
-    small = small.reshape(-1)[:used]
-    small = small.reshape(-1, width // devices)
     return (
         result[None],
         input_grad[None],
@@ -673,7 +674,7 @@
         small[experts],
         small[:experts].T,
         slices_out(gate_sum),
-        slices_out(up_sum),
+        up_out,
         down_sum.reshape(local_experts, hidden_size, cols).astype(F32),
     )
 

time: 878 us -> 875 us (level)
    unnamed x145 -> x147, local copies, waits for them, and re-layouts: 18.6 us -> 17.9 us
  transfers between devices with their start and end apart: 16 -> 16, of which waited for: 4 -> 5; matrix products, arithmetic and copies ran while one was open for 32% -> 31% of each run, Pallas kernels for 44% -> 43%
where the time goes in v8:
time: 875 us; the launch traced here: 869 us
  Pallas kernels  391 us (45%)
  matrix products  225 us (26%)
  local copies, waits for them, and re-layouts  67.3 us (8%)
  waiting for transfers between devices  63 us (7%)
  other arithmetic  54.1 us (6%)
  starting transfers between devices  53.4 us (6%)
  between operations  15.7 us (2%)
    pallas_call x4, Pallas kernels, gather_rows(): pl.pallas_call(functools.partial(gather_kernel, nz, groups // nz, pieces,...  256 us
    dot_general x14, matrix products, ein(): return jnp.einsum(spec, *ops, preferred_element_type=F32)  146 us
    pallas_call x1, Pallas kernels, reduce_rows(): pl.pallas_call(functools.partial(reduce_kernel, nz, ny, pieces), name='re...  53.6 us
    all_to_all x7, starting transfers between devices, exchange(): return lax.all_to_all(w, 'group', 0, 0, tiled=True)  52 us
    all_to_all x7, waiting for transfers between devices, exchange(): return lax.all_to_all(w, 'group', 0, 0, tiled=True)  48.9 us
    pallas_call x2, Pallas kernels, swap(): pl.pallas_call(functools.partial(swap_kernel, groups, to_rows), name='swa...  44.1 us
    pallas_call x2, Pallas kernels, small_sum(): pl.pallas_call(functools.partial(small_sum_kernel, axes, scatter), name='...  37 us
    dot_general x8, matrix products, mm(): return jnp.dot(left, right, preferred_element_type=F32)  29.6 us
  transfers between devices with their start and end apart: 16, of which 5 were waited for; matrix products, arithmetic and copies ran while one was open for 31% of the time, Pallas kernels for 43%

profile of v8, /device:TPU:0, one launch (start us, length us, event | category | flops | bytes accessed | tf_op | source)
XLA Modules:
  0.0 868.7 jit_solution(10430897619868410769)
XLA Ops:
  10.4 7.3 all-to-all-start
  27.1 80.4 %gather_rows.4 = (bf16[8,128,2048]{2,1,0:T(8,128)(2,1)}, f32[8,19,128]{2,1,0:T(8,128)}) custom-call(bf16[128,2048]{1,0:T(8,128)(2,1)} %copy-done.7, f32[19,128]{1,0:T(8,128)} %pad_maximum_fusion.6.refs_1_), custom_call_target="tpu_custom_call" | custom-call | bytes 200000000 | tf_op jit(solution)/shard_map/gather_rows/pallas_call | solution.py:153
  108.9 6.8 all-to-all-start.1
  138.9 24.6 %all-to-all-done.1 = bf16[8,512,256]{2,1,0:T(8,128)(2,1)} async-done(((bf16[8,512,256]{2,1,0:T(8,128)(2,1)}), bf16[8,512,256]{2,1,0:T(8,128)(2,1)}, u32[]{:S(2)}, u32[]{:S(2)}) %all-to-all-start.1) | async-done | bytes 2097184 | tf_op jit(solution)/shard_map/all_to_all | solution.py:485
  174.7 13.6 %swap.2 = bf16[128,2048]{1,0:T(8,128)(2,1)} custom-call(bf16[8,128,256]{2,1,0:T(8,128)(2,1)} %bitcast.294), custom_call_target="tpu_custom_call" | custom-call | bytes 30000000 | tf_op jit(solution)/shard_map/swap/pallas_call | solution.py:339
  193.5 7.9 all-to-all-start.2
  201.7 5.9 multiply_reduce_fusion.6
  209.6 78.1 %gather_rows.5 = bf16[8,128,2048]{2,1,0:T(8,128)(2,1)} custom-call(bf16[128,2048]{1,0:T(8,128)(2,1)} %multiply_convert_fusion.4.refs_0_), custom_call_target="tpu_custom_call" | custom-call | bytes 200000000 | tf_op jit(solution)/shard_map/gather_rows/pallas_call | solution.py:153
  292.7 14.6 %fusion.66 = f32[1024,4,512]{0,2,1:T(8,128)} fusion(bf16[1024,2048,1]{1,0,2:T(8,128)(2,1)} %bitcast.255, bf16[4,2048,512]{2,1,0:T(8,128)(2,1)} %all-gather.4.cloned.1.call-done), kind=kOutput, calls=%fused_computation.175 | convolution fusion | flops 8589934592 | bytes 20971520 | tf_op jit(solution)/shard_map/td,edf->tef/dot_general | solution.py:440
  307.3 48.4 %gather_rows.6 = bf16[8,128,2048]{2,1,0:T(8,128)(2,1)} custom-call(bf16[128,2048]{1,0:T(8,128)(2,1)} %bitcast.273), custom_call_target="tpu_custom_call" | custom-call | bytes 200000000 | tf_op jit(solution)/shard_map/gather_rows/pallas_call | solution.py:153
  355.8 17.9 %multiply_convert_fusion.3 = (bf16[1024,4,512]{0,2,1:T(8,128)(2,1)}, f32[1024,4,512]{0,2,1:T(8,128)}) fusion(f32[1024,4]{0,1:T(4,128)S(1)} %bitcast.323, f32[1024,4,512]{0,2,1:T(8,128)} %fusion.66, bf16[1024,2048,1]{1,0,2:T(8,128)(2,1)} %bitcast.256, bf16[4,2048,512]{2,1,0:T(8,128)(2,1)} %all-gather.8.cloned.1.call-done), kind=kOutput, calls=%fused_computation.12 | convolution fusion | flops 8604614656 | bytes 33570816 | tf_op jit(solution)/shard_map/td,edf->tef/dot_general | solution.py:440
  373.7 14.1 %bitcast_convert_fusion = bf16[1024,2048]{1,0:T(8,128)(2,1)} fusion(bf16[1024,4,512]{0,2,1:T(8,128)(2,1)} %get-tuple-element.111, bf16[4,512,2048]{2,1,0:T(8,128)(2,1)} %all-gather.6.cloned.1.call-done), kind=kOutput, calls=%fused_computation.3 | convolution fusion | flops 8592031744 | bytes 16777216 | tf_op jit(solution)/shard_map/tef,efd->td/dot_general | solution.py:440
  388.1 21.8 %multiply_reduce_fusion.1 = (f32[1024,4]{0,1:T(4,128)S(1)}, bf16[1024,4,512]{0,2,1:T(8,128)(2,1)}, bf16[1024,4,512]{0,2,1:T(8,128)(2,1)}) fusion(f32[1024,4,512]{0,2,1:T(8,128)} %get-tuple-element.197, f32[1024,4,512]{0,2,1:T(8,128)} %fusion.66, f32[1024,4]{0,1:T(4,128)S(1)} %bitcast.324, bf16[4,512,2048]{2,1,0:T(8,128)(2,1)} %all-gather.6.cloned.1.call-done, ...), kind=kOutput, calls=%fused_computation.8 | convolution fusion | flops 8627679232 | bytes 37781504 | tf_op jit(solution)/shard_map/td,efd->tef/dot_general | solution.py:440
  409.9 13.4 %convert_bitcast_fusion = bf16[4,2048,512]{1,2,0:T(8,128)(2,1)} fusion(bf16[1024,4,512]{0,2,1:T(8,128)(2,1)} %get-tuple-element.97, bf16[1024,2048]{1,0:T(8,128)(2,1)S(1)} %bitcast.258), kind=kOutput, calls=%fused_computation.7 | convolution fusion | flops 8594128896 | bytes 16777216 | tf_op jit(solution)/shard_map/td,tef->edf/dot_general | solution.py:440
  423.6 14.0 %convert_bitcast_fusion.1 = bf16[4,2048,512]{1,2,0:T(8,128)(2,1)} fusion(bf16[1024,4,512]{0,2,1:T(8,128)(2,1)} %get-tuple-element.98, bf16[1024,2048]{1,0:T(8,128)(2,1)} %bitcast.257), kind=kOutput, calls=%fused_computation.10 | convolution fusion | flops 8594128896 | bytes 16777216 | tf_op jit(solution)/shard_map/td,tef->edf/dot_general | solution.py:440
  439.8 12.9 %fusion.67 = f32[1024,2048,1]{1,0,2:T(8,128)S(1)} fusion(bf16[1024,4,512]{0,2,1:T(8,128)(2,1)} %get-tuple-element.97, bf16[4,2048,512]{2,1,0:T(8,128)(2,1)} %all-gather.4.cloned.1.call-done), kind=kOutput, calls=%fused_computation.176 | convolution fusion | flops 8589934592 | bytes 20971520 | tf_op jit(solution)/shard_map/tef,edf->td/dot_general | solution.py:440
  452.6 13.1 %fusion.1 = bf16[1024,2048]{1,0:T(8,128)(2,1)} fusion(f32[1024,2048,1]{1,0,2:T(8,128)S(1)} %fusion.67, bf16[1024,4,512]{0,2,1:T(8,128)(2,1)S(1)} %copy-done.65, bf16[4,2048,512]{2,1,0:T(8,128)(2,1)} %all-gather.8.cloned.1.call-done), kind=kOutput, calls=%fused_computation.2 | convolution fusion | flops 8594128896 | bytes 25165824 | tf_op jit(solution)/shard_map/tef,edf->td/dot_general | solution.py:440
  465.8 13.8 %reduce-scatter.7.cloned.1.call-done = bf16[128,2048]{1,0:T(8,128)(2,1)} async-done(((bf16[1024,2048]{1,0:T(8,128)(2,1)}), bf16[128,2048]{1,0:T(8,128)(2,1)}) %reduce-scatter.7.cloned.1.call-update) | async-done | bytes 524304 | tf_op jit(solution)/shard_map/reduce_scatter | solution.py:558
  479.5 53.6 %reduce_rows.1 = (f32[128,2048]{1,0:T(8,128)}, f32[16,128]{1,0:T(8,128)}) custom-call(bf16[8,128,2048]{2,1,0:T(8,128)(2,1)} %bitcast.280, f32[8,16,128]{2,1,0:T(8,128)} %bitcast_bitcast_fusion.note), custom_call_target="tpu_custom_call" | custom-call | bytes 200000000 | tf_op jit(solution)/shard_map/reduce_rows/pallas_call | solution.py:272
  537.6 49.1 %gather_rows.7 = bf16[8,128,2048]{2,1,0:T(8,128)(2,1)} custom-call(bf16[128,2048]{1,0:T(8,128)(2,1)} %fusion.60.refs_0_), custom_call_target="tpu_custom_call" | custom-call | bytes 200000000 | tf_op jit(solution)/shard_map/gather_rows/pallas_call | solution.py:153
  599.0 14.3 %multiply_convert_fusion = bf16[2,1024,1024]{1,2,0:T(8,128)(2,1)} fusion(f32[2,1024,1024]{1,2,0:T(8,128)} %copy-done.2, f32[2,1024]{1,0:T(2,128)S(1)} %copy-done.44, pred[1024,1024]{0,1:T(8,128)(4,1)S(1)} %copy-done.11, bf16[1024,2,128]{0,2,1:T(8,128)(2,1)} %bitcast.303, bf16[1024,2,128]{0,2,1:T(8,128)(2,1)} %bitcast.302), kind=kOutput, calls=%fused_computation.4 | convolution fusion | flops 1096813568 | bytes 14688256 | tf_op jit(solution)/shard_map/sub | solution.py:605
  619.9 11.1 %convolution_convert_fusion = bf16[4,512,2048]{2,1,0:T(8,128)(2,1)} fusion(bf16[1024,4,512]{0,2,1:T(8,128)(2,1)S(1)} %copy-done.64, bf16[1024,2048]{1,0:T(8,128)(2,1)S(1)} %bitcast.279), kind=kOutput, calls=%fused_computation.19 | convolution fusion | flops 8594128896 | bytes 16777216 | tf_op jit(solution)/shard_map/tef,td->efd/dot_general | solution.py:440
  631.0 10.4 %all-to-all-done.3 = bf16[8,256,512]{1,2,0:T(8,128)(2,1)} async-done(((bf16[8,256,512]{1,2,0:T(8,128)(2,1)}), bf16[8,256,512]{1,2,0:T(8,128)(2,1)}, u32[]{:S(2)}, u32[]{:S(2)}) %all-to-all-start.3) | async-done | bytes 2097184 | tf_op jit(solution)/shard_map/all_to_all | solution.py:485
  672.9 26.5 %small_sum.2 = f32[16,128]{1,0:T(8,128)} custom-call(f32[16,128]{1,0:T(8,128)} %reshape.462.values), custom_call_target="tpu_custom_call" | custom-call | bytes 10000000 | tf_op jit(solution)/shard_map/small_sum/pallas_call | solution.py:391
  705.5 30.5 %swap.3 = (bf16[128,2048]{1,0:T(8,128)(2,1)}, bf16[128,2048]{1,0:T(8,128)(2,1)}, bf16[128,2048]{1,0:T(8,128)(2,1)}) custom-call(bf16[8,128,256]{2,1,0:T(8,128)(2,1)} %bitcast.284, bf16[8,128,256]{2,1,0:T(8,128)(2,1)} %bitcast.285, bf16[8,128,256]{2,1,0:T(8,128)(2,1)} %bitcast.288), custom_call_target="tpu_custom_call" | custom-call | bytes 30000000 | tf_op jit(solution)/shard_map/swap/pallas_call | solution.py:339
  740.2 5.8 convolution_convert_fusion.1
  748.0 14.1 %all-to-all-start.5 = ((bf16[8,512,256]{2,1,0:T(8,128)(2,1)}), bf16[8,512,256]{2,1,0:T(8,128)(2,1)}, u32[]{:S(2)}, u32[]{:S(2)}) async-start(bf16[8,512,256]{2,1,0:T(8,128)(2,1)} %bitcast.265), calls=%async_computation.9 | async-start | bytes 4194304 | tf_op jit(solution)/shard_map/all_to_all | solution.py:485
  769.7 6.4 fusion.68
  776.2 6.5 convolution_add_fusion.2
  797.7 11.8 %all-to-all-done.5 = bf16[8,512,256]{2,1,0:T(8,128)(2,1)} async-done(((bf16[8,512,256]{2,1,0:T(8,128)(2,1)}), bf16[8,512,256]{2,1,0:T(8,128)(2,1)}, u32[]{:S(2)}, u32[]{:S(2)}) %all-to-all-start.5) | async-done | bytes 2097184 | tf_op jit(solution)/shard_map/all_to_all | solution.py:485
  809.5 10.5 %small_sum.3 = f32[16,128]{1,0:T(8,128)} custom-call(f32[32,16,128]{2,1,0:T(8,128)} %bitcast.299), custom_call_target="tpu_custom_call" | custom-call | bytes 10000000 | tf_op jit(solution)/shard_map/small_sum/pallas_call | solution.py:391
  820.0 7.2 all-to-all-start.6
  (297 shorter events, 186.6 us)
Async XLA Ops:
  7.2 282.0 %copy-start = (bf16[2048,16]{0,1:T(8,128)(2,1)S(1)}, bf16[2048,16]{0,1:T(8,128)(2,1)}, u32[]{:S(2)}) copy-start(bf16[2048,16]{0,1:T(8,128)(2,1)} %param.28) | copy-start | bytes 196612
  10.4 97.1 %all-to-all-start = ((bf16[8,256,512]{2,1,0:T(8,128)(2,1)}), bf16[8,256,512]{2,1,0:T(8,128)(2,1)S(1)}, u32[]{:S(2)}, u32[]{:S(2)}) async-start(bf16[8,256,512]{2,1,0:T(8,128)(2,1)} %bitcast.269), calls=%async_computation | async-start | bytes 4194304 | tf_op jit(solution)/shard_map/all_to_all | solution.py:485
  17.7 155.9 %all-gather.4.cloned.1.call-start = ((), (), s32[]{:S(2)}) async-start(), calls=%async_computation.13 | async-start | bytes 10485760 | tf_op jit(solution)/shard_map/all_gather | solution.py:488
  108.9 54.6 %all-to-all-start.1 = ((bf16[8,512,256]{2,1,0:T(8,128)(2,1)}), bf16[8,512,256]{2,1,0:T(8,128)(2,1)}, u32[]{:S(2)}, u32[]{:S(2)}) async-start(bf16[8,512,256]{2,1,0:T(8,128)(2,1)} %bitcast.290), calls=%async_computation.1 | async-start | bytes 4194304 | tf_op jit(solution)/shard_map/all_to_all | solution.py:485
  115.7 172.1 %all-gather.6.cloned.1.call-start = ((), (), s32[]{:S(2)}) async-start(), calls=%async_computation.14 | async-start | bytes 10485760 | tf_op jit(solution)/shard_map/all_gather | solution.py:488
  132.4 31.1 %copy-start.28 = (bf16[1024,2,128]{0,2,1:T(8,128)(2,1)}, bf16[1024,2,128]{0,2,1:T(8,128)(2,1)S(1)}, u32[]{:S(2)}) copy-start(bf16[1024,2,128]{0,2,1:T(8,128)(2,1)S(1)} %pad_maximum_fusion.4) | copy-start | bytes 1572868
  132.7 30.8 %copy-start.16 = (bf16[1024,2,128]{0,2,1:T(8,128)(2,1)}, bf16[1024,2,128]{0,2,1:T(8,128)(2,1)S(1)}, u32[]{:S(2)}) copy-start(bf16[1024,2,128]{0,2,1:T(8,128)(2,1)S(1)} %pad_maximum_fusion.5) | copy-start | bytes 1572868
  136.0 31.6 %copy-start.10 = (pred[1024,1024]{0,1:T(8,128)(4,1)}, pred[1024,1024]{0,1:T(8,128)(4,1)S(1)}, u32[]{:S(2)}) copy-start(pred[1024,1024]{0,1:T(8,128)(4,1)S(1)} %fusion.15) | copy-start | bytes 3145732
  138.9 32.0 %copy-start.30 = (bf16[1024,256]{0,1:T(8,128)(2,1)}, bf16[1024,256]{0,1:T(8,128)(2,1)S(1)}, u32[]{:S(2)}) copy-start(bf16[1024,256]{0,1:T(8,128)(2,1)S(1)} %convolution_convert_fusion.6) | copy-start | bytes 1572868
  173.6 17.5 %copy-start.25 = (bf16[2,128,1024]{2,1,0:T(8,128)(2,1)}, bf16[2,128,1024]{2,1,0:T(8,128)(2,1)S(1)}, u32[]{:S(2)}) copy-start(bf16[2,128,1024]{2,1,0:T(8,128)(2,1)S(1)} %convolution_convert_fusion.4) | copy-start | bytes 1572868
  193.5 94.2 %all-to-all-start.2 = ((bf16[8,256,512]{2,1,0:T(8,128)(2,1)}), bf16[8,256,512]{2,1,0:T(8,128)(2,1)S(1)}, u32[]{:S(2)}, u32[]{:S(2)}) async-start(bf16[8,256,512]{2,1,0:T(8,128)(2,1)} %bitcast.268), calls=%async_computation.2 | async-start | bytes 4194304 | tf_op jit(solution)/shard_map/all_to_all | solution.py:485
  201.4 154.4 %all-gather.8.cloned.1.call-start = ((), (), s32[]{:S(2)}) async-start(), calls=%async_computation.15 | async-start | bytes 10485760 | tf_op jit(solution)/shard_map/all_gather | solution.py:488
  289.1 190.5 %reduce-scatter.7.cloned.1.call-start = ((), (), s32[]{:S(2)}) async-start(), calls=%async_computation.16 | async-start | bytes 4718592 | tf_op jit(solution)/shard_map/reduce_scatter | solution.py:558
  387.8 198.9 %reduce-scatter.9.cloned.1.call-start = ((), (), s32[]{:S(2)}) async-start(), calls=%async_computation.17 | async-start | bytes 10485760 | tf_op jit(solution)/shard_map/reduce_scatter | solution.py:573
  388.0 21.8 %copy-start.5 = (bf16[8,128,2048]{2,1,0:T(8,128)(2,1)S(1)}, bf16[8,128,2048]{2,1,0:T(8,128)(2,1)}, u32[]{:S(2)}) copy-start(bf16[8,128,2048]{2,1,0:T(8,128)(2,1)} %gather_rows.5) | copy-start | bytes 12582916
  423.3 207.7 %reduce-scatter.11.cloned.1.call-start = ((), (), s32[]{:S(2)}) async-start(), calls=%async_computation.18 | async-start | bytes 10485760 | tf_op jit(solution)/shard_map/reduce_scatter | solution.py:573
  465.8 68.8 %copy-start.4 = (f32[128,2048]{1,0:T(8,128)S(1)}, f32[128,2048]{1,0:T(8,128)}, u32[]{:S(2)}) copy-start(f32[128,2048]{1,0:T(8,128)} %copy-done.3) | copy-start | bytes 3145732
  465.8 68.9 %copy-start.36 = (f32[2048]{0:T(1024)S(1)}, f32[2048]{0:T(1024)}, u32[]{:S(2)}) copy-start(f32[2048]{0:T(1024)} %param.27) | copy-start | bytes 24580
  465.8 68.9 %copy-start.51 = (f32[128]{0:T(128)S(1)}, f32[128]{0:T(128)}, u32[]{:S(2)}) copy-start(f32[128]{0:T(128)} %copy-done.50) | copy-start | bytes 1540
  465.8 70.6 %copy-start.58 = (f32[128]{0:T(128)S(1)}, f32[128]{0:T(128)}, u32[]{:S(2)}) copy-start(f32[128]{0:T(128)} %copy-done.57) | copy-start | bytes 1540
  465.8 70.6 %copy-start.17 = (bf16[1,128,2048]{2,1,0:T(8,128)(2,1)S(1)}, bf16[1,128,2048]{2,1,0:T(8,128)(2,1)}, u32[]{:S(2)}) copy-start(bf16[1,128,2048]{2,1,0:T(8,128)(2,1)} %param.19) | copy-start | bytes 1572868
  536.4 53.5 %copy-start.55 = (f32[128]{0:T(128)}, f32[128]{0:T(128)S(1)}, u32[]{:S(2)}) copy-start(f32[128]{0:T(128)S(1)} %multiply_multiply_fusion.8) | copy-start | bytes 1540
  589.9 51.5 %all-to-all-start.3 = ((bf16[8,256,512]{1,2,0:T(8,128)(2,1)}), bf16[8,256,512]{1,2,0:T(8,128)(2,1)}, u32[]{:S(2)}, u32[]{:S(2)}) async-start(bf16[8,256,512]{1,2,0:T(8,128)(2,1)} %bitcast.270), calls=%async_computation.5 | async-start | bytes 4194304 | tf_op jit(solution)/shard_map/all_to_all | solution.py:485
  594.4 141.6 %reduce-scatter.13.cloned.1.call-start = ((), (), s32[]{:S(2)}) async-start(), calls=%async_computation.19 | async-start | bytes 10485760 | tf_op jit(solution)/shard_map/reduce_scatter | solution.py:573
  644.6 95.6 %all-to-all-start.4 = ((bf16[8,256,512]{1,2,0:T(8,128)(2,1)}), bf16[8,256,512]{1,2,0:T(8,128)(2,1)}, u32[]{:S(2)}, u32[]{:S(2)}) async-start(bf16[8,256,512]{1,2,0:T(8,128)(2,1)} %bitcast.267), calls=%async_computation.7 | async-start | bytes 4194304 | tf_op jit(solution)/shard_map/all_to_all | solution.py:485
  649.0 171.0 %reduce-scatter.15.cloned.1.call-start = ((), (), s32[]{:S(2)}) async-start(), calls=%async_computation.20 | async-start | bytes 3932160 | tf_op jit(solution)/shard_map/reduce_scatter | solution.py:573
  748.0 14.4 %copy-start.13 = (bf16[128,2048]{1,0:T(8,128)(2,1)S(1)}, bf16[128,2048]{1,0:T(8,128)(2,1)}, u32[]{:S(2)}) copy-start(bf16[128,2048]{1,0:T(8,128)(2,1)} %multiply_convert_fusion.4.refs_0_) | copy-start | bytes 1572868
  748.0 15.0 %copy-start.26 = (bf16[2,128,1024]{2,1,0:T(8,128)(2,1)S(1)}, bf16[2,128,1024]{2,1,0:T(8,128)(2,1)}, u32[]{:S(2)}) copy-start(bf16[2,128,1024]{2,1,0:T(8,128)(2,1)} %copy-done.25) | copy-start | bytes 1572868
  748.0 61.5 %all-to-all-start.5 = ((bf16[8,512,256]{2,1,0:T(8,128)(2,1)}), bf16[8,512,256]{2,1,0:T(8,128)(2,1)}, u32[]{:S(2)}, u32[]{:S(2)}) async-start(bf16[8,512,256]{2,1,0:T(8,128)(2,1)} %bitcast.265), calls=%async_computation.9 | async-start | bytes 4194304 | tf_op jit(solution)/shard_map/all_to_all | solution.py:485
  762.1 65.1 %reduce-scatter.17.cloned.1.call-start = ((), (), s32[]{:S(2)}) async-start(), calls=%async_computation.21 | async-start | bytes 1310720 | tf_op jit(solution)/shard_map/reduce_scatter | solution.py:640
  769.7 13.0 %slice-start.2 = ((s8[8388608]{0:T(1024)(128)(4,1)}), s8[4194304]{0:T(1024)(128)(4,1)S(1)}, s32[]{:S(2)}) async-start(s8[8388608]{0:T(1024)(128)(4,1)} %bitcast.262), calls=%async_computation.24 | async-start | bytes 8388608
  820.0 27.6 %all-to-all-start.6 = ((bf16[8,64,768]{2,1,0:T(8,128)(2,1)}), bf16[8,64,768]{2,1,0:T(8,128)(2,1)}, u32[]{:S(2)}, u32[]{:S(2)}) async-start(bf16[8,64,768]{2,1,0:T(8,128)(2,1)} %bitcast.300), calls=%async_computation.11 | async-start | bytes 1572864 | tf_op jit(solution)/shard_map/all_to_all | solution.py:485
  (54 other events, 282.2 us)
Sparse Core Ops, SparseCore 0:
  109.0 60.4 all-gather.3
  193.6 61.3 all-gather.5
  289.2 59.7 all-gather.7
  387.9 91.5 reduce-scatter.6
  482.0 71.0 reduce-scatter.8
  555.5 71.3 reduce-scatter.10
  641.6 70.6 reduce-scatter.12
  748.1 47.5 reduce-scatter.14
  798.2 26.7 reduce-scatter.16

commit v9 on v8

--- a/solution.py
+++ b/solution.py
@@ -660,14 +660,17 @@
     qkv_part = exchange(qkv_part)
     small = small.reshape(-1)[:used].reshape(-1, width // devices)
     qkv_part, small = together((qkv_part, small))
-    qkv_part = qkv_part.transpose(1, 0, 2).reshape(-1, groups, 3, cols).astype(F32)
+    query_w_grad, key_w_grad, value_w_grad = [
+        qkv_part[:, :, i * cols : (i + 1) * cols].transpose(1, 0, 2).reshape(-1, width).astype(F32)
+        for i in range(3)
+    ]
     return (
         result[None],
         input_grad[None],
         small[experts + 1],
-        qkv_part[:, :, 0].reshape(-1, width),
-        qkv_part[:, :, 1].reshape(-1, width),
-        qkv_part[:, :, 2].reshape(-1, width),
+        query_w_grad,
+        key_w_grad,
+        value_w_grad,
         small[experts + 2],
         small[experts + 3],
         out_w_grad.astype(F32),

time: 875 us -> 865 us (0.989)
  local copies, waits for them, and re-layouts: 67.3 us -> 58.2 us
    unnamed x147 -> x144, local copies, waits for them, and re-layouts: 17.9 us -> 14.9 us
  transfers between devices with their start and end apart: 16 -> 16, of which waited for: 5 -> 5; matrix products, arithmetic and copies ran while one was open for 31% -> 32% of each run, Pallas kernels for 43% -> 44%
where the time goes in v9:
time: 865 us; the launch traced here: 859 us
  Pallas kernels  391 us (45%)
  matrix products  225 us (26%)
  waiting for transfers between devices  63.2 us (7%)
  local copies, waits for them, and re-layouts  58.2 us (7%)
  other arithmetic  54.1 us (6%)
  starting transfers between devices  53 us (6%)
  between operations  15.4 us (2%)
    pallas_call x4, Pallas kernels, gather_rows(): pl.pallas_call(functools.partial(gather_kernel, nz, groups // nz, pieces,...  256 us
    dot_general x14, matrix products, ein(): return jnp.einsum(spec, *ops, preferred_element_type=F32)  146 us
    pallas_call x1, Pallas kernels, reduce_rows(): pl.pallas_call(functools.partial(reduce_kernel, nz, ny, pieces), name='re...  53.6 us
    all_to_all x7, starting transfers between devices, exchange(): return lax.all_to_all(w, 'group', 0, 0, tiled=True)  51.6 us
    all_to_all x7, waiting for transfers between devices, exchange(): return lax.all_to_all(w, 'group', 0, 0, tiled=True)  49.1 us
    pallas_call x2, Pallas kernels, swap(): pl.pallas_call(functools.partial(swap_kernel, groups, to_rows), name='swa...  44.1 us
    pallas_call x2, Pallas kernels, small_sum(): pl.pallas_call(functools.partial(small_sum_kernel, axes, scatter), name='...  37 us
    dot_general x8, matrix products, mm(): return jnp.dot(left, right, preferred_element_type=F32)  29.6 us
  transfers between devices with their start and end apart: 16, of which 5 were waited for; matrix products, arithmetic and copies ran while one was open for 32% of the time, Pallas kernels for 44%

profile of v9, /device:TPU:0, one launch (start us, length us, event | category | flops | bytes accessed | tf_op | source)
XLA Modules:
  0.0 859.1 jit_solution(1923544553660193404)
XLA Ops:
  10.4 7.3 all-to-all-start
  27.1 80.4 %gather_rows.4 = (bf16[8,128,2048]{2,1,0:T(8,128)(2,1)}, f32[8,19,128]{2,1,0:T(8,128)}) custom-call(bf16[128,2048]{1,0:T(8,128)(2,1)} %copy-done.7, f32[19,128]{1,0:T(8,128)} %pad_maximum_fusion.6.refs_1_), custom_call_target="tpu_custom_call" | custom-call | bytes 200000000 | tf_op jit(solution)/shard_map/gather_rows/pallas_call | solution.py:153
  108.9 6.8 all-to-all-start.1
  138.8 24.7 %all-to-all-done.1 = bf16[8,512,256]{2,1,0:T(8,128)(2,1)} async-done(((bf16[8,512,256]{2,1,0:T(8,128)(2,1)}), bf16[8,512,256]{2,1,0:T(8,128)(2,1)}, u32[]{:S(2)}, u32[]{:S(2)}) %all-to-all-start.1) | async-done | bytes 2097184 | tf_op jit(solution)/shard_map/all_to_all | solution.py:485
  174.6 13.6 %swap.2 = bf16[128,2048]{1,0:T(8,128)(2,1)} custom-call(bf16[8,128,256]{2,1,0:T(8,128)(2,1)} %bitcast.298), custom_call_target="tpu_custom_call" | custom-call | bytes 30000000 | tf_op jit(solution)/shard_map/swap/pallas_call | solution.py:339
  193.5 7.9 all-to-all-start.2
  201.6 5.9 multiply_reduce_fusion.6
  209.5 78.2 %gather_rows.5 = bf16[8,128,2048]{2,1,0:T(8,128)(2,1)} custom-call(bf16[128,2048]{1,0:T(8,128)(2,1)} %multiply_convert_fusion.4.refs_0_), custom_call_target="tpu_custom_call" | custom-call | bytes 200000000 | tf_op jit(solution)/shard_map/gather_rows/pallas_call | solution.py:153
  292.7 14.6 %fusion.66 = f32[1024,4,512]{0,2,1:T(8,128)} fusion(bf16[1024,2048,1]{1,0,2:T(8,128)(2,1)} %bitcast.259, bf16[4,2048,512]{2,1,0:T(8,128)(2,1)} %all-gather.4.cloned.1.call-done), kind=kOutput, calls=%fused_computation.174 | convolution fusion | flops 8589934592 | bytes 20971520 | tf_op jit(solution)/shard_map/td,edf->tef/dot_general | solution.py:440
  307.3 48.4 %gather_rows.6 = bf16[8,128,2048]{2,1,0:T(8,128)(2,1)} custom-call(bf16[128,2048]{1,0:T(8,128)(2,1)} %bitcast.277), custom_call_target="tpu_custom_call" | custom-call | bytes 200000000 | tf_op jit(solution)/shard_map/gather_rows/pallas_call | solution.py:153
  355.7 17.9 %multiply_convert_fusion.3 = (bf16[1024,4,512]{0,2,1:T(8,128)(2,1)}, f32[1024,4,512]{0,2,1:T(8,128)}) fusion(f32[1024,4]{0,1:T(4,128)S(1)} %bitcast.324, f32[1024,4,512]{0,2,1:T(8,128)} %fusion.66, bf16[1024,2048,1]{1,0,2:T(8,128)(2,1)} %bitcast.260, bf16[4,2048,512]{2,1,0:T(8,128)(2,1)} %all-gather.8.cloned.1.call-done), kind=kOutput, calls=%fused_computation.12 | convolution fusion | flops 8604614656 | bytes 33570816 | tf_op jit(solution)/shard_map/td,edf->tef/dot_general | solution.py:440
  373.6 14.1 %bitcast_convert_fusion = bf16[1024,2048]{1,0:T(8,128)(2,1)} fusion(bf16[1024,4,512]{0,2,1:T(8,128)(2,1)} %get-tuple-element.111, bf16[4,512,2048]{2,1,0:T(8,128)(2,1)} %all-gather.6.cloned.1.call-done), kind=kOutput, calls=%fused_computation.3 | convolution fusion | flops 8592031744 | bytes 16777216 | tf_op jit(solution)/shard_map/tef,efd->td/dot_general | solution.py:440
  387.9 21.8 %multiply_reduce_fusion.1 = (f32[1024,4]{0,1:T(4,128)S(1)}, bf16[1024,4,512]{0,2,1:T(8,128)(2,1)}, bf16[1024,4,512]{0,2,1:T(8,128)(2,1)}) fusion(f32[1024,4,512]{0,2,1:T(8,128)} %get-tuple-element.197, f32[1024,4,512]{0,2,1:T(8,128)} %fusion.66, f32[1024,4]{0,1:T(4,128)S(1)} %bitcast.325, bf16[4,512,2048]{2,1,0:T(8,128)(2,1)} %all-gather.6.cloned.1.call-done, ...), kind=kOutput, calls=%fused_computation.8 | convolution fusion | flops 8627679232 | bytes 37781504 | tf_op jit(solution)/shard_map/td,efd->tef/dot_general | solution.py:440
  409.8 13.4 %convert_bitcast_fusion = bf16[4,2048,512]{1,2,0:T(8,128)(2,1)} fusion(bf16[1024,4,512]{0,2,1:T(8,128)(2,1)} %get-tuple-element.97, bf16[1024,2048]{1,0:T(8,128)(2,1)S(1)} %bitcast.262), kind=kOutput, calls=%fused_computation.7 | convolution fusion | flops 8594128896 | bytes 16777216 | tf_op jit(solution)/shard_map/td,tef->edf/dot_general | solution.py:440
  423.5 14.1 %convert_bitcast_fusion.1 = bf16[4,2048,512]{1,2,0:T(8,128)(2,1)} fusion(bf16[1024,4,512]{0,2,1:T(8,128)(2,1)} %get-tuple-element.98, bf16[1024,2048]{1,0:T(8,128)(2,1)} %bitcast.261), kind=kOutput, calls=%fused_computation.10 | convolution fusion | flops 8594128896 | bytes 16777216 | tf_op jit(solution)/shard_map/td,tef->edf/dot_general | solution.py:440
  439.6 12.8 %fusion.67 = f32[1024,2048,1]{1,0,2:T(8,128)S(1)} fusion(bf16[1024,4,512]{0,2,1:T(8,128)(2,1)} %get-tuple-element.97, bf16[4,2048,512]{2,1,0:T(8,128)(2,1)} %all-gather.4.cloned.1.call-done), kind=kOutput, calls=%fused_computation.175 | convolution fusion | flops 8589934592 | bytes 20971520 | tf_op jit(solution)/shard_map/tef,edf->td/dot_general | solution.py:440
  452.5 13.1 %fusion.1 = bf16[1024,2048]{1,0:T(8,128)(2,1)} fusion(f32[1024,2048,1]{1,0,2:T(8,128)S(1)} %fusion.67, bf16[1024,4,512]{0,2,1:T(8,128)(2,1)S(1)} %copy-done.65, bf16[4,2048,512]{2,1,0:T(8,128)(2,1)} %all-gather.8.cloned.1.call-done), kind=kOutput, calls=%fused_computation.2 | convolution fusion | flops 8594128896 | bytes 25165824 | tf_op jit(solution)/shard_map/tef,edf->td/dot_general | solution.py:440
  465.6 13.9 %reduce-scatter.7.cloned.1.call-done = bf16[128,2048]{1,0:T(8,128)(2,1)} async-done(((bf16[1024,2048]{1,0:T(8,128)(2,1)}), bf16[128,2048]{1,0:T(8,128)(2,1)}) %reduce-scatter.7.cloned.1.call-update) | async-done | bytes 524304 | tf_op jit(solution)/shard_map/reduce_scatter | solution.py:558
  479.5 53.6 %reduce_rows.1 = (f32[128,2048]{1,0:T(8,128)}, f32[16,128]{1,0:T(8,128)}) custom-call(bf16[8,128,2048]{2,1,0:T(8,128)(2,1)} %bitcast.284, f32[8,16,128]{2,1,0:T(8,128)} %bitcast_bitcast_fusion.note), custom_call_target="tpu_custom_call" | custom-call | bytes 200000000 | tf_op jit(solution)/shard_map/reduce_rows/pallas_call | solution.py:272
  537.6 49.2 %gather_rows.7 = bf16[8,128,2048]{2,1,0:T(8,128)(2,1)} custom-call(bf16[128,2048]{1,0:T(8,128)(2,1)} %fusion.60.refs_0_), custom_call_target="tpu_custom_call" | custom-call | bytes 200000000 | tf_op jit(solution)/shard_map/gather_rows/pallas_call | solution.py:153
  599.1 14.4 %multiply_convert_fusion = bf16[2,1024,1024]{1,2,0:T(8,128)(2,1)} fusion(f32[2,1024,1024]{1,2,0:T(8,128)} %copy-done.2, f32[2,1024]{1,0:T(2,128)S(1)} %copy-done.44, pred[1024,1024]{0,1:T(8,128)(4,1)S(1)} %copy-done.11, bf16[1024,2,128]{0,2,1:T(8,128)(2,1)} %bitcast.304, bf16[1024,2,128]{0,2,1:T(8,128)(2,1)} %bitcast.303), kind=kOutput, calls=%fused_computation.4 | convolution fusion | flops 1096813568 | bytes 14688256 | tf_op jit(solution)/shard_map/sub | solution.py:605
  620.0 11.0 %convolution_convert_fusion = bf16[4,512,2048]{2,1,0:T(8,128)(2,1)} fusion(bf16[1024,4,512]{0,2,1:T(8,128)(2,1)S(1)} %copy-done.64, bf16[1024,2048]{1,0:T(8,128)(2,1)S(1)} %bitcast.283), kind=kOutput, calls=%fused_computation.19 | convolution fusion | flops 8594128896 | bytes 16777216 | tf_op jit(solution)/shard_map/tef,td->efd/dot_general | solution.py:440
  631.1 10.4 %all-to-all-done.3 = bf16[8,256,512]{1,2,0:T(8,128)(2,1)} async-done(((bf16[8,256,512]{1,2,0:T(8,128)(2,1)}), bf16[8,256,512]{1,2,0:T(8,128)(2,1)}, u32[]{:S(2)}, u32[]{:S(2)}) %all-to-all-start.3) | async-done | bytes 2097184 | tf_op jit(solution)/shard_map/all_to_all | solution.py:485
  672.9 26.5 %small_sum.2 = f32[16,128]{1,0:T(8,128)} custom-call(f32[16,128]{1,0:T(8,128)} %reshape.468.values), custom_call_target="tpu_custom_call" | custom-call | bytes 10000000 | tf_op jit(solution)/shard_map/small_sum/pallas_call | solution.py:391
  705.5 30.5 %swap.3 = (bf16[128,2048]{1,0:T(8,128)(2,1)}, bf16[128,2048]{1,0:T(8,128)(2,1)}, bf16[128,2048]{1,0:T(8,128)(2,1)}) custom-call(bf16[8,128,256]{2,1,0:T(8,128)(2,1)} %bitcast.288, bf16[8,128,256]{2,1,0:T(8,128)(2,1)} %bitcast.289, bf16[8,128,256]{2,1,0:T(8,128)(2,1)} %bitcast.292), custom_call_target="tpu_custom_call" | custom-call | bytes 30000000 | tf_op jit(solution)/shard_map/swap/pallas_call | solution.py:339
  740.2 5.8 convolution_convert_fusion.1
  748.1 14.1 %all-to-all-start.5 = ((bf16[8,512,256]{2,1,0:T(8,128)(2,1)}), bf16[8,512,256]{2,1,0:T(8,128)(2,1)}, u32[]{:S(2)}, u32[]{:S(2)}) async-start(bf16[8,512,256]{2,1,0:T(8,128)(2,1)} %bitcast.269), calls=%async_computation.9 | async-start | bytes 4194304 | tf_op jit(solution)/shard_map/all_to_all | solution.py:485
  769.8 6.4 fusion.68
  776.3 6.5 convolution_add_fusion.2
  797.8 11.8 %all-to-all-done.5 = bf16[8,512,256]{2,1,0:T(8,128)(2,1)} async-done(((bf16[8,512,256]{2,1,0:T(8,128)(2,1)}), bf16[8,512,256]{2,1,0:T(8,128)(2,1)}, u32[]{:S(2)}, u32[]{:S(2)}) %all-to-all-start.5) | async-done | bytes 2097184 | tf_op jit(solution)/shard_map/all_to_all | solution.py:485
  809.5 10.5 %small_sum.3 = f32[16,128]{1,0:T(8,128)} custom-call(f32[32,16,128]{2,1,0:T(8,128)} %bitcast.300), custom_call_target="tpu_custom_call" | custom-call | bytes 10000000 | tf_op jit(solution)/shard_map/small_sum/pallas_call | solution.py:391
  820.0 6.8 all-to-all-start.6
  (294 shorter events, 177.4 us)
Async XLA Ops:
  7.2 281.9 %copy-start = (bf16[2048,16]{0,1:T(8,128)(2,1)S(1)}, bf16[2048,16]{0,1:T(8,128)(2,1)}, u32[]{:S(2)}) copy-start(bf16[2048,16]{0,1:T(8,128)(2,1)} %param.28) | copy-start | bytes 196612
  10.4 97.1 %all-to-all-start = ((bf16[8,256,512]{2,1,0:T(8,128)(2,1)}), bf16[8,256,512]{2,1,0:T(8,128)(2,1)S(1)}, u32[]{:S(2)}, u32[]{:S(2)}) async-start(bf16[8,256,512]{2,1,0:T(8,128)(2,1)} %bitcast.273), calls=%async_computation | async-start | bytes 4194304 | tf_op jit(solution)/shard_map/all_to_all | solution.py:485
  17.7 155.9 %all-gather.4.cloned.1.call-start = ((), (), s32[]{:S(2)}) async-start(), calls=%async_computation.13 | async-start | bytes 10485760 | tf_op jit(solution)/shard_map/all_gather | solution.py:488
  108.9 54.6 %all-to-all-start.1 = ((bf16[8,512,256]{2,1,0:T(8,128)(2,1)}), bf16[8,512,256]{2,1,0:T(8,128)(2,1)}, u32[]{:S(2)}, u32[]{:S(2)}) async-start(bf16[8,512,256]{2,1,0:T(8,128)(2,1)} %bitcast.294), calls=%async_computation.1 | async-start | bytes 4194304 | tf_op jit(solution)/shard_map/all_to_all | solution.py:485
  115.7 172.0 %all-gather.6.cloned.1.call-start = ((), (), s32[]{:S(2)}) async-start(), calls=%async_computation.14 | async-start | bytes 10485760 | tf_op jit(solution)/shard_map/all_gather | solution.py:488
  132.3 31.2 %copy-start.28 = (bf16[1024,2,128]{0,2,1:T(8,128)(2,1)}, bf16[1024,2,128]{0,2,1:T(8,128)(2,1)S(1)}, u32[]{:S(2)}) copy-start(bf16[1024,2,128]{0,2,1:T(8,128)(2,1)S(1)} %pad_maximum_fusion.4) | copy-start | bytes 1572868
  132.7 30.9 %copy-start.16 = (bf16[1024,2,128]{0,2,1:T(8,128)(2,1)}, bf16[1024,2,128]{0,2,1:T(8,128)(2,1)S(1)}, u32[]{:S(2)}) copy-start(bf16[1024,2,128]{0,2,1:T(8,128)(2,1)S(1)} %pad_maximum_fusion.5) | copy-start | bytes 1572868
  135.9 31.7 %copy-start.10 = (pred[1024,1024]{0,1:T(8,128)(4,1)}, pred[1024,1024]{0,1:T(8,128)(4,1)S(1)}, u32[]{:S(2)}) copy-start(pred[1024,1024]{0,1:T(8,128)(4,1)S(1)} %fusion.15) | copy-start | bytes 3145732
  138.8 32.1 %copy-start.30 = (bf16[1024,256]{0,1:T(8,128)(2,1)}, bf16[1024,256]{0,1:T(8,128)(2,1)S(1)}, u32[]{:S(2)}) copy-start(bf16[1024,256]{0,1:T(8,128)(2,1)S(1)} %convolution_convert_fusion.6) | copy-start | bytes 1572868
  173.6 17.5 %copy-start.25 = (bf16[2,128,1024]{2,1,0:T(8,128)(2,1)}, bf16[2,128,1024]{2,1,0:T(8,128)(2,1)S(1)}, u32[]{:S(2)}) copy-start(bf16[2,128,1024]{2,1,0:T(8,128)(2,1)S(1)} %convolution_convert_fusion.4) | copy-start | bytes 1572868
  193.5 94.2 %all-to-all-start.2 = ((bf16[8,256,512]{2,1,0:T(8,128)(2,1)}), bf16[8,256,512]{2,1,0:T(8,128)(2,1)S(1)}, u32[]{:S(2)}, u32[]{:S(2)}) async-start(bf16[8,256,512]{2,1,0:T(8,128)(2,1)} %bitcast.272), calls=%async_computation.2 | async-start | bytes 4194304 | tf_op jit(solution)/shard_map/all_to_all | solution.py:485
  201.3 154.3 %all-gather.8.cloned.1.call-start = ((), (), s32[]{:S(2)}) async-start(), calls=%async_computation.15 | async-start | bytes 10485760 | tf_op jit(solution)/shard_map/all_gather | solution.py:488
  289.0 190.5 %reduce-scatter.7.cloned.1.call-start = ((), (), s32[]{:S(2)}) async-start(), calls=%async_computation.16 | async-start | bytes 4718592 | tf_op jit(solution)/shard_map/reduce_scatter | solution.py:558
  387.7 199.0 %reduce-scatter.9.cloned.1.call-start = ((), (), s32[]{:S(2)}) async-start(), calls=%async_computation.17 | async-start | bytes 10485760 | tf_op jit(solution)/shard_map/reduce_scatter | solution.py:573
  387.9 21.8 %copy-start.5 = (bf16[8,128,2048]{2,1,0:T(8,128)(2,1)S(1)}, bf16[8,128,2048]{2,1,0:T(8,128)(2,1)}, u32[]{:S(2)}) copy-start(bf16[8,128,2048]{2,1,0:T(8,128)(2,1)} %gather_rows.5) | copy-start | bytes 12582916
  423.2 207.9 %reduce-scatter.11.cloned.1.call-start = ((), (), s32[]{:S(2)}) async-start(), calls=%async_computation.18 | async-start | bytes 10485760 | tf_op jit(solution)/shard_map/reduce_scatter | solution.py:573
  465.6 69.0 %copy-start.4 = (f32[128,2048]{1,0:T(8,128)S(1)}, f32[128,2048]{1,0:T(8,128)}, u32[]{:S(2)}) copy-start(f32[128,2048]{1,0:T(8,128)} %copy-done.3) | copy-start | bytes 3145732
  465.6 69.0 %copy-start.36 = (f32[2048]{0:T(1024)S(1)}, f32[2048]{0:T(1024)}, u32[]{:S(2)}) copy-start(f32[2048]{0:T(1024)} %param.27) | copy-start | bytes 24580
  465.6 69.0 %copy-start.51 = (f32[128]{0:T(128)S(1)}, f32[128]{0:T(128)}, u32[]{:S(2)}) copy-start(f32[128]{0:T(128)} %copy-done.50) | copy-start | bytes 1540
  465.6 70.7 %copy-start.58 = (f32[128]{0:T(128)S(1)}, f32[128]{0:T(128)}, u32[]{:S(2)}) copy-start(f32[128]{0:T(128)} %copy-done.57) | copy-start | bytes 1540
  465.6 70.8 %copy-start.17 = (bf16[1,128,2048]{2,1,0:T(8,128)(2,1)S(1)}, bf16[1,128,2048]{2,1,0:T(8,128)(2,1)}, u32[]{:S(2)}) copy-start(bf16[1,128,2048]{2,1,0:T(8,128)(2,1)} %param.19) | copy-start | bytes 1572868
  536.4 53.6 %copy-start.55 = (f32[128]{0:T(128)}, f32[128]{0:T(128)S(1)}, u32[]{:S(2)}) copy-start(f32[128]{0:T(128)S(1)} %multiply_multiply_fusion.8) | copy-start | bytes 1540
  590.0 51.5 %all-to-all-start.3 = ((bf16[8,256,512]{1,2,0:T(8,128)(2,1)}), bf16[8,256,512]{1,2,0:T(8,128)(2,1)}, u32[]{:S(2)}, u32[]{:S(2)}) async-start(bf16[8,256,512]{1,2,0:T(8,128)(2,1)} %bitcast.274), calls=%async_computation.5 | async-start | bytes 4194304 | tf_op jit(solution)/shard_map/all_to_all | solution.py:485
  594.4 141.7 %reduce-scatter.13.cloned.1.call-start = ((), (), s32[]{:S(2)}) async-start(), calls=%async_computation.19 | async-start | bytes 10485760 | tf_op jit(solution)/shard_map/reduce_scatter | solution.py:573
  644.6 95.6 %all-to-all-start.4 = ((bf16[8,256,512]{1,2,0:T(8,128)(2,1)}), bf16[8,256,512]{1,2,0:T(8,128)(2,1)}, u32[]{:S(2)}, u32[]{:S(2)}) async-start(bf16[8,256,512]{1,2,0:T(8,128)(2,1)} %bitcast.271), calls=%async_computation.7 | async-start | bytes 4194304 | tf_op jit(solution)/shard_map/all_to_all | solution.py:485
  648.9 171.1 %reduce-scatter.15.cloned.1.call-start = ((), (), s32[]{:S(2)}) async-start(), calls=%async_computation.20 | async-start | bytes 3932160 | tf_op jit(solution)/shard_map/reduce_scatter | solution.py:573
  748.0 14.4 %copy-start.13 = (bf16[128,2048]{1,0:T(8,128)(2,1)S(1)}, bf16[128,2048]{1,0:T(8,128)(2,1)}, u32[]{:S(2)}) copy-start(bf16[128,2048]{1,0:T(8,128)(2,1)} %multiply_convert_fusion.4.refs_0_) | copy-start | bytes 1572868
  748.0 15.0 %copy-start.26 = (bf16[2,128,1024]{2,1,0:T(8,128)(2,1)S(1)}, bf16[2,128,1024]{2,1,0:T(8,128)(2,1)}, u32[]{:S(2)}) copy-start(bf16[2,128,1024]{2,1,0:T(8,128)(2,1)} %copy-done.25) | copy-start | bytes 1572868
  748.1 61.5 %all-to-all-start.5 = ((bf16[8,512,256]{2,1,0:T(8,128)(2,1)}), bf16[8,512,256]{2,1,0:T(8,128)(2,1)}, u32[]{:S(2)}, u32[]{:S(2)}) async-start(bf16[8,512,256]{2,1,0:T(8,128)(2,1)} %bitcast.269), calls=%async_computation.9 | async-start | bytes 4194304 | tf_op jit(solution)/shard_map/all_to_all | solution.py:485
  762.2 64.7 %reduce-scatter.17.cloned.1.call-start = ((), (), s32[]{:S(2)}) async-start(), calls=%async_computation.21 | async-start | bytes 1310720 | tf_op jit(solution)/shard_map/reduce_scatter | solution.py:640
  769.8 13.0 %slice-start.2 = ((s8[8388608]{0:T(1024)(128)(4,1)}), s8[4194304]{0:T(1024)(128)(4,1)S(1)}, s32[]{:S(2)}) async-start(s8[8388608]{0:T(1024)(128)(4,1)} %bitcast.266), calls=%async_computation.24 | async-start | bytes 8388608
  820.0 27.3 %all-to-all-start.6 = ((bf16[8,64,768]{2,1,0:T(8,128)(2,1)}), bf16[8,64,768]{2,1,0:T(8,128)(2,1)}, u32[]{:S(2)}, u32[]{:S(2)}) async-start(bf16[8,64,768]{2,1,0:T(8,128)(2,1)} %bitcast.301), calls=%async_computation.11 | async-start | bytes 1572864 | tf_op jit(solution)/shard_map/all_to_all | solution.py:485
  (54 other events, 281.9 us)
Sparse Core Ops, SparseCore 0:
  109.0 60.4 all-gather.3
  193.6 61.3 all-gather.5
  289.2 59.7 all-gather.7
  387.8 91.6 reduce-scatter.6
  481.9 71.0 reduce-scatter.8
  555.5 71.3 reduce-scatter.10
  641.6 70.6 reduce-scatter.12
  748.2 47.5 reduce-scatter.14
  798.3 26.7 reduce-scatter.16
